TPU v7x, 128 devices: a whole 4x4x4 slice. The times are simulated.
128 devices in a mesh: row: 16 (over y_lo, x, core), col: 8 (over y_hi, z).
Axes of the slice: x: 4, y: 4 (y_hi: 2, y_lo: 2; y = y_hi * 2 + y_lo), z: 4, core: 2. Of those that a mesh axis runs over, the one named last changes fastest.
Arguments:
- pair: bfloat16 [384, 384, 128], P('row', 'col'), may hold values from -6 to 6
- mask: int32 [384], replicated, may hold values 0 or 1
- in_gain: float32 [128], replicated, may hold values from 0.5 to 1.5
- in_bias: float32 [128], replicated, may hold values from -3 to 3
- w_in: bfloat16 [128, 640], replicated, may hold values from -0.5 to 0.5
- out_gain: float32 [128], replicated, may hold values from 0.5 to 1.5
- out_bias: float32 [128], replicated, may hold values from -3 to 3
- w_out: bfloat16 [128, 128], replicated, may hold values from -0.5 to 0.5
- cotangent: bfloat16 [384, 384, 128], P('row', 'col'), may hold values from -6 to 6
Outputs:
- update: bfloat16 [384, 384, 128], P('row', 'col')
- pair_grad: bfloat16 [384, 384, 128], P('row', 'col')
- w_in_grad: float32 [128, 640], replicated
- w_out_grad: float32 [128, 128], replicated
Inputs may be any that keep to these rules, and one draw needn't show every extreme that they name: `mask`: 0 or 1 per residue.
All inputs are finite; a program needn't handle non-finite values.
Results may differ from a plain program's by a relative error of at most 0.013.
Values may be sent and summed in bfloat16 or wider, within the bound.
No kernel may reach another device: no remote copies, remote signals or barrier semaphores. Data moves between devices by JAX's collectives and lax.ppermute only.
A program may use at most 64 MiB of HBM per device.

v0:
```python
import jax
import jax.numpy as jnp
from jax import lax
from jax.sharding import PartitionSpec as P


def layer_norm(values, gain, shift):
    center = values - jnp.mean(values, -1, keepdims=True)
    scale = lax.rsqrt(jnp.mean(center * center, -1, keepdims=True) + 1e-05)
    normal = center * scale
    return (normal * gain + shift, normal, scale)


def norm_back(grad, gain, normal, scale):
    weighted = grad * gain
    return scale * (
        weighted
        - jnp.mean(weighted, -1, keepdims=True)
        - normal * jnp.mean(weighted * normal, -1, keepdims=True)
    )


def assemble(joined, n_row, n_col, tile_rows, tile_cols):
    share = joined.shape[0]
    blocks = joined.reshape(share, n_row, n_col, tile_rows, tile_cols)
    return jnp.transpose(blocks, (0, 1, 3, 2, 4)).reshape(
        share, n_row * tile_rows, n_col * tile_cols
    )


def disassemble(channels, n_row, n_col, tile_rows, tile_cols):
    share = channels.shape[0]
    blocks = channels.reshape(share, n_row, tile_rows, n_col, tile_cols)
    return jnp.transpose(blocks, (0, 1, 3, 2, 4)).reshape(
        share, n_row * n_col * tile_rows, tile_cols
    )


def on_device(pair, mask, in_gain, in_bias, w_in, out_gain, out_bias, w_out, cotangent):
    tile_rows, tile_cols, width = pair.shape
    hidden = w_out.shape[0]
    n_row = lax.axis_size("row")
    n_col = lax.axis_size("col")
    row_index = lax.axis_index("row")
    column_index = lax.axis_index("col")
    row_mask = lax.dynamic_slice_in_dim(mask, row_index * tile_rows, tile_rows).astype(jnp.float32)
    col_mask = lax.dynamic_slice_in_dim(mask, column_index * tile_cols, tile_cols).astype(
        jnp.float32
    )
    pair_mask = (row_mask[:, None] * col_mask[None, :])[:, :, None]
    normed, in_normal, in_scale = layer_norm(pair.astype(jnp.float32), in_gain, in_bias)
    normed = normed.astype(jnp.bfloat16)
    flat = normed.reshape(-1, width)
    pre = jnp.dot(flat, w_in, preferred_element_type=jnp.float32).reshape(tile_rows, tile_cols, -1)
    left_value = pre[..., :hidden]
    left_gate = jax.nn.sigmoid(pre[..., hidden : 2 * hidden])
    right_value = pre[..., 2 * hidden : 3 * hidden]
    right_gate = jax.nn.sigmoid(pre[..., 3 * hidden : 4 * hidden])
    out_gate = jax.nn.sigmoid(pre[..., 4 * hidden :])
    left = (pair_mask * left_gate * left_value).astype(jnp.bfloat16)
    right = (pair_mask * right_gate * right_value).astype(jnp.bfloat16)
    left_lead = jnp.transpose(left, (2, 0, 1))
    right_lead = jnp.transpose(right, (2, 0, 1))
    left_moved, right_moved = (
        lax.all_to_all(left_lead, ("row", "col"), split_axis=0, concat_axis=1, tiled=True),
        lax.all_to_all(right_lead, ("row", "col"), split_axis=0, concat_axis=1, tiled=True),
    )
    left_chan = assemble(left_moved, n_row, n_col, tile_rows, tile_cols)
    right_chan = assemble(right_moved, n_row, n_col, tile_rows, tile_cols)
    mixed_chan = jnp.einsum(
        "hik,hjk->hij", left_chan, right_chan, preferred_element_type=jnp.float32
    )
    back = lax.all_to_all(
        disassemble(mixed_chan, n_row, n_col, tile_rows, tile_cols).astype(jnp.bfloat16),
        ("row", "col"),
        split_axis=1,
        concat_axis=0,
        tiled=True,
    ).astype(jnp.float32)
    mixed = jnp.transpose(back, (1, 2, 0))
    out_normed, out_normal, out_scale = layer_norm(mixed, out_gain, out_bias)
    out_normed = out_normed.astype(jnp.bfloat16)
    out_flat = out_normed.reshape(-1, hidden)
    projected = jnp.dot(out_flat, w_out, preferred_element_type=jnp.float32).reshape(
        tile_rows, tile_cols, width
    )
    update = (out_gate * projected).astype(jnp.bfloat16)
    upstream = cotangent.astype(jnp.float32)
    d_projected = (upstream * out_gate).astype(jnp.bfloat16)
    d_outgate = upstream * projected * out_gate * (1.0 - out_gate)
    d_flat = d_projected.reshape(-1, width)
    grad_out = jnp.einsum("nh,nc->hc", out_flat, d_flat, preferred_element_type=jnp.float32)
    d_outnormed = jnp.dot(d_flat, w_out.T, preferred_element_type=jnp.float32).reshape(
        tile_rows, tile_cols, hidden
    )
    d_mixed = norm_back(d_outnormed, out_gain, out_normal, out_scale).astype(jnp.bfloat16)
    d_lead = jnp.transpose(d_mixed, (2, 0, 1))
    d_moved = lax.all_to_all(d_lead, ("row", "col"), split_axis=0, concat_axis=1, tiled=True)
    d_chan = assemble(d_moved, n_row, n_col, tile_rows, tile_cols)
    d_left_chan = jnp.einsum("hij,hjk->hik", d_chan, right_chan, preferred_element_type=jnp.float32)
    d_right_chan = jnp.einsum("hij,hik->hjk", d_chan, left_chan, preferred_element_type=jnp.float32)
    left_back, right_back = (
        lax.all_to_all(
            disassemble(d_left_chan, n_row, n_col, tile_rows, tile_cols).astype(jnp.bfloat16),
            ("row", "col"),
            split_axis=1,
            concat_axis=0,
            tiled=True,
        ).astype(jnp.float32),
        lax.all_to_all(
            disassemble(d_right_chan, n_row, n_col, tile_rows, tile_cols).astype(jnp.bfloat16),
            ("row", "col"),
            split_axis=1,
            concat_axis=0,
            tiled=True,
        ).astype(jnp.float32),
    )
    d_left = jnp.transpose(left_back, (1, 2, 0))
    d_right = jnp.transpose(right_back, (1, 2, 0))
    d_pre = jnp.concatenate(
        [
            d_left * pair_mask * left_gate,
            d_left * pair_mask * left_value * left_gate * (1.0 - left_gate),
            d_right * pair_mask * right_gate,
            d_right * pair_mask * right_value * right_gate * (1.0 - right_gate),
            d_outgate,
        ],
        -1,
    ).astype(jnp.bfloat16)
    d_preflat = d_pre.reshape(-1, 4 * hidden + width)
    grad_in = jnp.einsum("nc,nf->cf", flat, d_preflat, preferred_element_type=jnp.float32)
    grad_in, grad_out = lax.psum((grad_in, grad_out), ("row", "col"))
    d_normed = jnp.dot(d_preflat, w_in.T, preferred_element_type=jnp.float32).reshape(
        tile_rows, tile_cols, width
    )
    pair_grad = norm_back(d_normed, in_gain, in_normal, in_scale).astype(jnp.bfloat16)
    return (update, pair_grad, grad_in, grad_out)


def solution(mesh):
    placed = (P("row", "col", None), P(), P(), P(), P(), P(), P(), P(), P("row", "col", None))
    return jax.shard_map(
        on_device,
        mesh=mesh,
        in_specs=placed,
        out_specs=(P("row", "col", None), P("row", "col", None), P(), P()),
        check_vma=False,
    )
```

profile of v0, /device:TPU:1, one launch (start us, length us, event | category | flops | bytes accessed | tf_op | source)
XLA Modules:
  0.0 448.8 jit_solution(13118473043888244437)
XLA Ops:
  15.4 2.9 reshape.271
  18.3 11.5 %all-to-all-start = ((bf16[128,2,576]{2,1,0:T(2,128)(2,1)}), bf16[128,2,576]{2,1,0:T(2,128)(2,1)S(1)}, u32[]{:S(2)}, u32[]{:S(2)}) async-start(bf16[128,2,576]{2,1,0:T(2,128)(2,1)} %reshape.271), calls=%async_computation | async-start | bytes 655360 | tf_op jit(solution)/shard_map/all_to_all | solution.py:65
  31.9 2.9 reshape.269
  34.8 5.5 %all-to-all-done = bf16[128,2,576]{2,1,0:T(2,128)(2,1)S(1)} async-done(((bf16[128,2,576]{2,1,0:T(2,128)(2,1)}), bf16[128,2,576]{2,1,0:T(2,128)(2,1)S(1)}, u32[]{:S(2)}, u32[]{:S(2)}) %all-to-all-start) | async-done | bytes 294944 | tf_op jit(solution)/shard_map/all_to_all | solution.py:65
  40.4 6.5 %all-to-all-start.1 = ((bf16[128,2,576]{2,1,0:T(2,128)(2,1)}), bf16[128,2,576]{2,1,0:T(2,128)(2,1)}, u32[]{:S(2)}, u32[]{:S(2)}) async-start(bf16[128,2,576]{2,1,0:T(2,128)(2,1)} %reshape.269), calls=%async_computation.1 | async-start | bytes 655360 | tf_op jit(solution)/shard_map/all_to_all | solution.py:66
  52.7 4.4 all-to-all-done.1
  57.1 3.1 reshape.270
  66.3 13.0 %copy.59 = bf16[1,3072,48]{2,0,1:T(2,128)(2,1)} copy(bf16[1,3072,48]{2,1,0:T(8,128)(2,1)S(1)} %bitcast.167) | data formatting | bytes 589824 | tf_op jit(solution)/shard_map/convert_element_type | solution.py:74
  79.9 19.3 %reduce = bf16[3072,48]{1,0:T(8,128)(2,1)} reduce(bf16[3072,1,48]{2,1,0:T(2,128)(2,1)} %bitcast.155, bf16[]{:T(256)} %broadcast.142), dimensions={1}, to_apply=%bitcast.154.reduce_sub_computation | reduce | bytes 589826
  101.5 16.0 %all_to_all.24 = bf16[128,2,576]{2,1,0:T(2,128)(2,1)} all-to-all(bf16[128,2,576]{2,1,0:T(2,128)(2,1)S(1)} %reshape.273), channel_id=1, replica_groups=mesh['row'=16,'col'=8] {'row','col'}, dimensions={0} | all-to-all | bytes 589824 | tf_op jit(solution)/shard_map/all_to_all | solution.py:73
  117.5 5.7 %reshape.274 = bf16[3072,1,48]{2,1,0:T(2,128)(2,1)} reshape(bf16[128,2,576]{2,1,0:T(2,128)(2,1)} %all_to_all.24) | data formatting | bytes 589824
  123.2 4.2 bitcast_convert_fusion.2
  127.4 2.7 copy.37
  136.9 2.9 reshape.275
  139.8 5.3 %all-to-all-start.3 = ((bf16[128,2,576]{2,1,0:T(2,128)(2,1)}), bf16[128,2,576]{2,1,0:T(2,128)(2,1)S(1)}, u32[]{:S(2)}, u32[]{:S(2)}) async-start(bf16[128,2,576]{2,1,0:T(2,128)(2,1)} %reshape.275), calls=%async_computation.3 | async-start | bytes 655360 | tf_op jit(solution)/shard_map/all_to_all | solution.py:98
  145.1 2.4 reshape.252
  147.5 2.4 reshape.249
  153.6 2.5 multiply_convert_fusion
  164.5 13.0 %copy.57 = bf16[1,3072,48]{2,0,1:T(2,128)(2,1)} copy(bf16[1,3072,48]{2,1,0:T(8,128)(2,1)S(1)} %bitcast.168) | data formatting | bytes 589824 | tf_op jit(solution)/shard_map/convert_element_type | solution.py:111
  177.5 18.9 %reduce.2 = bf16[3072,48]{1,0:T(8,128)(2,1)} reduce(bf16[3072,1,48]{2,1,0:T(2,128)(2,1)} %bitcast.158, bf16[]{:T(256)} %broadcast.142), dimensions={1}, to_apply=%bitcast.152.reduce_sub_computation | reduce | bytes 589826
  196.4 2.9 reshape.279
  199.3 10.2 %all-to-all-start.5 = ((bf16[128,2,576]{2,1,0:T(2,128)(2,1)}), bf16[128,2,576]{2,1,0:T(2,128)(2,1)S(1)}, u32[]{:S(2)}, u32[]{:S(2)}) async-start(bf16[128,2,576]{2,1,0:T(2,128)(2,1)} %reshape.279), calls=%async_computation.5 | async-start | bytes 655360 | tf_op jit(solution)/shard_map/all_to_all | solution.py:110
  216.0 13.0 %copy.58 = bf16[1,3072,48]{2,0,1:T(2,128)(2,1)} copy(bf16[1,3072,48]{2,1,0:T(8,128)(2,1)S(1)} %bitcast.169) | data formatting | bytes 589824 | tf_op jit(solution)/shard_map/convert_element_type | solution.py:104
  229.0 18.9 %reduce.1 = bf16[3072,48]{1,0:T(8,128)(2,1)} reduce(bf16[3072,1,48]{2,1,0:T(2,128)(2,1)} %bitcast.156, bf16[]{:T(256)} %broadcast.142), dimensions={1}, to_apply=%bitcast.153.reduce_sub_computation | reduce | bytes 589826
  247.8 3.1 reshape.277
  251.0 10.2 %all-to-all-start.4 = ((bf16[128,2,576]{2,1,0:T(2,128)(2,1)}), bf16[128,2,576]{2,1,0:T(2,128)(2,1)}, u32[]{:S(2)}, u32[]{:S(2)}) async-start(bf16[128,2,576]{2,1,0:T(2,128)(2,1)} %reshape.277), calls=%async_computation.4 | async-start | bytes 655360 | tf_op jit(solution)/shard_map/all_to_all | solution.py:103
  263.4 4.2 bitcast_convert_fusion
  267.6 2.7 copy.50
  271.4 5.7 %reshape.278 = bf16[3072,1,48]{2,1,0:T(2,128)(2,1)} reshape(bf16[128,2,576]{2,1,0:T(2,128)(2,1)} %all-to-all-done.4) | data formatting | bytes 589824
  277.2 4.2 bitcast_convert_fusion.1
  281.3 2.7 copy.44
  293.5 144.8 %all-reduce.3.cloned.1.call-done = (f32[128,640]{1,0:T(8,128)}, f32[128,128]{1,0:T(8,128)}) async-done(((f32[128,640]{1,0:T(8,128)}, f32[128,128]{1,0:T(8,128)}), (f32[128,640]{1,0:T(8,128)}, f32[128,128]{1,0:T(8,128)})) %all-reduce.3.cloned.1.call-update) | async-done | bytes 393232 | tf_op jit(solution)/shard_map/psum | solution.py:132
  (83 shorter events, 66.4 us)
Async XLA Ops:
  7.2 4.2 copy-start
  18.3 22.1 %all-to-all-start = ((bf16[128,2,576]{2,1,0:T(2,128)(2,1)}), bf16[128,2,576]{2,1,0:T(2,128)(2,1)S(1)}, u32[]{:S(2)}, u32[]{:S(2)}) async-start(bf16[128,2,576]{2,1,0:T(2,128)(2,1)} %reshape.271), calls=%async_computation | async-start | bytes 655360 | tf_op jit(solution)/shard_map/all_to_all | solution.py:65
  40.4 16.7 %all-to-all-start.1 = ((bf16[128,2,576]{2,1,0:T(2,128)(2,1)}), bf16[128,2,576]{2,1,0:T(2,128)(2,1)}, u32[]{:S(2)}, u32[]{:S(2)}) async-start(bf16[128,2,576]{2,1,0:T(2,128)(2,1)} %reshape.269), calls=%async_computation.1 | async-start | bytes 655360 | tf_op jit(solution)/shard_map/all_to_all | solution.py:66
  127.4 5.5 %copy-start.7 = (bf16[24,48,128]{2,1,0:T(8,128)(2,1)S(1)}, bf16[24,48,128]{2,1,0:T(8,128)(2,1)}, u32[]{:S(2)}) copy-start(bf16[24,48,128]{2,1,0:T(8,128)(2,1)} %param.17) | copy-start | bytes 884740
  127.4 5.6 %copy-start.11 = (bf16[128,128]{1,0:T(8,128)(2,1)S(1)}, bf16[128,128]{1,0:T(8,128)(2,1)}, u32[]{:S(2)}) copy-start(bf16[128,128]{1,0:T(8,128)(2,1)} %param.16) | copy-start | bytes 98308
  127.4 5.6 %copy-start.13 = (f32[128]{0:T(128)S(1)}, f32[128]{0:T(128)}, u32[]{:S(2)}) copy-start(f32[128]{0:T(128)} %param.14) | copy-start | bytes 1540
  133.0 1.9 copy-start.1
  139.8 16.3 %all-to-all-start.3 = ((bf16[128,2,576]{2,1,0:T(2,128)(2,1)}), bf16[128,2,576]{2,1,0:T(2,128)(2,1)S(1)}, u32[]{:S(2)}, u32[]{:S(2)}) async-start(bf16[128,2,576]{2,1,0:T(2,128)(2,1)} %reshape.275), calls=%async_computation.3 | async-start | bytes 655360 | tf_op jit(solution)/shard_map/all_to_all | solution.py:98
  145.1 8.6 %copy-start.12 = (f32[128]{0:T(128)S(1)}, f32[128]{0:T(128)}, u32[]{:S(2)}) copy-start(f32[128]{0:T(128)} %param.15) | copy-start | bytes 1540
  199.3 51.7 %all-to-all-start.5 = ((bf16[128,2,576]{2,1,0:T(2,128)(2,1)}), bf16[128,2,576]{2,1,0:T(2,128)(2,1)S(1)}, u32[]{:S(2)}, u32[]{:S(2)}) async-start(bf16[128,2,576]{2,1,0:T(2,128)(2,1)} %reshape.279), calls=%async_computation.5 | async-start | bytes 655360 | tf_op jit(solution)/shard_map/all_to_all | solution.py:110
  251.0 20.5 %all-to-all-start.4 = ((bf16[128,2,576]{2,1,0:T(2,128)(2,1)}), bf16[128,2,576]{2,1,0:T(2,128)(2,1)}, u32[]{:S(2)}, u32[]{:S(2)}) async-start(bf16[128,2,576]{2,1,0:T(2,128)(2,1)} %reshape.277), calls=%async_computation.4 | async-start | bytes 655360 | tf_op jit(solution)/shard_map/all_to_all | solution.py:103
  261.1 177.2 %all-reduce.3.cloned.1.call-start = ((), (), s32[]{:S(2)}) async-start(), calls=%async_computation.6 | async-start | bytes 786432 | tf_op jit(solution)/shard_map/psum | solution.py:132
  284.0 1.4 copy-start.4
  284.0 1.7 copy-start.3
  285.7 1.1 copy-start.6
  285.7 1.1 copy-start.8
  286.0 2.2 copy-start.2
  286.0 2.2 copy-start.9
  286.1 2.2 copy-start.10
  287.1 1.1 copy-start.5
Sparse Core Ops, SparseCore 0:
  292.2 146.0 all-reduce.2
where the time goes:
time: 456 us; the launch traced here: 449 us
  waiting for transfers between devices  156 us (34%)
  local copies, waits for them, and re-layouts  119 us (26%)
  other arithmetic  82.4 us (18%)
  starting transfers between devices  43.7 us (10%)
  matrix products  17 us (4%)
  blocking collectives  16 us (4%)
  between operations  14.8 us (3%)
    psum x1, waiting for transfers between devices, on_device(): grad_in, grad_out = lax.psum((grad_in, grad_out), ('row', 'col'))  145 us
    unnamed x7, other arithmetic  59.3 us
    unnamed x43, local copies, waits for them, and re-layouts  42.9 us
    all_to_all x1, blocking collectives, on_device(): lax.all_to_all(disassemble(mixed_chan, n_row, n_col, tile_rows, tile_cols...  16 us
    convert_element_type x1, local copies, waits for them, and re-layouts, on_device(): disassemble(mixed_chan, n_row, n_col, tile_rows, tile_cols)  13 us
    convert_element_type x1, local copies, waits for them, and re-layouts, on_device(): disassemble(d_right_chan, n_row, n_col, tile_rows, tile_cols)  13 us
    convert_element_type x1, local copies, waits for them, and re-layouts, on_device(): disassemble(d_left_chan, n_row, n_col, tile_rows, tile_cols)  13 us
    all_to_all x1, starting transfers between devices, on_device(): lax.all_to_all(left_lead, ('row', 'col'), split_axis=0, concat_axis=1, ti...  11.5 us
  transfers between devices with their start and end apart: 6, of which 4 were waited for; matrix products, arithmetic and copies ran while one was open for 16% of the time, Pallas kernels for 0%

commit v1 on v0

v1 whole, which is shorter than its diff:
```python
import functools

import jax
import jax.numpy as jnp
from jax import lax
from jax.experimental import pallas as pl
from jax.experimental.pallas import tpu as pltpu
from jax.sharding import PartitionSpec as P

F32 = jnp.float32
BF16 = jnp.bfloat16
EPS = 1e-05
AXES = ("row", "col")

A, B, HALF, LANES = 24, 48, 64, 128
NR, NC, ND = 16, 8, 128
CELLS = A * B
H = 128
N = NR * A


def dot(x, y, contract):
    return lax.dot_general(x, y, (contract, ((), ())), preferred_element_type=F32)


NT = ((1,), (1,))
TN = ((0,), (0,))
NN = ((1,), (0,))


def lane_low(shape):
    return lax.broadcasted_iota(jnp.int32, shape, len(shape) - 1) < HALF


def swap_halves(x):
    return pltpu.roll(x, HALF, x.ndim - 1)


def pad_cells(x):
    return jnp.concatenate([x, jnp.zeros((HALF - B, x.shape[1]), x.dtype)], 0)


def two_sided(x):
    padded = pad_cells(x)
    none = jnp.zeros_like(padded)
    return jnp.concatenate(
        [jnp.concatenate([padded, none], 1), jnp.concatenate([none, padded], 1)], 0
    )


def column(row):
    at = lax.broadcasted_iota(jnp.int32, (H, LANES), 0)
    lane = lax.broadcasted_iota(jnp.int32, (H, LANES), 1)
    return jnp.sum(jnp.where(at == lane, row, 0.0), 1, keepdims=True)


def stacked_weights(w_ref):
    part = [w_ref[:, p * H : (p + 1) * H].astype(F32).T.astype(BF16) for p in range(4)]
    return jnp.concatenate(
        [jnp.concatenate([part[0], part[2]], 1), jnp.concatenate([part[1], part[3]], 1)], 0
    )


def project_kernel(mask_s, mask_ref, pair_ref, gain_ref, bias_ref, w_ref,
                   send_ref, normed_ref, pg_ref, pvg_ref, scratch):
    row = lax.axis_index("row")
    col = lax.axis_index("col")
    weights = stacked_weights(w_ref)
    at = lax.broadcasted_iota(jnp.int32, (N, LANES), 0)
    lane = lax.rem(lax.broadcasted_iota(jnp.int32, (N, LANES), 1), HALF)
    pick = jnp.where((at == col * B + lane) & (lane < B), 1.0, 0.0).astype(BF16)
    mask_row = jnp.broadcast_to(mask_ref[...].astype(F32), (8, N)).astype(BF16)
    col_mask = dot(mask_row, pick, NN)[0:1, :]
    gain, bias = gain_ref[...], bias_ref[...]
    for pair_at in range(A // 2):
        rows = pl.ds(pair_at * 2 * B, 2 * B)
        x = pair_ref[rows, :].astype(F32)
        center = x - jnp.mean(x, 1, keepdims=True)
        scale = lax.rsqrt(jnp.mean(center * center, 1, keepdims=True) + EPS)
        normed = (center * scale * gain + bias).astype(BF16)
        normed_ref[rows, :] = normed
        cells = jnp.concatenate([two_sided(normed[:B]), two_sided(normed[B:])], 0)
        pre = dot(weights, cells, NT)
        for k in range(2):
            a = pair_at * 2 + k
            value = pre[:H, k * LANES : (k + 1) * LANES]
            gate = jax.nn.sigmoid(pre[H:, k * LANES : (k + 1) * LANES])
            seen = col_mask * mask_s[row * A + a].astype(F32)
            pg = gate * seen
            out = pg * value
            pg_ref[a] = pg
            pvg_ref[a] = out * (1.0 - gate)
            scratch[pl.ds(a, H, stride=A), :] = out
    send_ref[...] = scratch[...].astype(BF16)


def gate_kernel(normed_ref, w_ref, cot_ref, w_out_ref, gain_ref, sig_ref, dproj_ref, wt_ref):
    gain = column(gain_ref[...])
    w_og = w_ref[:, 4 * H :]
    w_out = w_out_ref[...]
    sig = jax.nn.sigmoid(dot(normed_ref[...], w_og, NN))
    sig_ref[...] = sig
    dproj_ref[...] = (cot_ref[...].astype(F32) * sig).astype(BF16)
    for q in range(16):
        wt_ref[q] = dot(w_out, row_cells(dproj_ref, q), NT) * gain


def row_cells(ref, q):
    low = pad_cells(ref[q * B : (q + 1) * B, :])
    high = pad_cells(ref[(q + 16) * B : (q + 17) * B, :]) if q < 8 else jnp.zeros_like(low)
    return jnp.concatenate([low, high], 0)


def mix_kernel(recv_ref, send_ref, left_ref, right_ref, mixed):
    right_ref[...] = jnp.zeros_like(right_ref)
    low = lane_low((A, LANES))
    for r2 in range(NR // 2):
        for p in range(NC // 2):
            lefts, rights = [], []
            for r in (2 * r2, 2 * r2 + 1):
                both = recv_ref[pl.ds((r * NC + 2 * p) * A, 2 * A), :].astype(F32)
                x, y = both[:A], both[A:]
                lefts.append(jnp.where(low, x, swap_halves(y)))
                rights.append(jnp.where(low, swap_halves(x), y))
            lanes = slice(p * LANES, (p + 1) * LANES)
            left_ref[r2 * B : (r2 + 1) * B, lanes] = jnp.concatenate(lefts, 0).astype(BF16)
            right_ref[r2 * HALF : r2 * HALF + B, lanes] = jnp.concatenate(rights, 0).astype(BF16)
    mixed[...] = dot(left_ref[...], right_ref[...], NT)
    low = lane_low((8, LANES))
    for r in range(NR):
        for p in range(NC // 2):
            t0, t1, t2 = (
                mixed[r * A + 8 * t : r * A + 8 * t + 8, p * LANES : (p + 1) * LANES]
                for t in range(3)
            )
            rows = jnp.concatenate(
                [jnp.where(low, t0, swap_halves(t2)), t1,
                 jnp.where(low, swap_halves(t0), t2), swap_halves(t1)], 0
            )
            send_ref[pl.ds((r * NC + 2 * p) * 16, 32), :] = rows.astype(BF16)


def norm_cells(x):
    center = x - jnp.mean(x, 0, keepdims=True)
    scale = lax.rsqrt(jnp.mean(center * center, 0, keepdims=True) + EPS)
    return center * scale, scale


def d_mixed_kernel(recv_ref, wt_ref, send_ref, scratch):
    scratch[...] = recv_ref[...].astype(F32)
    for q in range(16):
        normal, scale = norm_cells(scratch[pl.ds(q, H, stride=16), :])
        wt = wt_ref[q]
        d = scale * (
            wt - jnp.mean(wt, 0, keepdims=True) - normal * jnp.mean(wt * normal, 0, keepdims=True)
        )
        scratch[pl.ds(q, H, stride=16), :] = d
    send_ref[...] = scratch[...].astype(BF16)


def update_kernel(recv_ref, w_out_ref, gain_ref, bias_ref, sig_ref, dproj_ref, cot_ref,
                  normed_ref, w_ref, update_ref, dn_ref, grads_ref, scratch, d_og):
    scratch[...] = recv_ref[...].astype(F32)
    gain, bias = column(gain_ref[...]), column(bias_ref[...])
    w_out = w_out_ref[...]
    grad = jnp.zeros((H, H), F32)
    for q in range(16):
        normal, _ = norm_cells(scratch[pl.ds(q, H, stride=16), :])
        normed = (normal * gain + bias).astype(BF16)
        projected = dot(normed, w_out, TN)
        grad = grad + dot(normed, row_cells(dproj_ref, q), NN)
        for k in range(2 if q < 8 else 1):
            rows = pl.ds((q + 16 * k) * B, B)
            sig = sig_ref[rows, :]
            proj = projected[k * HALF : k * HALF + B]
            update_ref[rows, :] = (sig * proj).astype(BF16)
            d_og[rows, :] = (cot_ref[rows, :].astype(F32) * proj * sig * (1.0 - sig)).astype(BF16)
    grads_ref[1] = grad
    grads_ref[0] = dot(d_og[...], normed_ref[...], TN)
    dn_ref[...] = dot(d_og[...], w_ref[:, 4 * H :], NT)


def back_kernel(recv_ref, left_ref, right_ref, send_ref, d_mixed, d_left, d_right):
    low = lane_low((8, LANES))
    for r2 in range(NR // 2):
        for p in range(NC // 2):
            rows = []
            for r in (2 * r2, 2 * r2 + 1):
                both = recv_ref[pl.ds((r * NC + 2 * p) * 16, 32), :].astype(F32)
                x0, x1, y0, y1 = (both[8 * t : 8 * t + 8] for t in range(4))
                rows += [jnp.where(low, x0, swap_halves(y0)), jnp.where(low, x1, swap_halves(y1)),
                         jnp.where(low, swap_halves(x0), y0)]
            d_mixed[r2 * B : (r2 + 1) * B, p * LANES : (p + 1) * LANES] = (
                jnp.concatenate(rows, 0).astype(BF16)
            )
    d = d_mixed[...]
    d_left[...] = dot(d, right_ref[...], NN)
    d_right[...] = dot(d, left_ref[...], TN)
    low = lane_low((A, LANES))
    for r in range(NR):
        for p in range(NC // 2):
            lanes = slice(p * LANES, (p + 1) * LANES)
            x = d_left[r * A : (r + 1) * A, lanes]
            start = (r // 2) * HALF + (r % 2) * A
            y = d_right[start : start + A, lanes]
            rows = jnp.concatenate(
                [jnp.where(low, x, swap_halves(y)), jnp.where(low, swap_halves(x), y)], 0
            )
            send_ref[pl.ds((r * NC + 2 * p) * A, 2 * A), :] = rows.astype(BF16)


def grad_kernel(recv_ref, pg_ref, pvg_ref, normed_ref, grads_ref, send_ref, dvg_ref,
                scratch, packed):
    scratch[...] = recv_ref[...].astype(F32)
    total = jnp.zeros((2 * H, 2 * H), F32)
    for pair_at in range(A // 2):
        sides, cells = [], []
        for k in range(2):
            a = pair_at * 2 + k
            d = scratch[pl.ds(a, H, stride=A), :]
            side = jnp.concatenate([d * pg_ref[a], d * pvg_ref[a]], 0).astype(BF16)
            dvg_ref[a] = side
            sides.append(side)
            cells.append(two_sided(normed_ref[a * B : (a + 1) * B, :]))
        total = total + dot(jnp.concatenate(sides, 1), jnp.concatenate(cells, 0), NN)
    blocks = [total[:H, :H], total[H:, :H], total[:H, H:], total[H:, H:],
              grads_ref[0], grads_ref[1], jnp.zeros((H, H), F32), jnp.zeros((H, H), F32)]
    for g, block in enumerate(blocks):
        packed[pl.ds(g, H, stride=8), :] = block
    send_ref[...] = packed[...].astype(BF16)


def pair_grad_kernel(dvg_ref, dn_ref, pair_ref, gain_ref, w_ref, out_ref):
    weights = stacked_weights(w_ref)
    gain = gain_ref[...]
    for a in range(A):
        rows = pl.ds(a * B, B)
        both = dot(dvg_ref[a], weights, TN)
        d = both[:B, :H] + both[HALF : HALF + B, H:] + dn_ref[rows, :]
        x = pair_ref[rows, :].astype(F32)
        center = x - jnp.mean(x, 1, keepdims=True)
        scale = lax.rsqrt(jnp.mean(center * center, 1, keepdims=True) + EPS)
        normal = center * scale
        weighted = d * gain
        out_ref[rows, :] = (
            scale * (weighted - jnp.mean(weighted, 1, keepdims=True)
                     - normal * jnp.mean(weighted * normal, 1, keepdims=True))
        ).astype(BF16)


def sum_kernel(recv_ref, send_ref):
    total = jnp.sum(recv_ref[...].astype(F32).reshape(ND, 8, LANES), 0)
    twice = jnp.concatenate([total, total], 0).astype(BF16)
    for s in range(ND // 2):
        send_ref[s * 16 : (s + 1) * 16, :] = twice


def unpack_kernel(recv_ref, w_in_ref, w_out_ref, scratch):
    scratch[...] = recv_ref[...].astype(F32)
    for g in range(5):
        w_in_ref[:, g * H : (g + 1) * H] = scratch[pl.ds(g, H, stride=8), :].T
    w_out_ref[...] = scratch[pl.ds(5, H, stride=8), :]


def call(kernel, outs, scratch, args, flops, smem=0):
    in_specs = [pl.BlockSpec(memory_space=pltpu.SMEM)] * smem
    in_specs += [pl.BlockSpec(memory_space=pltpu.VMEM)] * (len(args) - smem)
    size = lambda v: v.size * v.dtype.itemsize
    shapes = [jax.ShapeDtypeStruct(s, d) for s, d in outs]
    total = sum(size(v) for v in args) + sum(size(v) for v in shapes)
    return pl.pallas_call(
        kernel,
        out_shape=shapes,
        in_specs=in_specs,
        out_specs=[pl.BlockSpec(memory_space=pltpu.VMEM)] * len(shapes),
        scratch_shapes=[pltpu.VMEM(s, d) for s, d in scratch],
        cost_estimate=pl.CostEstimate(flops=flops, bytes_accessed=total, transcendentals=0),
        compiler_params=pltpu.CompilerParams(vmem_limit_bytes=40 * 2**20),
    )(*args)


def exchange(x, rows):
    moved = lax.all_to_all(x.reshape(ND, rows, LANES), AXES, 0, 0, tiled=True)
    return moved.reshape(ND * rows, LANES)


def on_device(pair, mask, in_gain, in_bias, w_in, out_gain, out_bias, w_out, cotangent):
    pair2 = pair.reshape(CELLS, H)
    cot2 = cotangent.reshape(CELLS, H)
    line = lambda v: v.reshape(1, -1)
    send, normed, pg, pvg = call(
        project_kernel,
        [((ND * A, LANES), BF16), ((CELLS, H), BF16), ((A, H, LANES), F32), ((A, H, LANES), F32)],
        [((ND * A, LANES), F32)],
        [mask, line(mask), pair2, line(in_gain), line(in_bias), w_in],
        400_000_000, smem=1,
    )
    recv = exchange(send, A)
    sig, dproj, wt = call(
        gate_kernel,
        [((CELLS, H), F32), ((CELLS, H), BF16), ((16, H, LANES), F32)],
        [],
        [normed, w_in, cot2, w_out, line(out_gain)],
        100_000_000,
    )
    send, left, right = call(
        mix_kernel,
        [((ND * 16, LANES), BF16), ((N, 512), BF16), ((512, 512), BF16)],
        [((N, 512), F32)],
        [recv],
        200_000_000,
    )
    mixed = exchange(send, 16)
    (send,) = call(
        d_mixed_kernel, [((ND * 16, LANES), BF16)], [((ND * 16, LANES), F32)], [mixed, wt], 10_000_000
    )
    recv = exchange(send, 16)
    update, dn, grads = call(
        update_kernel,
        [((CELLS, H), BF16), ((CELLS, H), F32), ((2, H, H), F32)],
        [((ND * 16, LANES), F32), ((CELLS, H), BF16)],
        [mixed, w_out, line(out_gain), line(out_bias), sig, dproj, cot2, normed, w_in],
        200_000_000,
    )
    (send,) = call(
        back_kernel,
        [((ND * A, LANES), BF16)],
        [((N, 512), BF16), ((N, 512), F32), ((512, 512), F32)],
        [recv, left, right],
        400_000_000,
    )
    recv = exchange(send, A)
    send, dvg = call(
        grad_kernel,
        [((ND * 8, LANES), BF16), ((A, 2 * H, LANES), BF16)],
        [((ND * A, LANES), F32), ((ND * 8, LANES), F32)],
        [recv, pg, pvg, normed, grads],
        400_000_000,
    )
    recv = exchange(send, 8)
    (pair_grad,) = call(
        pair_grad_kernel, [((CELLS, H), BF16)], [], [dvg, dn, pair2, line(in_gain), w_in], 400_000_000
    )
    (send,) = call(sum_kernel, [((ND * 8, LANES), BF16)], [], [recv], 1_000_000)
    recv = exchange(send, 8)
    w_in_grad, w_out_grad = call(
        unpack_kernel,
        [((H, 5 * H), F32), ((H, H), F32)],
        [((ND * 8, LANES), F32)],
        [recv],
        1_000_000,
    )
    return (update.reshape(A, B, H), pair_grad.reshape(A, B, H), w_in_grad, w_out_grad)


def solution(mesh):
    placed = (P("row", "col", None), P(), P(), P(), P(), P(), P(), P(), P("row", "col", None))
    return jax.shard_map(
        on_device,
        mesh=mesh,
        in_specs=placed,
        out_specs=(P("row", "col", None), P("row", "col", None), P(), P()),
        check_vma=False,
    )
```

time: 456 us -> 134 us (0.29); the launches traced: 449 us -> 133 us
  waiting for transfers between devices: 156 us -> 21.4 us
  local copies, waits for them, and re-layouts: 119 us -> 18.7 us
  other arithmetic: 82.4 us -> 0 us
  blocking collectives: 16 us -> 59.2 us
  starting transfers between devices: 43.7 us -> 16.2 us
  matrix products: 17 us -> 0 us
  Pallas kernels: 0 us -> 16.4 us
  between operations: 14.8 us -> 0.81 us
    psum x1 -> x0, waiting for transfers between devices: 145 us -> none  [on_device(): grad_in, grad_out = lax.psum((grad_in, grad_out), ('row', 'col'))]
    unnamed x7 -> x0, other arithmetic: 59.3 us -> none
    convert_element_type x7 -> x0, local copies, waits for them, and re-layouts: 48.3 us -> none  [the longest x1 13 us: on_device(): disassemble(mixed_chan, n_row, n_col, tile_rows, tile_cols)]
    all_to_all x1 -> x3, blocking collectives: 16 us -> 59.2 us  [exchange(): moved = lax.all_to_all(x.reshape(ND, rows, LANES), AXES, 0, 0, tiled=True)]
    all_to_all x5 -> x3, starting transfers between devices: 43.6 us -> 16.2 us  [exchange(): moved = lax.all_to_all(x.reshape(ND, rows, LANES), AXES, 0, 0, tiled=True)]
    unnamed x43 -> x54, local copies, waits for them, and re-layouts: 42.9 us -> 18 us
    dot_general x9 -> x0, matrix products: 17 us -> none  [the longest x1 2.47 us: on_device(): jnp.dot(out_flat, w_out, preferred_element_type=jnp.float32)]
    pallas_call x0 -> x10, Pallas kernels: none -> 16.4 us  [call(): pl.pallas_call(kernel, out_shape=shapes, in_specs=in_specs, out_specs=[pl...]
  transfers between devices with their start and end apart: 6 -> 3, of which waited for: 4 -> 3; matrix products, arithmetic and copies ran while one was open for 16% -> 0% of each run, Pallas kernels for 0% -> 6%
where the time goes in v1:
time: 134 us; the launch traced here: 133 us
  blocking collectives  59.2 us (44%)
  waiting for transfers between devices  21.4 us (16%)
  local copies, waits for them, and re-layouts  18.7 us (14%)
  Pallas kernels  16.4 us (12%)
  starting transfers between devices  16.2 us (12%)
    all_to_all x3, blocking collectives, exchange(): moved = lax.all_to_all(x.reshape(ND, rows, LANES), AXES, 0, 0, tiled=True)  59.2 us
    all_to_all x3, waiting for transfers between devices, exchange(): moved = lax.all_to_all(x.reshape(ND, rows, LANES), AXES, 0, 0, tiled=True)  21.4 us
    unnamed x54, local copies, waits for them, and re-layouts  18 us
    pallas_call x10, Pallas kernels, call(): pl.pallas_call(kernel, out_shape=shapes, in_specs=in_specs, out_specs=[pl...  16.4 us
    all_to_all x3, starting transfers between devices, exchange(): moved = lax.all_to_all(x.reshape(ND, rows, LANES), AXES, 0, 0, tiled=True)  16.2 us
  transfers between devices with their start and end apart: 3, of which 3 were waited for; matrix products, arithmetic and copies ran while one was open for 0% of the time, Pallas kernels for 6%

profile of v1, /device:TPU:1, one launch (start us, length us, event | category | flops | bytes accessed | tf_op | source)
XLA Modules:
  0.0 132.7 jit_solution(9138628229901742965)
XLA Ops:
  1.3 0.9 copy-done.4
  2.2 1.0 copy-done.16
  5.2 1.8 %shard_map.120 = (bf16[3072,128]{1,0:T(8,128)(2,1)S(1)}, bf16[1152,128]{1,0:T(8,128)(2,1)S(1)}, f32[24,128,128]{2,1,0:T(8,128)S(1)}, f32[24,128,128]{2,1,0:T(8,128)S(1)}) custom-call(s32[384]{0:T(512)S(1)} %copy-done.21, s32[1,384]{1,0:T(1,128)S(1)} %reshape.73.mask_ref, bf16[1152,128]{1,0:T(8,128)(2,1)S(1)} %bitcast.31, f32[1,128]{1,0:T(1,128)S(1)} %bitcast.36, ...), custom_call_target="tpu_custom_call" | custom-call | flops 400000000 | bytes 4689920 | tf_op jit(solution)/shard_map/pallas_call | solution.py:271
  7.0 1.2 copy-done
  8.2 26.2 %all_to_all.30 = bf16[128,24,128]{2,1,0:T(8,128)(2,1)S(1)} all-to-all(bf16[128,24,128]{2,1,0:T(8,128)(2,1)S(1)} %bitcast.30), channel_id=1, replica_groups=mesh['row'=16,'col'=8] {'row','col'}, dimensions={0} | all-to-all | bytes 1572864 | tf_op jit(solution)/shard_map/all_to_all | solution.py:283
  34.5 1.5 %shard_map.121 = (bf16[2048,128]{1,0:T(8,128)(2,1)}, bf16[384,512]{1,0:T(8,128)(2,1)S(1)}, bf16[512,512]{1,0:T(8,128)(2,1)S(1)}) custom-call(bf16[3072,128]{1,0:T(8,128)(2,1)S(1)} %bitcast.22), custom_call_target="tpu_custom_call" | custom-call | flops 200000000 | bytes 2228224 | tf_op jit(solution)/shard_map/pallas_call | solution.py:271
  36.8 5.5 %all-to-all-start.1 = ((bf16[128,16,128]{2,1,0:T(8,128)(2,1)}), bf16[128,16,128]{2,1,0:T(8,128)(2,1)S(1)}, u32[]{:S(2)}, u32[]{:S(2)}) async-start(bf16[128,16,128]{2,1,0:T(8,128)(2,1)} %bitcast.5), calls=%async_computation.1 | async-start | bytes 1048576 | tf_op jit(solution)/shard_map/all_to_all | solution.py:283
  43.0 1.0 copy-done.8
  44.0 0.8 copy-done.12
  45.6 8.9 %all-to-all-done.1 = bf16[128,16,128]{2,1,0:T(8,128)(2,1)S(1)} async-done(((bf16[128,16,128]{2,1,0:T(8,128)(2,1)}), bf16[128,16,128]{2,1,0:T(8,128)(2,1)S(1)}, u32[]{:S(2)}, u32[]{:S(2)}) %all-to-all-start.1) | async-done | bytes 524320 | tf_op jit(solution)/shard_map/all_to_all | solution.py:283
  54.5 1.2 copy-done.9
  55.7 1.4 %shard_map.124 = bf16[2048,128]{1,0:T(8,128)(2,1)S(1)} custom-call(bf16[2048,128]{1,0:T(8,128)(2,1)S(1)} %bitcast.20, f32[16,128,128]{2,1,0:T(8,128)S(1)} %copy-done.9), custom_call_target="tpu_custom_call" | custom-call | flops 10000000 | bytes 2097152 | tf_op jit(solution)/shard_map/pallas_call | solution.py:271
  57.1 17.5 %all_to_all.31 = bf16[128,16,128]{2,1,0:T(8,128)(2,1)S(1)} all-to-all(bf16[128,16,128]{2,1,0:T(8,128)(2,1)S(1)} %bitcast.25), channel_id=1, replica_groups=mesh['row'=16,'col'=8] {'row','col'}, dimensions={0} | all-to-all | bytes 1048576 | tf_op jit(solution)/shard_map/all_to_all | solution.py:283
  74.6 1.7 %shard_map.125 = bf16[3072,128]{1,0:T(8,128)(2,1)} custom-call(bf16[2048,128]{1,0:T(8,128)(2,1)S(1)} %bitcast.24, bf16[384,512]{1,0:T(8,128)(2,1)S(1)} %get-tuple-element.28.left_ref, bf16[512,512]{1,0:T(8,128)(2,1)S(1)} %copy-done.15), custom_call_target="tpu_custom_call" | custom-call | flops 400000000 | bytes 2228224 | tf_op jit(solution)/shard_map/pallas_call | solution.py:271
  76.3 5.5 %all-to-all-start.3 = ((bf16[128,24,128]{2,1,0:T(8,128)(2,1)}), bf16[128,24,128]{2,1,0:T(8,128)(2,1)S(1)}, u32[]{:S(2)}, u32[]{:S(2)}) async-start(bf16[128,24,128]{2,1,0:T(8,128)(2,1)} %bitcast.13), calls=%async_computation.3 | async-start | bytes 1572864 | tf_op jit(solution)/shard_map/all_to_all | solution.py:283
  81.9 1.0 copy-done.7
  82.8 1.1 copy-done.13
  83.9 1.0 copy-done.19
  84.8 1.7 %shard_map.123 = (bf16[1152,128]{1,0:T(8,128)(2,1)}, f32[1152,128]{1,0:T(8,128)S(1)}, f32[2,128,128]{2,1,0:T(8,128)S(1)}) custom-call(bf16[2048,128]{1,0:T(8,128)(2,1)S(1)} %bitcast.21, bf16[128,128]{1,0:T(8,128)(2,1)S(1)} %copy-done.20, f32[1,128]{1,0:T(1,128)S(1)} %bitcast.35, f32[1,128]{1,0:T(1,128)S(1)} %bitcast.38, f32[1152,128]{1,0:T(8,128)S(1)} %copy-done.13, ...), custom_call_target="tpu_custom_call" | custom-call | flops 200000000 | bytes 3212288 | tf_op jit(solution)/shard_map/pallas_call | solution.py:271
  86.5 0.8 copy-done.10
  87.4 9.4 %all-to-all-done.3 = bf16[128,24,128]{2,1,0:T(8,128)(2,1)S(1)} async-done(((bf16[128,24,128]{2,1,0:T(8,128)(2,1)}), bf16[128,24,128]{2,1,0:T(8,128)(2,1)S(1)}, u32[]{:S(2)}, u32[]{:S(2)}) %all-to-all-start.3) | async-done | bytes 786464 | tf_op jit(solution)/shard_map/all_to_all | solution.py:283
  96.8 1.4 %copy-done.1 = f32[24,128,128]{2,1,0:T(8,128)S(1)} copy-done((f32[24,128,128]{2,1,0:T(8,128)S(1)}, f32[24,128,128]{2,1,0:T(8,128)}, u32[]{:S(2)}) %copy-start.1) | copy-done | bytes 1572888
  98.2 0.9 shard_map.126
  99.1 1.2 copy-done.2
  100.3 15.4 %all_to_all.32 = bf16[128,8,128]{2,1,0:T(8,128)(2,1)S(1)} all-to-all(bf16[128,8,128]{2,1,0:T(8,128)(2,1)S(1)} %bitcast.33), channel_id=1, replica_groups=mesh['row'=16,'col'=8] {'row','col'}, dimensions={0} | all-to-all | bytes 524288 | tf_op jit(solution)/shard_map/all_to_all | solution.py:283
  115.7 0.9 shard_map.128
  116.5 5.1 %all-to-all-start.5 = ((bf16[128,8,128]{2,1,0:T(8,128)(2,1)}), bf16[128,8,128]{2,1,0:T(8,128)(2,1)S(1)}, u32[]{:S(2)}, u32[]{:S(2)}) async-start(bf16[128,8,128]{2,1,0:T(8,128)(2,1)} %bitcast.18), calls=%async_computation.5 | async-start | bytes 524288 | tf_op jit(solution)/shard_map/all_to_all | solution.py:283
  121.7 1.1 copy-done.11
  122.7 1.0 copy-done.17
  123.7 5.0 %shard_map.127 = bf16[1152,128]{1,0:T(8,128)(2,1)} custom-call(bf16[24,256,128]{2,1,0:T(8,128)(2,1)S(1)} %copy-done.3, f32[1152,128]{1,0:T(8,128)S(1)} %copy-done.11, bf16[1152,128]{1,0:T(8,128)(2,1)S(1)} %bitcast.32, f32[1,128]{1,0:T(1,128)S(1)} %bitcast.37, bf16[128,640]{1,0:T(8,128)(2,1)S(1)} %copy-done.5), custom_call_target="tpu_custom_call" | custom-call | flops 400000000 | bytes 2916864 | tf_op jit(solution)/shard_map/pallas_call | solution.py:271
  128.7 3.1 %all-to-all-done.5 = bf16[128,8,128]{2,1,0:T(8,128)(2,1)S(1)} async-done(((bf16[128,8,128]{2,1,0:T(8,128)(2,1)}), bf16[128,8,128]{2,1,0:T(8,128)(2,1)S(1)}, u32[]{:S(2)}, u32[]{:S(2)}) %all-to-all-start.5) | async-done | bytes 262176 | tf_op jit(solution)/shard_map/all_to_all | solution.py:283
  131.7 0.9 shard_map.129
  (42 shorter events, 4.9 us)
Async XLA Ops:
  1.3 0.9 copy-start.4
  2.2 1.0 copy-start.16
  3.2 0.7 copy-start.21
  3.9 0.7 copy-start.23
  4.5 0.7 copy-start.26
  7.0 1.2 copy-start
  8.2 34.1 %copy-start.5 = (bf16[128,640]{1,0:T(8,128)(2,1)S(1)}, bf16[128,640]{1,0:T(8,128)(2,1)}, u32[]{:S(2)}) copy-start(bf16[128,640]{1,0:T(8,128)(2,1)} %w_ref.7) | copy-start | bytes 491524
  8.2 34.1 %copy-start.6 = (bf16[24,48,128]{2,1,0:T(8,128)(2,1)S(1)}, bf16[24,48,128]{2,1,0:T(8,128)(2,1)}, u32[]{:S(2)}) copy-start(bf16[24,48,128]{2,1,0:T(8,128)(2,1)} %param.17) | copy-start | bytes 884740
  8.2 34.1 %copy-start.20 = (bf16[128,128]{1,0:T(8,128)(2,1)S(1)}, bf16[128,128]{1,0:T(8,128)(2,1)}, u32[]{:S(2)}) copy-start(bf16[128,128]{1,0:T(8,128)(2,1)} %w_out_ref.3) | copy-start | bytes 98308
  8.2 34.1 %copy-start.22 = (f32[128]{0:T(128)S(1)}, f32[128]{0:T(128)}, u32[]{:S(2)}) copy-start(f32[128]{0:T(128)} %param.14) | copy-start | bytes 1540
  36.0 0.8 copy-start.14
  36.8 17.7 %all-to-all-start.1 = ((bf16[128,16,128]{2,1,0:T(8,128)(2,1)}), bf16[128,16,128]{2,1,0:T(8,128)(2,1)S(1)}, u32[]{:S(2)}, u32[]{:S(2)}) async-start(bf16[128,16,128]{2,1,0:T(8,128)(2,1)} %bitcast.5), calls=%async_computation.1 | async-start | bytes 1048576 | tf_op jit(solution)/shard_map/all_to_all | solution.py:283
  43.0 1.0 copy-start.8
  44.0 0.8 copy-start.12
  44.9 0.7 copy-start.18
  54.5 1.2 copy-start.9
  55.7 18.9 %copy-start.15 = (bf16[512,512]{1,0:T(8,128)(2,1)S(1)}, bf16[512,512]{1,0:T(8,128)(2,1)}, u32[]{:S(2)}) copy-start(bf16[512,512]{1,0:T(8,128)(2,1)} %copy-done.14) | copy-start | bytes 1572868
  74.6 7.2 %copy-start.25 = (f32[128]{0:T(128)S(1)}, f32[128]{0:T(128)}, u32[]{:S(2)}) copy-start(f32[128]{0:T(128)} %param.15) | copy-start | bytes 1540
  76.3 20.5 %all-to-all-start.3 = ((bf16[128,24,128]{2,1,0:T(8,128)(2,1)}), bf16[128,24,128]{2,1,0:T(8,128)(2,1)S(1)}, u32[]{:S(2)}, u32[]{:S(2)}) async-start(bf16[128,24,128]{2,1,0:T(8,128)(2,1)} %bitcast.13), calls=%async_computation.3 | async-start | bytes 1572864 | tf_op jit(solution)/shard_map/all_to_all | solution.py:283
  81.9 1.0 copy-start.7
  82.8 1.1 copy-start.13
  83.9 1.0 copy-start.19
  86.5 0.8 copy-start.10
  96.8 1.4 %copy-start.1 = (f32[24,128,128]{2,1,0:T(8,128)S(1)}, f32[24,128,128]{2,1,0:T(8,128)}, u32[]{:S(2)}) copy-start(f32[24,128,128]{2,1,0:T(8,128)} %copy-done) | copy-start | bytes 4718596
  99.1 1.2 copy-start.2
  100.3 21.4 %copy-start.24 = (f32[128]{0:T(128)S(1)}, f32[128]{0:T(128)}, u32[]{:S(2)}) copy-start(f32[128]{0:T(128)} %param.11) | copy-start | bytes 1540
  100.3 21.4 %copy-start.3 = (bf16[24,256,128]{2,1,0:T(8,128)(2,1)S(1)}, bf16[24,256,128]{2,1,0:T(8,128)(2,1)}, u32[]{:S(2)}) copy-start(bf16[24,256,128]{2,1,0:T(8,128)(2,1)} %copy-done.2) | copy-start | bytes 4718596
  116.5 15.2 %all-to-all-start.5 = ((bf16[128,8,128]{2,1,0:T(8,128)(2,1)}), bf16[128,8,128]{2,1,0:T(8,128)(2,1)S(1)}, u32[]{:S(2)}, u32[]{:S(2)}) async-start(bf16[128,8,128]{2,1,0:T(8,128)(2,1)} %bitcast.18), calls=%async_computation.5 | async-start | bytes 524288 | tf_op jit(solution)/shard_map/all_to_all | solution.py:283
  121.7 1.1 copy-start.11
  122.7 1.0 copy-start.17

commit v2 on v0

v2 whole, which is shorter than its diff:
```python
import jax
import jax.numpy as jnp
from jax import lax
from jax.experimental import pallas as pl
from jax.experimental.pallas import tpu as pltpu
from jax.sharding import PartitionSpec as P

F32 = jnp.float32
BF16 = jnp.bfloat16
EPS = 1e-05
AXES = ("row", "col")

A, B, HALF, LANES = 24, 48, 64, 128
NR, NC, ND = 16, 8, 128
CELLS = A * B
H = 128
N = NR * A
BOTH, ONE, SUMS = 18, 12, 6
GROUP = NC * BOTH
SINGLE = NC * ONE

NT = ((1,), (1,))
TN = ((0,), (0,))
NN = ((1,), (0,))
VMEM_SPEC = pl.BlockSpec(memory_space=pltpu.VMEM)
HBM_SPEC = pl.BlockSpec(memory_space=pltpu.HBM)


def dot(x, y, contract):
    return lax.dot_general(x, y, (contract, ((), ())), preferred_element_type=F32)


def roll(x, shift):
    return pltpu.roll(x, shift % LANES, x.ndim - 1)


def lane_of(shape):
    return lax.broadcasted_iota(jnp.int32, shape, len(shape) - 1)


def two_sided(x):
    none = jnp.zeros_like(x)
    rest = jnp.zeros((LANES - 2 * B, 2 * x.shape[1]), x.dtype)
    return jnp.concatenate(
        [jnp.concatenate([x, none], 1), jnp.concatenate([none, x], 1), rest], 0
    )


def row_cells(ref, q):
    none = jnp.zeros((HALF - B, H), BF16)
    return jnp.concatenate(
        [ref[q * B : (q + 1) * B, :], none, ref[(q + ONE) * B : (q + ONE + 1) * B, :], none], 0
    )


def column(row):
    at = lax.broadcasted_iota(jnp.int32, (H, LANES), 0)
    return jnp.sum(jnp.where(at == lane_of((H, LANES)), row, 0.0), 1, keepdims=True)


def stacked_weights(w_ref, first, second):
    part = [w_ref[:, p * H : (p + 1) * H].astype(F32).T.astype(BF16) for p in range(4)]
    value = jnp.concatenate([part[2 * first], part[2 * second]], 1)
    gate = jnp.concatenate([part[2 * first + 1], part[2 * second + 1]], 1)
    return jnp.concatenate([value, gate], 0)


def column_mask(mask_s):
    start = lax.axis_index("col") * B
    lane = lane_of((8, LANES))
    place = jnp.where(lane < B, lane, lane - B)
    out = jnp.zeros((8, LANES), F32)
    for b in range(B):
        out = jnp.where(place == b, mask_s[start + b].astype(F32), out)
    return out[0:1, :]


def gate_parts(weights, normed, pair_at, col_mask, mask_s):
    cells = jnp.concatenate([two_sided(normed[:B]), two_sided(normed[B:])], 0)
    pre = dot(weights, cells, NT)
    start = lax.axis_index("row") * A
    for k in range(2):
        value = pre[:H, k * LANES : (k + 1) * LANES]
        gate = jax.nn.sigmoid(pre[H:, k * LANES : (k + 1) * LANES])
        seen = col_mask * mask_s[start + 2 * pair_at + k].astype(F32)
        yield value, gate, gate * seen


def pack_both(block, third, a):
    shift = LANES - 32 if a < 8 else HALF
    return jnp.where(lane_of(block.shape) < 2 * B, block, roll(third, shift))


def pack_tail(third, n):
    lane = lane_of(third(n).shape)
    out = roll(third(n), -HALF)
    for m in range(1, 4):
        out = jnp.where(lane >= 32 * m, roll(third(2 * m + n), 32 * m - HALF), out)
    return out


def unpack_third(block, s):
    first, second, last = block(s), block(8 + s), block(16 + s % 2)
    lane = lane_of(first.shape)
    return jnp.where(
        lane < 32, roll(first, 32),
        jnp.where(lane < HALF, roll(second, HALF), roll(last, HALF - 32 * (s // 2))),
    )


def norm_rows(x):
    center = x - jnp.mean(x, 1, keepdims=True)
    scale = lax.rsqrt(jnp.mean(center * center, 1, keepdims=True) + EPS)
    return center * scale, scale


def norm_cells(x):
    center = x - jnp.mean(x, 0, keepdims=True)
    scale = lax.rsqrt(jnp.mean(center * center, 0, keepdims=True) + EPS)
    return center * scale, scale


def project_kernel(mask_h, pair_h, gain_h, bias_h, w_h, send_ref, normed_ref,
                   mask_s, pair_v, gain_v, bias_v, w_v, third, scratch, sems):
    copies = [
        pltpu.make_async_copy(src, dst, sems.at[n])
        for n, (src, dst) in enumerate(
            [(w_h, w_v), (pair_h, pair_v), (mask_h, mask_s), (gain_h, gain_v), (bias_h, bias_v)]
        )
    ]
    for copy in copies:
        copy.start()
    for copy in copies:
        copy.wait()
    weights = stacked_weights(w_v, 0, 1)
    col_mask = column_mask(mask_s)
    gain, bias = gain_v[...], bias_v[...]
    for pair_at in (8, 9, 10, 11, 0, 1, 2, 3, 4, 5, 6, 7):
        rows = pl.ds(pair_at * 2 * B, 2 * B)
        normal, _ = norm_rows(pair_v[rows, :].astype(F32))
        normed = (normal * gain + bias).astype(BF16)
        normed_ref[rows, :] = normed
        for k, (value, _, pg) in enumerate(gate_parts(weights, normed, pair_at, col_mask, mask_s)):
            a = pair_at * 2 + k
            if a >= 16:
                third[a - 16] = pg * value
            else:
                scratch[pl.ds(a, H, stride=BOTH), :] = pack_both(pg * value, third[a % 8], a)
        if pair_at == 11:
            for n in range(2):
                scratch[pl.ds(16 + n, H, stride=BOTH), :] = pack_tail(lambda s: third[s], n)
    send_ref[...] = scratch[...].astype(BF16)


def gate_kernel(normed_ref, w_ref, cot_ref, pair_ref, dproj_ref, normal_ref, scale_ref):
    sig = jax.nn.sigmoid(dot(normed_ref[...], w_ref[:, 4 * H :], NN))
    dproj_ref[...] = (cot_ref[...].astype(F32) * sig).astype(BF16)
    normal, scale = norm_rows(pair_ref[...].astype(F32))
    normal_ref[...] = normal
    scale_ref[...] = jnp.broadcast_to(scale, (CELLS, H))


def order_matrix():
    target = lax.broadcasted_iota(jnp.int32, (512, N), 0)
    at = lax.broadcasted_iota(jnp.int32, (512, N), 1)
    a, r = at >> 4, at & 15
    place = (r >> 1) * HALF + (r & 1) * A + a
    return jnp.where(target == place, 1.0, 0.0).astype(BF16)


def mix_kernel(recv_ref, send_ref, both_h, order_ref, scratch, both, right, mixed, out, sem):
    scratch[...] = recv_ref[...].astype(F32)
    lane = lane_of((NR, LANES))
    for c in range(NC):
        block = lambda p: scratch[pl.ds(c * BOTH + p, NR, stride=GROUP), :]
        lanes = slice(c * LANES, (c + 1) * LANES)
        for a in range(A):
            x = block(a) if a < 16 else unpack_third(block, a - 16)
            rows = slice(a * NR, (a + 1) * NR)
            both[rows, lanes] = x.astype(BF16)
            right[rows, lanes] = jnp.where(lane < B, roll(x, -B), 0.0).astype(BF16)
    copy = pltpu.make_async_copy(both, both_h, sem)
    copy.start()
    order = order_matrix()
    order_ref[...] = order
    product = dot(both[...], right[...], NT).astype(BF16)
    mixed[...] = dot(product, order, NT)
    low = lane < HALF
    for q in range(ONE):
        for p in range(NC // 2):
            lanes = slice(p * LANES, (p + 1) * LANES)
            x = mixed[q * NR : (q + 1) * NR, lanes]
            y = mixed[(q + ONE) * NR : (q + ONE + 1) * NR, lanes]
            out[pl.ds(2 * p * ONE + q, NR, stride=SINGLE), :] = jnp.where(low, x, roll(y, HALF))
            out[pl.ds((2 * p + 1) * ONE + q, NR, stride=SINGLE), :] = jnp.where(low, roll(x, HALF), y)
    send_ref[...] = out[...].astype(BF16)
    copy.wait()


def d_mixed_kernel(recv_ref, dproj_ref, w_out_ref, gain_ref, send_ref, scratch):
    scratch[...] = recv_ref[...].astype(F32)
    gain = column(gain_ref[...])
    w_out = w_out_ref[...]
    for q in range(ONE):
        wt = dot(w_out, row_cells(dproj_ref, q), NT) * gain
        normal, scale = norm_cells(scratch[pl.ds(q, H, stride=ONE), :])
        scratch[pl.ds(q, H, stride=ONE), :] = scale * (
            wt - jnp.mean(wt, 0, keepdims=True) - normal * jnp.mean(wt * normal, 0, keepdims=True)
        )
    send_ref[...] = scratch[...].astype(BF16)


def update_kernel(mask_s, recv_ref, w_out_ref, gain_ref, bias_ref, dproj_ref, cot_ref,
                  normed_ref, w_ref, update_ref, d_og_ref, grads_ref, pg_h, pvg_h,
                  scratch, pg_v, pvg_v, sems):
    weights = stacked_weights(w_ref, 1, 0)
    col_mask = column_mask(mask_s)
    for pair_at in range(A // 2):
        normed = normed_ref[pl.ds(pair_at * 2 * B, 2 * B), :]
        for k, (value, gate, pg) in enumerate(gate_parts(weights, normed, pair_at, col_mask, mask_s)):
            pg_v[2 * pair_at + k] = pg.astype(BF16)
            pvg_v[2 * pair_at + k] = (pg * value * (1.0 - gate)).astype(BF16)
    copies = [pltpu.make_async_copy(pg_v, pg_h, sems.at[0]),
              pltpu.make_async_copy(pvg_v, pvg_h, sems.at[1])]
    for copy in copies:
        copy.start()
    scratch[...] = recv_ref[...].astype(F32)
    gain, bias = column(gain_ref[...]), column(bias_ref[...])
    w_out, w_og = w_out_ref[...], w_ref[:, 4 * H :]
    grad = jnp.zeros((H, H), F32)
    for q in range(ONE):
        normal, _ = norm_cells(scratch[pl.ds(q, H, stride=ONE), :])
        out_normed = (normal * gain + bias).astype(BF16)
        projected = dot(out_normed, w_out, TN)
        grad = grad + dot(out_normed, row_cells(dproj_ref, q), NN)
        for k in range(2):
            rows = pl.ds((q + ONE * k) * B, B)
            sig = jax.nn.sigmoid(dot(normed_ref[rows, :], w_og, NN))
            proj = projected[k * HALF : k * HALF + B]
            update_ref[rows, :] = (sig * proj).astype(BF16)
            d_og_ref[rows, :] = (
                cot_ref[rows, :].astype(F32) * proj * sig * (1.0 - sig)
            ).astype(BF16)
    grads_ref[0] = dot(d_og_ref[...], normed_ref[...], TN)
    grads_ref[1] = grad
    for copy in copies:
        copy.wait()


def back_kernel(recv_ref, both_h, order_ref, send_ref, both, scratch, d_tile, first, second, out, sem):
    copy = pltpu.make_async_copy(both_h, both, sem)
    copy.start()
    scratch[...] = recv_ref[...].astype(F32)
    low = lane_of((NR, LANES)) < HALF
    for q in range(ONE):
        for p in range(NC // 2):
            lanes = slice(p * LANES, (p + 1) * LANES)
            x = scratch[pl.ds(2 * p * ONE + q, NR, stride=SINGLE), :]
            y = scratch[pl.ds((2 * p + 1) * ONE + q, NR, stride=SINGLE), :]
            d_tile[q * NR : (q + 1) * NR, lanes] = jnp.where(low, x, roll(y, HALF)).astype(BF16)
            d_tile[(q + ONE) * NR : (q + ONE + 1) * NR, lanes] = (
                jnp.where(low, roll(x, HALF), y).astype(BF16)
            )
    d = dot(d_tile[...], order_ref[...], NN).astype(BF16)
    copy.wait()
    first[...] = dot(d, both[...], TN)
    second[...] = dot(d, both[...], NN)
    lane = lane_of((NR, LANES))
    for c in range(NC):
        lanes = slice(c * LANES, (c + 1) * LANES)

        def block(a):
            rows = slice(a * NR, (a + 1) * NR)
            return jnp.where(lane < B, first[rows, lanes], second[rows, lanes])

        third = [block(16 + s) for s in range(8)]
        for a in range(16):
            out[pl.ds(c * BOTH + a, NR, stride=GROUP), :] = pack_both(block(a), third[a % 8], a)
        for n in range(2):
            out[pl.ds(c * BOTH + 16 + n, NR, stride=GROUP), :] = pack_tail(lambda s: third[s], n)
    send_ref[...] = out[...].astype(BF16)


def start_gates(pg_h, pvg_h, pg_v, pvg_v, sems):
    copies = []
    for pair_at in range(A // 2):
        part = pl.ds(2 * pair_at, 2)
        two = [pltpu.make_async_copy(src.at[part], dst.at[part], sems.at[n, pair_at])
               for n, (src, dst) in enumerate([(pg_h, pg_v), (pvg_h, pvg_v)])]
        for copy in two:
            copy.start()
        copies.append(two)
    return copies


def gated(scratch, a, pg_v, pvg_v):
    block = lambda p: scratch[pl.ds(p, H, stride=BOTH), :]
    d = block(a) if a < 16 else unpack_third(block, a - 16)
    return jnp.concatenate([d * pg_v[a].astype(F32), d * pvg_v[a].astype(F32)], 0).astype(BF16)


def grad_kernel(recv_ref, pg_h, pvg_h, normed_ref, grads_ref, send_ref,
                scratch, packed, pg_v, pvg_v, sems):
    copies = start_gates(pg_h, pvg_h, pg_v, pvg_v, sems)
    scratch[...] = recv_ref[...].astype(F32)
    packed[pl.ds(4, H, stride=SUMS), :] = grads_ref[0]
    packed[pl.ds(5, H, stride=SUMS), :] = grads_ref[1]
    total = jnp.zeros((2 * H, 2 * H), F32)
    for pair_at in range(A // 2):
        for copy in copies[pair_at]:
            copy.wait()
        a = 2 * pair_at
        sides = [gated(scratch, a + k, pg_v, pvg_v) for k in range(2)]
        cells = [two_sided(normed_ref[(a + k) * B : (a + k + 1) * B, :]) for k in range(2)]
        total = total + dot(jnp.concatenate(sides, 1), jnp.concatenate(cells, 0), NN)
    for g, block in enumerate([total[:H, H:], total[H:, H:], total[:H, :H], total[H:, :H]]):
        packed[pl.ds(g, H, stride=SUMS), :] = block
    send_ref[...] = packed[...].astype(BF16)


def pair_grad_kernel(recv_ref, pg_h, pvg_h, d_og_ref, normal_ref, scale_ref, gain_ref, w_ref,
                     out_ref, scratch, pg_v, pvg_v, sems):
    copies = start_gates(pg_h, pvg_h, pg_v, pvg_v, sems)
    scratch[...] = recv_ref[...].astype(F32)
    weights = stacked_weights(w_ref, 1, 0)
    w_og = w_ref[:, 4 * H :]
    gain = gain_ref[...]
    for a in range(A):
        if a % 2 == 0:
            for copy in copies[a // 2]:
                copy.wait()
        rows = pl.ds(a * B, B)
        both = dot(gated(scratch, a, pg_v, pvg_v), weights, TN)
        d = both[:B, :H] + both[B : 2 * B, H:] + dot(d_og_ref[rows, :], w_og, NT)
        normal = normal_ref[rows, :]
        weighted = d * gain
        out_ref[rows, :] = (
            scale_ref[rows, :] * (weighted - jnp.mean(weighted, 1, keepdims=True)
                                  - normal * jnp.mean(weighted * normal, 1, keepdims=True))
        ).astype(BF16)


def sum_kernel(recv_ref, send_ref):
    parts = jnp.sum(recv_ref[...].astype(F32).reshape(16, 8 * SUMS, LANES), 0)
    total = parts[:SUMS]
    for k in range(1, 8):
        total = total + parts[k * SUMS : (k + 1) * SUMS]
    many = jnp.concatenate([total] * 8, 0).astype(BF16)
    for s in range(16):
        send_ref[s * 8 * SUMS : (s + 1) * 8 * SUMS, :] = many


def unpack_kernel(recv_ref, w_in_ref, w_out_ref, scratch):
    scratch[...] = recv_ref[...].astype(F32)
    for g in range(5):
        w_in_ref[:, g * H : (g + 1) * H] = scratch[pl.ds(g, H, stride=SUMS), :].T
    w_out_ref[...] = scratch[pl.ds(5, H, stride=SUMS), :]


def call(kernel, args, outs, scratch, flops, hbm_in=(), smem_in=(), hbm_out=()):
    shapes = [jax.ShapeDtypeStruct(s, d) for s, d in outs]
    specs = [
        HBM_SPEC if n in hbm_in else pl.BlockSpec(memory_space=pltpu.SMEM) if n in smem_in else VMEM_SPEC
        for n in range(len(args))
    ]
    moved = sum(v.size * v.dtype.itemsize for v in list(args) + shapes)
    return pl.pallas_call(
        kernel,
        out_shape=shapes,
        in_specs=specs,
        out_specs=[HBM_SPEC if n in hbm_out else VMEM_SPEC for n in range(len(shapes))],
        scratch_shapes=scratch,
        cost_estimate=pl.CostEstimate(flops=flops, bytes_accessed=moved, transcendentals=0),
        compiler_params=pltpu.CompilerParams(vmem_limit_bytes=40 * 2**20),
    )(*args)


def vm(*shape, dtype=F32):
    return pltpu.VMEM(shape, dtype)


def exchange(x, *tile):
    moved = lax.all_to_all(x.reshape(ND, *tile, LANES), AXES, 0, 0, tiled=True)
    return moved.reshape(x.shape)


def on_device(pair, mask, in_gain, in_bias, w_in, out_gain, out_bias, w_out, cotangent):
    pair2 = pair.reshape(CELLS, H)
    cot2 = cotangent.reshape(CELLS, H)
    line = lambda v: v.reshape(1, -1)
    dma = pltpu.SemaphoreType.DMA
    both_shape, one_shape, sum_shape = ((ND * n, LANES) for n in (BOTH, ONE, SUMS))
    gates = [vm(A, H, LANES, dtype=BF16)] * 2

    send, normed = call(
        project_kernel,
        [mask, pair2, line(in_gain), line(in_bias), w_in],
        [(both_shape, BF16), ((CELLS, H), BF16)],
        [pltpu.SMEM((N,), jnp.int32), vm(CELLS, H, dtype=BF16), vm(1, H), vm(1, H),
         vm(H, 5 * H, dtype=BF16), vm(8, H, LANES), vm(*both_shape), dma((5,))],
        400_000_000, hbm_in=range(5),
    )
    recv = exchange(send, 9, 2)
    dproj, normal, scale = call(
        gate_kernel,
        [normed, w_in, cot2, pair2],
        [((CELLS, H), BF16), ((CELLS, H), F32), ((CELLS, H), F32)],
        [],
        100_000_000,
    )
    send, both, order = call(
        mix_kernel,
        [recv],
        [(one_shape, BF16), ((N, NC * LANES), BF16), ((512, N), BF16)],
        [vm(*both_shape), vm(N, NC * LANES, dtype=BF16), vm(N, NC * LANES, dtype=BF16),
         vm(N, 512), vm(*one_shape), dma],
        400_000_000, hbm_out=(1,),
    )
    mixed = exchange(send, 3, 4)
    (send,) = call(
        d_mixed_kernel,
        [mixed, dproj, w_out, line(out_gain)],
        [(one_shape, BF16)],
        [vm(*one_shape)],
        50_000_000,
    )
    recv = exchange(send, 3, 4)
    update, d_og, grads, pg, pvg = call(
        update_kernel,
        [mask, mixed, w_out, line(out_gain), line(out_bias), dproj, cot2, normed, w_in],
        [((CELLS, H), BF16), ((CELLS, H), BF16), ((2, H, H), F32),
         ((A, H, LANES), BF16), ((A, H, LANES), BF16)],
        [vm(*one_shape), *gates, dma((2,))],
        600_000_000, smem_in=(0,), hbm_out=(3, 4),
    )
    (send,) = call(
        back_kernel,
        [recv, both, order],
        [(both_shape, BF16)],
        [vm(N, NC * LANES, dtype=BF16), vm(*one_shape), vm(N, 512, dtype=BF16),
         vm(N, NC * LANES), vm(N, NC * LANES), vm(*both_shape), dma],
        800_000_000, hbm_in=(1,),
    )
    recv = exchange(send, 9, 2)
    (send,) = call(
        grad_kernel,
        [recv, pg, pvg, normed, grads],
        [(sum_shape, BF16)],
        [vm(*both_shape), vm(*sum_shape), *gates, dma((2, A // 2))],
        400_000_000, hbm_in=(1, 2),
    )
    parts = exchange(send, 3, 2)
    (pair_grad,) = call(
        pair_grad_kernel,
        [recv, pg, pvg, d_og, normal, scale, line(in_gain), w_in],
        [((CELLS, H), BF16)],
        [vm(*both_shape), *gates, dma((2, A // 2))],
        400_000_000, hbm_in=(1, 2),
    )
    (send,) = call(sum_kernel, [parts], [(sum_shape, BF16)], [], 1_000_000)
    sums = exchange(send, 3, 2)
    w_in_grad, w_out_grad = call(
        unpack_kernel,
        [sums],
        [((H, 5 * H), F32), ((H, H), F32)],
        [vm(*sum_shape)],
        1_000_000,
    )
    return (update.reshape(A, B, H), pair_grad.reshape(A, B, H), w_in_grad, w_out_grad)


def solution(mesh):
    placed = (P("row", "col", None), P(), P(), P(), P(), P(), P(), P(), P("row", "col", None))
    return jax.shard_map(
        on_device,
        mesh=mesh,
        in_specs=placed,
        out_specs=(P("row", "col", None), P("row", "col", None), P(), P()),
        check_vma=False,
    )
```

time: 456 us -> 127 us (0.28); the launches traced: 449 us -> 127 us
  waiting for transfers between devices: 156 us -> 16.4 us
  local copies, waits for them, and re-layouts: 119 us -> 9.59 us
  other arithmetic: 82.4 us -> 0 us
  blocking collectives: 16 us -> 55.6 us
  Pallas kernels: 0 us -> 28.8 us
  starting transfers between devices: 43.7 us -> 15.5 us
  matrix products: 17 us -> 0 us
  between operations: 14.8 us -> 0.84 us
    psum x1 -> x0, waiting for transfers between devices: 145 us -> none  [on_device(): grad_in, grad_out = lax.psum((grad_in, grad_out), ('row', 'col'))]
    unnamed x7 -> x0, other arithmetic: 59.3 us -> none
    convert_element_type x7 -> x0, local copies, waits for them, and re-layouts: 48.3 us -> none  [the longest x1 13 us: on_device(): disassemble(mixed_chan, n_row, n_col, tile_rows, tile_cols)]
    all_to_all x1 -> x3, blocking collectives: 16 us -> 55.6 us  [exchange(): moved = lax.all_to_all(x.reshape(ND, *tile, LANES), AXES, 0, 0, tiled=True)]
    unnamed x43 -> x36, local copies, waits for them, and re-layouts: 42.9 us -> 9.59 us
    pallas_call x0 -> x10, Pallas kernels: none -> 28.8 us  [call(): pl.pallas_call(kernel, out_shape=shapes, in_specs=specs, out_specs=[HBM_S...]
    all_to_all x5 -> x3, starting transfers between devices: 43.6 us -> 15.5 us  [exchange(): moved = lax.all_to_all(x.reshape(ND, *tile, LANES), AXES, 0, 0, tiled=True)]
    dot_general x9 -> x0, matrix products: 17 us -> none  [the longest x1 2.47 us: on_device(): jnp.dot(out_flat, w_out, preferred_element_type=jnp.float32)]
  transfers between devices with their start and end apart: 6 -> 3, of which waited for: 4 -> 3; matrix products, arithmetic and copies ran while one was open for 16% -> 0% of each run, Pallas kernels for 0% -> 9%
where the time goes in v2:
time: 127 us
  blocking collectives  55.6 us (44%)
  Pallas kernels  28.8 us (23%)
  waiting for transfers between devices  16.4 us (13%)
  starting transfers between devices  15.5 us (12%)
  local copies, waits for them, and re-layouts  9.59 us (8%)
    all_to_all x3, blocking collectives, exchange(): moved = lax.all_to_all(x.reshape(ND, *tile, LANES), AXES, 0, 0, tiled=True)  55.6 us
    pallas_call x10, Pallas kernels, call(): pl.pallas_call(kernel, out_shape=shapes, in_specs=specs, out_specs=[HBM_S...  28.8 us
    all_to_all x3, waiting for transfers between devices, exchange(): moved = lax.all_to_all(x.reshape(ND, *tile, LANES), AXES, 0, 0, tiled=True)  16.4 us
    all_to_all x3, starting transfers between devices, exchange(): moved = lax.all_to_all(x.reshape(ND, *tile, LANES), AXES, 0, 0, tiled=True)  15.5 us
    unnamed x36, local copies, waits for them, and re-layouts  9.59 us
  transfers between devices with their start and end apart: 3, of which 3 were waited for; matrix products, arithmetic and copies ran while one was open for 0% of the time, Pallas kernels for 9%

profile of v2, /device:TPU:1, one launch (start us, length us, event | category | flops | bytes accessed | tf_op | source)
XLA Modules:
  0.0 126.7 jit_solution(17201968895670799752)
XLA Ops:
  0.7 0.7 copy-done.15
  1.3 0.9 copy-done
  2.2 1.0 copy-done.6
  3.2 2.5 %shard_map.120 = (bf16[2304,128]{1,0:T(8,128)(2,1)S(1)}, bf16[1152,128]{1,0:T(8,128)(2,1)S(1)}) custom-call(s32[384]{0:T(512)S(1)} %copy-done.15, bf16[1152,128]{1,0:T(8,128)(2,1)S(1)} %bitcast.31, f32[1,128]{1,0:T(1,128)S(1)} %bitcast.37, f32[1,128]{1,0:T(1,128)S(1)} %bitcast.39, bf16[128,640]{1,0:T(8,128)(2,1)S(1)} %copy-done), custom_call_target="tpu_custom_call" | custom-call | flops 400000000 | bytes 1346048 | tf_op jit(solution)/shard_map/pallas_call | solution.py:367
  5.7 24.2 %all_to_all.30 = bf16[128,9,2,128]{3,2,1,0:T(2,128)(2,1)S(1)} all-to-all(bf16[128,9,2,128]{3,2,1,0:T(2,128)(2,1)S(1)} %bitcast.29), channel_id=1, replica_groups=mesh['row'=16,'col'=8] {'row','col'}, dimensions={0} | all-to-all | bytes 1179648 | tf_op jit(solution)/shard_map/all_to_all | solution.py:383
  29.8 6.0 %shard_map.121 = (bf16[1536,128]{1,0:T(8,128)(2,1)}, bf16[384,1024]{1,0:T(8,128)(2,1)S(1)}, bf16[512,384]{1,0:T(8,128)(2,1)S(1)}) custom-call(bf16[2304,128]{1,0:T(8,128)(2,1)S(1)} %bitcast.28), custom_call_target="tpu_custom_call" | custom-call | flops 400000000 | bytes 2162688 | tf_op jit(solution)/shard_map/pallas_call | solution.py:367
  35.8 0.0 copy-start.1
  35.8 0.0 copy-start.7
  35.8 5.5 %all-to-all-start.1 = ((bf16[128,3,4,128]{3,2,1,0:T(4,128)(2,1)}), bf16[128,3,4,128]{3,2,1,0:T(4,128)(2,1)S(1)}, u32[]{:S(2)}, u32[]{:S(2)}) async-start(bf16[128,3,4,128]{3,2,1,0:T(4,128)(2,1)} %bitcast.5), calls=%async_computation.1 | async-start | bytes 786432 | tf_op jit(solution)/shard_map/all_to_all | solution.py:383
  41.4 0.5 shard_map.122
  41.9 0.8 copy-done.2
  42.7 0.8 copy-done.4
  43.6 8.9 %all-to-all-done.1 = bf16[128,3,4,128]{3,2,1,0:T(4,128)(2,1)S(1)} async-done(((bf16[128,3,4,128]{3,2,1,0:T(4,128)(2,1)}), bf16[128,3,4,128]{3,2,1,0:T(4,128)(2,1)S(1)}, u32[]{:S(2)}, u32[]{:S(2)}) %all-to-all-start.1) | async-done | bytes 393248 | tf_op jit(solution)/shard_map/all_to_all | solution.py:383
  52.5 0.7 copy-done.13
  53.2 0.7 shard_map.124
  53.9 16.2 %all_to_all.31 = bf16[128,3,4,128]{3,2,1,0:T(4,128)(2,1)S(1)} all-to-all(bf16[128,3,4,128]{3,2,1,0:T(4,128)(2,1)S(1)} %bitcast.24), channel_id=1, replica_groups=mesh['row'=16,'col'=8] {'row','col'}, dimensions={0} | all-to-all | bytes 786432 | tf_op jit(solution)/shard_map/all_to_all | solution.py:383
  70.1 3.0 %shard_map.125 = bf16[2304,128]{1,0:T(8,128)(2,1)} custom-call(bf16[1536,128]{1,0:T(8,128)(2,1)S(1)} %bitcast.30, bf16[384,1024]{1,0:T(8,128)(2,1)S(1)} %get-tuple-element.24.both_h, bf16[512,384]{1,0:T(8,128)(2,1)S(1)} %get-tuple-element.25.order_ref), custom_call_target="tpu_custom_call" | custom-call | flops 800000000 | bytes 2162688 | tf_op jit(solution)/shard_map/pallas_call | solution.py:367
  73.1 5.3 %all-to-all-start.3 = ((bf16[128,9,2,128]{3,2,1,0:T(2,128)(2,1)}), bf16[128,9,2,128]{3,2,1,0:T(2,128)(2,1)S(1)}, u32[]{:S(2)}, u32[]{:S(2)}) async-start(bf16[128,9,2,128]{3,2,1,0:T(2,128)(2,1)} %bitcast.13), calls=%async_computation.3 | async-start | bytes 1179648 | tf_op jit(solution)/shard_map/all_to_all | solution.py:383
  78.4 0.6 copy-done.17
  79.0 1.0 copy-done.9
  80.0 1.0 copy-done.11
  80.9 3.1 %shard_map.123 = (bf16[1152,128]{1,0:T(8,128)(2,1)}, bf16[1152,128]{1,0:T(8,128)(2,1)S(1)}, f32[2,128,128]{2,1,0:T(8,128)S(1)}, bf16[24,128,128]{2,1,0:T(8,128)(2,1)S(1)}, bf16[24,128,128]{2,1,0:T(8,128)(2,1)S(1)}) custom-call(s32[384]{0:T(512)S(1)} %copy-done.15, bf16[1536,128]{1,0:T(8,128)(2,1)S(1)} %bitcast.23, bf16[128,128]{1,0:T(8,128)(2,1)S(1)} %copy-done.12, ...), custom_call_target="tpu_custom_call" | custom-call | flops 600000000 | bytes 3770880 | tf_op jit(solution)/shard_map/pallas_call | solution.py:367
  84.1 7.2 %all-to-all-done.3 = bf16[128,9,2,128]{3,2,1,0:T(2,128)(2,1)S(1)} async-done(((bf16[128,9,2,128]{3,2,1,0:T(2,128)(2,1)}), bf16[128,9,2,128]{3,2,1,0:T(2,128)(2,1)S(1)}, u32[]{:S(2)}, u32[]{:S(2)}) %all-to-all-start.3) | async-done | bytes 589856 | tf_op jit(solution)/shard_map/all_to_all | solution.py:383
  91.3 4.1 %shard_map.127 = bf16[768,128]{1,0:T(8,128)(2,1)S(1)} custom-call(bf16[2304,128]{1,0:T(8,128)(2,1)S(1)} %bitcast.20, bf16[24,128,128]{2,1,0:T(8,128)(2,1)S(1)} %get-tuple-element.26.pg_h, bf16[24,128,128]{2,1,0:T(8,128)(2,1)S(1)} %get-tuple-element.27.pvg_h, bf16[1152,128]{1,0:T(8,128)(2,1)S(1)} %get-tuple-element.21.normed_ref, ...), custom_call_target="tpu_custom_call" | custom-call | flops 400000000 | bytes 2785280 | tf_op jit(solution)/shard_map/pallas_call | solution.py:367
  95.4 15.2 %all_to_all.32 = bf16[128,3,2,128]{3,2,1,0:T(2,128)(2,1)S(1)} all-to-all(bf16[128,3,2,128]{3,2,1,0:T(2,128)(2,1)S(1)} %bitcast.27), channel_id=1, replica_groups=mesh['row'=16,'col'=8] {'row','col'}, dimensions={0} | all-to-all | bytes 393216 | tf_op jit(solution)/shard_map/all_to_all | solution.py:383
  110.6 0.7 shard_map.128
  111.4 4.7 %all-to-all-start.5 = ((bf16[128,3,2,128]{3,2,1,0:T(2,128)(2,1)}), bf16[128,3,2,128]{3,2,1,0:T(2,128)(2,1)S(1)}, u32[]{:S(2)}, u32[]{:S(2)}) async-start(bf16[128,3,2,128]{3,2,1,0:T(2,128)(2,1)} %bitcast.18), calls=%async_computation.5 | async-start | bytes 393216 | tf_op jit(solution)/shard_map/all_to_all | solution.py:383
  116.1 1.1 copy-done.3
  117.1 1.1 copy-done.5
  118.2 7.4 %shard_map.126 = bf16[1152,128]{1,0:T(8,128)(2,1)} custom-call(bf16[2304,128]{1,0:T(8,128)(2,1)S(1)} %bitcast.21, bf16[24,128,128]{2,1,0:T(8,128)(2,1)S(1)} %get-tuple-element.26.pg_h, bf16[24,128,128]{2,1,0:T(8,128)(2,1)S(1)} %get-tuple-element.27.pvg_h, bf16[1152,128]{1,0:T(8,128)(2,1)S(1)} %get-tuple-element.28.d_og_ref, f32[1152,128]{1,0:T(8,128)S(1)} %copy-done.3, ...), custom_call_target="tpu_custom_call" | custom-call | flops 400000000 | bytes 4096512 | tf_op jit(solution)/shard_map/pallas_call | solution.py:367
  125.6 0.3 all-to-all-done.5
  125.8 0.9 shard_map.129
  (23 shorter events, 0.1 us)
Async XLA Ops:
  0.6 0.7 copy-start.15
  0.6 0.7 copy-start.14
  0.7 0.7 copy-start.16
  1.3 0.9 copy-start
  2.2 1.0 copy-start.6
  35.8 5.6 %copy-start.1 = (bf16[128,640]{1,0:T(8,128)(2,1)S(1)}, bf16[128,640]{1,0:T(8,128)(2,1)}, u32[]{:S(2)}) copy-start(bf16[128,640]{1,0:T(8,128)(2,1)} %w_ref.5) | copy-start | bytes 491524
  35.8 5.6 %copy-start.7 = (bf16[24,48,128]{2,1,0:T(8,128)(2,1)S(1)}, bf16[24,48,128]{2,1,0:T(8,128)(2,1)}, u32[]{:S(2)}) copy-start(bf16[24,48,128]{2,1,0:T(8,128)(2,1)} %param.9) | copy-start | bytes 884740
  35.8 5.6 %copy-start.8 = (bf16[24,48,128]{2,1,0:T(8,128)(2,1)S(1)}, bf16[24,48,128]{2,1,0:T(8,128)(2,1)}, u32[]{:S(2)}) copy-start(bf16[24,48,128]{2,1,0:T(8,128)(2,1)} %param.17) | copy-start | bytes 884740
  35.8 16.7 %all-to-all-start.1 = ((bf16[128,3,4,128]{3,2,1,0:T(4,128)(2,1)}), bf16[128,3,4,128]{3,2,1,0:T(4,128)(2,1)S(1)}, u32[]{:S(2)}, u32[]{:S(2)}) async-start(bf16[128,3,4,128]{3,2,1,0:T(4,128)(2,1)} %bitcast.5), calls=%async_computation.1 | async-start | bytes 786432 | tf_op jit(solution)/shard_map/all_to_all | solution.py:383
  41.4 11.1 %copy-start.12 = (bf16[128,128]{1,0:T(8,128)(2,1)S(1)}, bf16[128,128]{1,0:T(8,128)(2,1)}, u32[]{:S(2)}) copy-start(bf16[128,128]{1,0:T(8,128)(2,1)} %w_out_ref.3) | copy-start | bytes 98308
  41.9 0.8 copy-start.2
  42.7 0.8 copy-start.4
  43.5 10.3 %copy-start.10 = (bf16[1152,128]{1,0:T(8,128)(2,1)}, bf16[1152,128]{1,0:T(8,128)(2,1)S(1)}, u32[]{:S(2)}) copy-start(bf16[1152,128]{1,0:T(8,128)(2,1)S(1)} %get-tuple-element.22.dproj_ref) | copy-start | bytes 884740
  52.5 0.7 copy-start.13
  73.1 18.2 %all-to-all-start.3 = ((bf16[128,9,2,128]{3,2,1,0:T(2,128)(2,1)}), bf16[128,9,2,128]{3,2,1,0:T(2,128)(2,1)S(1)}, u32[]{:S(2)}, u32[]{:S(2)}) async-start(bf16[128,9,2,128]{3,2,1,0:T(2,128)(2,1)} %bitcast.13), calls=%async_computation.3 | async-start | bytes 1179648 | tf_op jit(solution)/shard_map/all_to_all | solution.py:383
  78.4 0.7 copy-start.17
  79.0 1.0 copy-start.9
  80.0 1.0 copy-start.11
  111.4 14.5 %all-to-all-start.5 = ((bf16[128,3,2,128]{3,2,1,0:T(2,128)(2,1)}), bf16[128,3,2,128]{3,2,1,0:T(2,128)(2,1)S(1)}, u32[]{:S(2)}, u32[]{:S(2)}) async-start(bf16[128,3,2,128]{3,2,1,0:T(2,128)(2,1)} %bitcast.18), calls=%async_computation.5 | async-start | bytes 393216 | tf_op jit(solution)/shard_map/all_to_all | solution.py:383
  116.0 1.1 copy-start.3
  117.1 1.1 copy-start.5

commit v3 on v2

--- a/solution.py
+++ b/solution.py
@@ -1,3 +1,5 @@
+import math
+
 import jax
 import jax.numpy as jnp
 from jax import lax
@@ -16,8 +18,6 @@
 H = 128
 N = NR * A
 BOTH, ONE, SUMS = 18, 12, 6
-GROUP = NC * BOTH
-SINGLE = NC * ONE
 
 NT = ((1,), (1,))
 TN = ((0,), (0,))
@@ -58,11 +58,11 @@
     return jnp.sum(jnp.where(at == lane_of((H, LANES)), row, 0.0), 1, keepdims=True)
 
 
-def stacked_weights(w_ref, first, second):
+def stacked_weights(w_ref):
     part = [w_ref[:, p * H : (p + 1) * H].astype(F32).T.astype(BF16) for p in range(4)]
-    value = jnp.concatenate([part[2 * first], part[2 * second]], 1)
-    gate = jnp.concatenate([part[2 * first + 1], part[2 * second + 1]], 1)
-    return jnp.concatenate([value, gate], 0)
+    return jnp.concatenate(
+        [jnp.concatenate([part[0], part[2]], 1), jnp.concatenate([part[1], part[3]], 1)], 0
+    )
 
 
 def column_mask(mask_s):
@@ -92,19 +92,19 @@
 
 
 def pack_tail(third, n):
-    lane = lane_of(third(n).shape)
-    out = roll(third(n), -HALF)
+    lane = lane_of((H, LANES))
+    out = roll(third[4 * n], -HALF)
     for m in range(1, 4):
-        out = jnp.where(lane >= 32 * m, roll(third(2 * m + n), 32 * m - HALF), out)
+        out = jnp.where(lane >= 32 * m, roll(third[4 * n + m], 32 * m - HALF), out)
     return out
 
 
 def unpack_third(block, s):
-    first, second, last = block(s), block(8 + s), block(16 + s % 2)
+    first, second, last = block(s), block(8 + s), block(16 + s // 4)
     lane = lane_of(first.shape)
     return jnp.where(
         lane < 32, roll(first, 32),
-        jnp.where(lane < HALF, roll(second, HALF), roll(last, HALF - 32 * (s // 2))),
+        jnp.where(lane < HALF, roll(second, HALF), roll(last, HALF - 32 * (s % 4))),
     )
 
 
@@ -132,7 +132,7 @@
         copy.start()
     for copy in copies:
         copy.wait()
-    weights = stacked_weights(w_v, 0, 1)
+    weights = stacked_weights(w_v)
     col_mask = column_mask(mask_s)
     gain, bias = gain_v[...], bias_v[...]
     for pair_at in (8, 9, 10, 11, 0, 1, 2, 3, 4, 5, 6, 7):
@@ -148,11 +148,13 @@
                 scratch[pl.ds(a, H, stride=BOTH), :] = pack_both(pg * value, third[a % 8], a)
         if pair_at == 11:
             for n in range(2):
-                scratch[pl.ds(16 + n, H, stride=BOTH), :] = pack_tail(lambda s: third[s], n)
+                scratch[pl.ds(16 + n, H, stride=BOTH), :] = pack_tail(third, n)
     send_ref[...] = scratch[...].astype(BF16)
 
 
-def gate_kernel(normed_ref, w_ref, cot_ref, pair_ref, dproj_ref, normal_ref, scale_ref):
+def gate_kernel(normed_ref, w_ref, cot_ref, pair_ref, gain_ref,
+                dproj_ref, normal_ref, scale_ref, spread_ref):
+    spread_ref[...] = jnp.broadcast_to(column(gain_ref[...]), (H, LANES))
     sig = jax.nn.sigmoid(dot(normed_ref[...], w_ref[:, 4 * H :], NN))
     dproj_ref[...] = (cot_ref[...].astype(F32) * sig).astype(BF16)
     normal, scale = norm_rows(pair_ref[...].astype(F32))
@@ -160,46 +162,83 @@
     scale_ref[...] = jnp.broadcast_to(scale, (CELLS, H))
 
 
-def order_matrix():
-    target = lax.broadcasted_iota(jnp.int32, (512, N), 0)
-    at = lax.broadcasted_iota(jnp.int32, (512, N), 1)
-    a, r = at >> 4, at & 15
-    place = (r >> 1) * HALF + (r & 1) * A + a
-    return jnp.where(target == place, 1.0, 0.0).astype(BF16)
-
-
-def mix_kernel(recv_ref, send_ref, both_h, order_ref, scratch, both, right, mixed, out, sem):
-    scratch[...] = recv_ref[...].astype(F32)
-    lane = lane_of((NR, LANES))
-    for c in range(NC):
-        block = lambda p: scratch[pl.ds(c * BOTH + p, NR, stride=GROUP), :]
-        lanes = slice(c * LANES, (c + 1) * LANES)
-        for a in range(A):
-            x = block(a) if a < 16 else unpack_third(block, a - 16)
-            rows = slice(a * NR, (a + 1) * NR)
-            both[rows, lanes] = x.astype(BF16)
-            right[rows, lanes] = jnp.where(lane < B, roll(x, -B), 0.0).astype(BF16)
-    copy = pltpu.make_async_copy(both, both_h, sem)
-    copy.start()
-    order = order_matrix()
-    order_ref[...] = order
-    product = dot(both[...], right[...], NT).astype(BF16)
-    mixed[...] = dot(product, order, NT)
-    low = lane < HALF
-    for q in range(ONE):
+def third_tile(scratch, start, first, second):
+    lane, at = lane_of((8, LANES)), lax.broadcasted_iota(jnp.int32, (8, LANES), 0)
+    tail = jnp.where(
+        at < 4,
+        jnp.broadcast_to(scratch[pl.ds(start + 16, 1), :], (8, LANES)),
+        jnp.broadcast_to(scratch[pl.ds(start + 17, 1), :], (8, LANES)),
+    )
+    last = roll(tail, HALF)
+    for m in range(1, 4):
+        last = jnp.where((at & 3) == m, roll(tail, HALF - 32 * m), last)
+    return jnp.where(lane < 32, roll(first, 32), jnp.where(lane < HALF, roll(second, HALF), last))
+
+
+def store_both(out, start, x):
+    lane, at = lane_of((8, LANES)), lax.broadcasted_iota(jnp.int32, (8, LANES), 0)
+    t0, t1, t2 = x[:8], x[8:16], x[16:]
+    out[pl.ds(start, 8), :] = jnp.where(lane < 2 * B, t0, roll(t2, LANES - 32))
+    out[pl.ds(start + 8, 8), :] = jnp.where(lane < 2 * B, t1, roll(t2, HALF))
+    tail = jnp.zeros((8, LANES), F32)
+    for m in range(4):
+        here = ((at & 3) == m) & (lane >= 32 * m) & (lane < 32 * m + 32)
+        tail = jnp.where(here, roll(t2, 32 * m - HALF), tail)
+    tail = tail + pltpu.roll(tail, 1, 0)
+    tail = tail + pltpu.roll(tail, 2, 0)
+    out[pl.ds(start + 16, 1), :] = tail[3:4]
+    out[pl.ds(start + 17, 1), :] = tail[7:8]
+
+
+def mix_kernel(recv_ref, send_ref, left_h, right_h, left_ref, right_ref, scratch, mixed, out, sems):
+    scratch[...] = recv_ref[...].astype(F32)
+    right_ref[...] = jnp.zeros_like(right_ref)
+    lane = lane_of((A, LANES))
+    for r2 in range(NR // 2):
+        for p in range(NC // 2):
+            lefts, rights = [], []
+            for r in (2 * r2, 2 * r2 + 1):
+                two = []
+                for c in (2 * p, 2 * p + 1):
+                    start = (r * NC + c) * BOTH
+                    top = scratch[pl.ds(start, 16), :]
+                    two.append(
+                        jnp.concatenate([top, third_tile(scratch, start, top[:8], top[8:])], 0)
+                    )
+                x, y = two
+                lefts.append(jnp.where(lane < HALF, x, roll(y, HALF)))
+                rights.append(
+                    jnp.where(
+                        lane < HALF,
+                        jnp.where(lane < B, roll(x, -B), 0.0),
+                        jnp.where(lane < HALF + B, roll(y, HALF - B), 0.0),
+                    )
+                )
+            lanes = slice(p * LANES, (p + 1) * LANES)
+            left_ref[r2 * B : (r2 + 1) * B, lanes] = jnp.concatenate(lefts, 0).astype(BF16)
+            right_ref[r2 * HALF : r2 * HALF + B, lanes] = jnp.concatenate(rights, 0).astype(BF16)
+    copies = [pltpu.make_async_copy(left_ref, left_h, sems.at[0]),
+              pltpu.make_async_copy(right_ref, right_h, sems.at[1])]
+    for copy in copies:
+        copy.start()
+    mixed[...] = dot(left_ref[...], right_ref[...], NT)
+    low = lane_of((ONE, LANES)) < HALF
+    for r in range(NR):
         for p in range(NC // 2):
             lanes = slice(p * LANES, (p + 1) * LANES)
-            x = mixed[q * NR : (q + 1) * NR, lanes]
-            y = mixed[(q + ONE) * NR : (q + ONE + 1) * NR, lanes]
-            out[pl.ds(2 * p * ONE + q, NR, stride=SINGLE), :] = jnp.where(low, x, roll(y, HALF))
-            out[pl.ds((2 * p + 1) * ONE + q, NR, stride=SINGLE), :] = jnp.where(low, roll(x, HALF), y)
+            x = mixed[pl.ds(r * A, ONE), lanes]
+            y = mixed[pl.ds(r * A + ONE, ONE), lanes]
+            start = (r * NC + 2 * p) * ONE
+            out[pl.ds(start, ONE), :] = jnp.where(low, x, roll(y, HALF))
+            out[pl.ds(start + ONE, ONE), :] = jnp.where(low, roll(x, HALF), y)
     send_ref[...] = out[...].astype(BF16)
-    copy.wait()
-
-
-def d_mixed_kernel(recv_ref, dproj_ref, w_out_ref, gain_ref, send_ref, scratch):
-    scratch[...] = recv_ref[...].astype(F32)
-    gain = column(gain_ref[...])
+    for copy in copies:
+        copy.wait()
+
+
+def d_mixed_kernel(recv_ref, dproj_ref, w_out_ref, spread_ref, send_ref, scratch):
+    scratch[...] = recv_ref[...].astype(F32)
+    gain = spread_ref[...]
     w_out = w_out_ref[...]
     for q in range(ONE):
         wt = dot(w_out, row_cells(dproj_ref, q), NT) * gain
@@ -213,7 +252,7 @@
 def update_kernel(mask_s, recv_ref, w_out_ref, gain_ref, bias_ref, dproj_ref, cot_ref,
                   normed_ref, w_ref, update_ref, d_og_ref, grads_ref, pg_h, pvg_h,
                   scratch, pg_v, pvg_v, sems):
-    weights = stacked_weights(w_ref, 1, 0)
+    weights = stacked_weights(w_ref)
     col_mask = column_mask(mask_s)
     for pair_at in range(A // 2):
         normed = normed_ref[pl.ds(pair_at * 2 * B, 2 * B), :]
@@ -241,56 +280,50 @@
             d_og_ref[rows, :] = (
                 cot_ref[rows, :].astype(F32) * proj * sig * (1.0 - sig)
             ).astype(BF16)
-    grads_ref[0] = dot(d_og_ref[...], normed_ref[...], TN)
-    grads_ref[1] = grad
+    grads_ref[0] = dot(d_og_ref[...], normed_ref[...], TN).astype(BF16)
+    grads_ref[1] = grad.astype(BF16)
     for copy in copies:
         copy.wait()
 
 
-def back_kernel(recv_ref, both_h, order_ref, send_ref, both, scratch, d_tile, first, second, out, sem):
-    copy = pltpu.make_async_copy(both_h, both, sem)
-    copy.start()
-    scratch[...] = recv_ref[...].astype(F32)
-    low = lane_of((NR, LANES)) < HALF
-    for q in range(ONE):
+def back_kernel(recv_ref, left_h, right_h, pg_h, pvg_h, send_ref, pg_ref, pvg_ref,
+                left_ref, right_ref, scratch, d_tile, d_left, d_right, out, sems):
+    copies = [
+        pltpu.make_async_copy(src, dst, sems.at[n])
+        for n, (src, dst) in enumerate(
+            [(right_h, right_ref), (left_h, left_ref), (pg_h, pg_ref), (pvg_h, pvg_ref)]
+        )
+    ]
+    for copy in copies:
+        copy.start()
+    scratch[...] = recv_ref[...].astype(F32)
+    low = lane_of((ONE, LANES)) < HALF
+    for r in range(NR):
         for p in range(NC // 2):
             lanes = slice(p * LANES, (p + 1) * LANES)
-            x = scratch[pl.ds(2 * p * ONE + q, NR, stride=SINGLE), :]
-            y = scratch[pl.ds((2 * p + 1) * ONE + q, NR, stride=SINGLE), :]
-            d_tile[q * NR : (q + 1) * NR, lanes] = jnp.where(low, x, roll(y, HALF)).astype(BF16)
-            d_tile[(q + ONE) * NR : (q + ONE + 1) * NR, lanes] = (
-                jnp.where(low, roll(x, HALF), y).astype(BF16)
-            )
-    d = dot(d_tile[...], order_ref[...], NN).astype(BF16)
-    copy.wait()
-    first[...] = dot(d, both[...], TN)
-    second[...] = dot(d, both[...], NN)
-    lane = lane_of((NR, LANES))
-    for c in range(NC):
-        lanes = slice(c * LANES, (c + 1) * LANES)
-
-        def block(a):
-            rows = slice(a * NR, (a + 1) * NR)
-            return jnp.where(lane < B, first[rows, lanes], second[rows, lanes])
-
-        third = [block(16 + s) for s in range(8)]
-        for a in range(16):
-            out[pl.ds(c * BOTH + a, NR, stride=GROUP), :] = pack_both(block(a), third[a % 8], a)
-        for n in range(2):
-            out[pl.ds(c * BOTH + 16 + n, NR, stride=GROUP), :] = pack_tail(lambda s: third[s], n)
+            start = (r * NC + 2 * p) * ONE
+            x = scratch[pl.ds(start, ONE), :]
+            y = scratch[pl.ds(start + ONE, ONE), :]
+            d_tile[pl.ds(r * A, ONE), lanes] = jnp.where(low, x, roll(y, HALF))
+            d_tile[pl.ds(r * A + ONE, ONE), lanes] = jnp.where(low, roll(x, HALF), y)
+    d = d_tile[...].astype(BF16)
+    copies[0].wait()
+    copies[1].wait()
+    d_left[...] = dot(d, right_ref[...], NN)
+    d_right[...] = dot(d, left_ref[...], TN)
+    lane = lane_of((A, LANES))
+    for r in range(NR):
+        for p in range(NC // 2):
+            lanes = slice(p * LANES, (p + 1) * LANES)
+            x = d_left[r * A : (r + 1) * A, lanes]
+            at = (r // 2) * HALF + (r % 2) * A
+            y = d_right[at : at + A, lanes]
+            start = (r * NC + 2 * p) * BOTH
+            store_both(out, start, jnp.where(lane < B, x, roll(y, B)))
+            store_both(out, start + BOTH, jnp.where(lane < B, roll(x, HALF), roll(y, B - HALF)))
     send_ref[...] = out[...].astype(BF16)
-
-
-def start_gates(pg_h, pvg_h, pg_v, pvg_v, sems):
-    copies = []
-    for pair_at in range(A // 2):
-        part = pl.ds(2 * pair_at, 2)
-        two = [pltpu.make_async_copy(src.at[part], dst.at[part], sems.at[n, pair_at])
-               for n, (src, dst) in enumerate([(pg_h, pg_v), (pvg_h, pvg_v)])]
-        for copy in two:
-            copy.start()
-        copies.append(two)
-    return copies
+    copies[2].wait()
+    copies[3].wait()
 
 
 def gated(scratch, a, pg_v, pvg_v):
@@ -299,36 +332,34 @@
     return jnp.concatenate([d * pg_v[a].astype(F32), d * pvg_v[a].astype(F32)], 0).astype(BF16)
 
 
-def grad_kernel(recv_ref, pg_h, pvg_h, normed_ref, grads_ref, send_ref,
-                scratch, packed, pg_v, pvg_v, sems):
-    copies = start_gates(pg_h, pvg_h, pg_v, pvg_v, sems)
-    scratch[...] = recv_ref[...].astype(F32)
-    packed[pl.ds(4, H, stride=SUMS), :] = grads_ref[0]
-    packed[pl.ds(5, H, stride=SUMS), :] = grads_ref[1]
+def grad_kernel(recv_ref, pg_v, pvg_v, normed_ref, grads_ref, send_ref, scratch, packed):
+    scratch[...] = recv_ref[...].astype(F32)
+    for g in range(2):
+        packed[pl.ds(4 + g, H, stride=SUMS), :] = grads_ref[g].astype(F32)
     total = jnp.zeros((2 * H, 2 * H), F32)
     for pair_at in range(A // 2):
-        for copy in copies[pair_at]:
-            copy.wait()
         a = 2 * pair_at
         sides = [gated(scratch, a + k, pg_v, pvg_v) for k in range(2)]
         cells = [two_sided(normed_ref[(a + k) * B : (a + k + 1) * B, :]) for k in range(2)]
         total = total + dot(jnp.concatenate(sides, 1), jnp.concatenate(cells, 0), NN)
-    for g, block in enumerate([total[:H, H:], total[H:, H:], total[:H, :H], total[H:, :H]]):
+    for g, block in enumerate([total[:H, :H], total[H:, :H], total[:H, H:], total[H:, H:]]):
         packed[pl.ds(g, H, stride=SUMS), :] = block
     send_ref[...] = packed[...].astype(BF16)
 
 
 def pair_grad_kernel(recv_ref, pg_h, pvg_h, d_og_ref, normal_ref, scale_ref, gain_ref, w_ref,
                      out_ref, scratch, pg_v, pvg_v, sems):
-    copies = start_gates(pg_h, pvg_h, pg_v, pvg_v, sems)
-    scratch[...] = recv_ref[...].astype(F32)
-    weights = stacked_weights(w_ref, 1, 0)
+    copies = [pltpu.make_async_copy(pg_h, pg_v, sems.at[0]),
+              pltpu.make_async_copy(pvg_h, pvg_v, sems.at[1])]
+    for copy in copies:
+        copy.start()
+    scratch[...] = recv_ref[...].astype(F32)
+    weights = stacked_weights(w_ref)
     w_og = w_ref[:, 4 * H :]
     gain = gain_ref[...]
+    for copy in copies:
+        copy.wait()
     for a in range(A):
-        if a % 2 == 0:
-            for copy in copies[a // 2]:
-                copy.wait()
         rows = pl.ds(a * B, B)
         both = dot(gated(scratch, a, pg_v, pvg_v), weights, TN)
         d = both[:B, :H] + both[B : 2 * B, H:] + dot(d_og_ref[rows, :], w_og, NT)
@@ -358,12 +389,19 @@
 
 
 def call(kernel, args, outs, scratch, flops, hbm_in=(), smem_in=(), hbm_out=()):
-    shapes = [jax.ShapeDtypeStruct(s, d) for s, d in outs]
+    shapes = [
+        pltpu.HBM(s, d) if n in hbm_out else jax.ShapeDtypeStruct(s, d)
+        for n, (s, d) in enumerate(outs)
+    ]
+    args = [
+        pltpu.with_memory_space_constraint(v, pltpu.HBM) if n in hbm_in else v
+        for n, v in enumerate(args)
+    ]
     specs = [
         HBM_SPEC if n in hbm_in else pl.BlockSpec(memory_space=pltpu.SMEM) if n in smem_in else VMEM_SPEC
         for n in range(len(args))
     ]
-    moved = sum(v.size * v.dtype.itemsize for v in list(args) + shapes)
+    moved = 2 * (sum(v.size for v in args) + sum(math.prod(s) for s, _ in outs))
     return pl.pallas_call(
         kernel,
         out_shape=shapes,
@@ -401,25 +439,25 @@
         400_000_000, hbm_in=range(5),
     )
     recv = exchange(send, 9, 2)
-    dproj, normal, scale = call(
+    dproj, normal, scale, spread = call(
         gate_kernel,
-        [normed, w_in, cot2, pair2],
-        [((CELLS, H), BF16), ((CELLS, H), F32), ((CELLS, H), F32)],
+        [normed, w_in, cot2, pair2, line(out_gain)],
+        [((CELLS, H), BF16), ((CELLS, H), F32), ((CELLS, H), F32), ((H, LANES), F32)],
         [],
         100_000_000,
     )
-    send, both, order = call(
+    send, left, right = call(
         mix_kernel,
         [recv],
-        [(one_shape, BF16), ((N, NC * LANES), BF16), ((512, N), BF16)],
-        [vm(*both_shape), vm(N, NC * LANES, dtype=BF16), vm(N, NC * LANES, dtype=BF16),
-         vm(N, 512), vm(*one_shape), dma],
-        400_000_000, hbm_out=(1,),
+        [(one_shape, BF16), ((N, 512), BF16), ((512, 512), BF16)],
+        [vm(N, 512, dtype=BF16), vm(512, 512, dtype=BF16), vm(*both_shape), vm(N, 512),
+         vm(*one_shape), dma((2,))],
+        400_000_000, hbm_out=(1, 2),
     )
     mixed = exchange(send, 3, 4)
     (send,) = call(
         d_mixed_kernel,
-        [mixed, dproj, w_out, line(out_gain)],
+        [mixed, dproj, w_out, spread],
         [(one_shape, BF16)],
         [vm(*one_shape)],
         50_000_000,
@@ -428,33 +466,33 @@
     update, d_og, grads, pg, pvg = call(
         update_kernel,
         [mask, mixed, w_out, line(out_gain), line(out_bias), dproj, cot2, normed, w_in],
-        [((CELLS, H), BF16), ((CELLS, H), BF16), ((2, H, H), F32),
+        [((CELLS, H), BF16), ((CELLS, H), BF16), ((2, H, H), BF16),
          ((A, H, LANES), BF16), ((A, H, LANES), BF16)],
         [vm(*one_shape), *gates, dma((2,))],
         600_000_000, smem_in=(0,), hbm_out=(3, 4),
     )
-    (send,) = call(
+    send, pg_near, pvg_near = call(
         back_kernel,
-        [recv, both, order],
-        [(both_shape, BF16)],
-        [vm(N, NC * LANES, dtype=BF16), vm(*one_shape), vm(N, 512, dtype=BF16),
-         vm(N, NC * LANES), vm(N, NC * LANES), vm(*both_shape), dma],
-        800_000_000, hbm_in=(1,),
+        [recv, left, right, pg, pvg],
+        [(both_shape, BF16), ((A, H, LANES), BF16), ((A, H, LANES), BF16)],
+        [vm(N, 512, dtype=BF16), vm(512, 512, dtype=BF16), vm(*one_shape), vm(N, 512),
+         vm(N, 512), vm(512, 512), vm(*both_shape), dma((4,))],
+        800_000_000, hbm_in=(1, 2, 3, 4),
     )
     recv = exchange(send, 9, 2)
     (send,) = call(
         grad_kernel,
-        [recv, pg, pvg, normed, grads],
+        [recv, pg_near, pvg_near, normed, grads],
         [(sum_shape, BF16)],
-        [vm(*both_shape), vm(*sum_shape), *gates, dma((2, A // 2))],
-        400_000_000, hbm_in=(1, 2),
+        [vm(*both_shape), vm(*sum_shape)],
+        400_000_000,
     )
     parts = exchange(send, 3, 2)
     (pair_grad,) = call(
         pair_grad_kernel,
         [recv, pg, pvg, d_og, normal, scale, line(in_gain), w_in],
         [((CELLS, H), BF16)],
-        [vm(*both_shape), *gates, dma((2, A // 2))],
+        [vm(*both_shape), *gates, dma((2,))],
         400_000_000, hbm_in=(1, 2),
     )
     (send,) = call(sum_kernel, [parts], [(sum_shape, BF16)], [], 1_000_000)

time: 127 us -> 125 us (0.984)
  local copies, waits for them, and re-layouts: 9.59 us -> 1.95 us
  waiting for transfers between devices: 16.4 us -> 21.1 us
  blocking collectives: 55.6 us -> 57.4 us
    unnamed x36 -> x20, local copies, waits for them, and re-layouts: 9.59 us -> 1.95 us
    all_to_all x3, waiting for transfers between devices: 16.4 us -> 21.1 us  [exchange(): moved = lax.all_to_all(x.reshape(ND, *tile, LANES), AXES, 0, 0, tiled=True)]
    all_to_all x3, blocking collectives: 55.6 us -> 57.4 us  [exchange(): moved = lax.all_to_all(x.reshape(ND, *tile, LANES), AXES, 0, 0, tiled=True)]
  transfers between devices with their start and end apart: 3 -> 3, of which waited for: 3 -> 3; matrix products, arithmetic and copies ran while one was open for 0% -> 0% of each run, Pallas kernels for 9% -> 7%
where the time goes in v3:
time: 125 us
  blocking collectives  57.4 us (46%)
  Pallas kernels  27.9 us (22%)
  waiting for transfers between devices  21.1 us (17%)
  starting transfers between devices  15.5 us (12%)
  local copies, waits for them, and re-layouts  1.95 us (2%)
    all_to_all x3, blocking collectives, exchange(): moved = lax.all_to_all(x.reshape(ND, *tile, LANES), AXES, 0, 0, tiled=True)  57.4 us
    pallas_call x10, Pallas kernels, call(): pl.pallas_call(kernel, out_shape=shapes, in_specs=specs, out_specs=[HBM_S...  27.9 us
    all_to_all x3, waiting for transfers between devices, exchange(): moved = lax.all_to_all(x.reshape(ND, *tile, LANES), AXES, 0, 0, tiled=True)  21.1 us
    all_to_all x3, starting transfers between devices, exchange(): moved = lax.all_to_all(x.reshape(ND, *tile, LANES), AXES, 0, 0, tiled=True)  15.5 us
  transfers between devices with their start and end apart: 3, of which 3 were waited for; matrix products, arithmetic and copies ran while one was open for 0% of the time, Pallas kernels for 7%

profile of v3, /device:TPU:1, one launch (start us, length us, event | category | flops | bytes accessed | tf_op | source)
XLA Modules:
  0.0 124.6 jit_solution(10082015881904779894)
XLA Ops:
  0.6 2.7 %shard_map.120 = (bf16[2304,128]{1,0:T(8,128)(2,1)S(1)}, bf16[1152,128]{1,0:T(8,128)(2,1)S(1)}) custom-call(s32[384]{0:T(512)} %mask_s.1, bf16[1152,128]{1,0:T(8,128)(2,1)} %bitcast.31, f32[1,128]{1,0:T(1,128)} %bitcast.37, f32[1,128]{1,0:T(1,128)} %bitcast.41, bf16[128,640]{1,0:T(8,128)(2,1)} %w_ref.5), custom_call_target="tpu_custom_call" | custom-call | flops 400000000 | bytes 1344768 | tf_op jit(solution)/shard_map/pallas_call | solution.py:405
  3.3 24.2 %all_to_all.30 = bf16[128,9,2,128]{3,2,1,0:T(2,128)(2,1)S(1)} all-to-all(bf16[128,9,2,128]{3,2,1,0:T(2,128)(2,1)S(1)} %bitcast.29), channel_id=1, replica_groups=mesh['row'=16,'col'=8] {'row','col'}, dimensions={0} | all-to-all | bytes 1179648 | tf_op jit(solution)/shard_map/all_to_all | solution.py:421
  27.5 6.0 %shard_map.121 = (bf16[1536,128]{1,0:T(8,128)(2,1)}, bf16[384,512]{1,0:T(8,128)(2,1)}, bf16[512,512]{1,0:T(8,128)(2,1)}) custom-call(bf16[2304,128]{1,0:T(8,128)(2,1)S(1)} %bitcast.28), custom_call_target="tpu_custom_call" | custom-call | flops 400000000 | bytes 1900544 | tf_op jit(solution)/shard_map/pallas_call | solution.py:405
  33.5 0.0 copy-start
  33.5 0.0 copy-start.1
  33.5 0.0 copy-start.2
  33.5 5.5 %all-to-all-start.1 = ((bf16[128,3,4,128]{3,2,1,0:T(4,128)(2,1)}), bf16[128,3,4,128]{3,2,1,0:T(4,128)(2,1)S(1)}, u32[]{:S(2)}, u32[]{:S(2)}) async-start(bf16[128,3,4,128]{3,2,1,0:T(4,128)(2,1)} %bitcast.5), calls=%async_computation.1 | async-start | bytes 786432 | tf_op jit(solution)/shard_map/all_to_all | solution.py:421
  39.1 0.0 copy-start.6
  39.1 0.6 copy-done.6
  39.7 0.5 shard_map.122
  40.2 10.0 %all-to-all-done.1 = bf16[128,3,4,128]{3,2,1,0:T(4,128)(2,1)S(1)} async-done(((bf16[128,3,4,128]{3,2,1,0:T(4,128)(2,1)}), bf16[128,3,4,128]{3,2,1,0:T(4,128)(2,1)S(1)}, u32[]{:S(2)}, u32[]{:S(2)}) %all-to-all-start.1) | async-done | bytes 393248 | tf_op jit(solution)/shard_map/all_to_all | solution.py:421
  50.2 1.4 %shard_map.124 = bf16[1536,128]{1,0:T(8,128)(2,1)} custom-call(bf16[1536,128]{1,0:T(8,128)(2,1)S(1)} %bitcast.22, bf16[1152,128]{1,0:T(8,128)(2,1)S(1)} %get-tuple-element.26.dproj_ref, bf16[128,128]{1,0:T(8,128)(2,1)S(1)} %copy-done.5, f32[128,128]{1,0:T(8,128)S(1)} %get-tuple-element.28.spread_ref), custom_call_target="tpu_custom_call" | custom-call | flops 50000000 | bytes 1146880 | tf_op jit(solution)/shard_map/pallas_call | solution.py:405
  51.7 5.3 %all-to-all-start.2 = ((bf16[128,3,4,128]{3,2,1,0:T(4,128)(2,1)}), bf16[128,3,4,128]{3,2,1,0:T(4,128)(2,1)S(1)}, u32[]{:S(2)}, u32[]{:S(2)}) async-start(bf16[128,3,4,128]{3,2,1,0:T(4,128)(2,1)} %bitcast.11), calls=%async_computation.2 | async-start | bytes 786432 | tf_op jit(solution)/shard_map/all_to_all | solution.py:421
  57.0 0.0 copy-start.9
  57.0 0.6 copy-done.9
  57.6 3.9 %shard_map.123 = (bf16[1152,128]{1,0:T(8,128)(2,1)}, bf16[1152,128]{1,0:T(8,128)(2,1)S(1)}, bf16[2,128,128]{2,1,0:T(8,128)(2,1)S(1)}, bf16[24,128,128]{2,1,0:T(8,128)(2,1)}, bf16[24,128,128]{2,1,0:T(8,128)(2,1)}) custom-call(s32[384]{0:T(512)S(1)} %copy-done.8, bf16[1536,128]{1,0:T(8,128)(2,1)S(1)} %bitcast.23, bf16[128,128]{1,0:T(8,128)(2,1)S(1)} %copy-done.5, ...), custom_call_target="tpu_custom_call" | custom-call | flops 600000000 | bytes 3704064 | tf_op jit(solution)/shard_map/pallas_call | solution.py:405
  61.5 0.0 copy-start.3
  61.5 6.7 %all-to-all-done.2 = bf16[128,3,4,128]{3,2,1,0:T(4,128)(2,1)S(1)} async-done(((bf16[128,3,4,128]{3,2,1,0:T(4,128)(2,1)}), bf16[128,3,4,128]{3,2,1,0:T(4,128)(2,1)S(1)}, u32[]{:S(2)}, u32[]{:S(2)}) %all-to-all-start.2) | async-done | bytes 393248 | tf_op jit(solution)/shard_map/all_to_all | solution.py:421
  68.2 6.4 %shard_map.125 = (bf16[2304,128]{1,0:T(8,128)(2,1)S(1)}, bf16[24,128,128]{2,1,0:T(8,128)(2,1)S(1)}, bf16[24,128,128]{2,1,0:T(8,128)(2,1)S(1)}) custom-call(bf16[1536,128]{1,0:T(8,128)(2,1)S(1)} %bitcast.30, bf16[384,512]{1,0:T(8,128)(2,1)} %get-tuple-element.29.left_h, bf16[512,512]{1,0:T(8,128)(2,1)} %get-tuple-element.30.right_h, ...), custom_call_target="tpu_custom_call" | custom-call | flops 800000000 | bytes 5046272 | tf_op jit(solution)/shard_map/pallas_call | solution.py:405
  74.6 0.0 copy-done.3
  74.7 0.0 copy-start.4
  74.7 18.0 %all_to_all.31 = bf16[128,9,2,128]{3,2,1,0:T(2,128)(2,1)S(1)} all-to-all(bf16[128,9,2,128]{3,2,1,0:T(2,128)(2,1)S(1)} %bitcast.27), channel_id=1, replica_groups=mesh['row'=16,'col'=8] {'row','col'}, dimensions={0} | all-to-all | bytes 1179648 | tf_op jit(solution)/shard_map/all_to_all | solution.py:421
  92.6 0.0 copy-done.4
  92.6 0.6 shard_map.127
  93.3 15.2 %all_to_all.32 = bf16[128,3,2,128]{3,2,1,0:T(2,128)(2,1)S(1)} all-to-all(bf16[128,3,2,128]{3,2,1,0:T(2,128)(2,1)S(1)} %bitcast.26), channel_id=1, replica_groups=mesh['row'=16,'col'=8] {'row','col'}, dimensions={0} | all-to-all | bytes 393216 | tf_op jit(solution)/shard_map/all_to_all | solution.py:421
  108.5 0.7 shard_map.128
  109.3 4.7 %all-to-all-start.5 = ((bf16[128,3,2,128]{3,2,1,0:T(2,128)(2,1)}), bf16[128,3,2,128]{3,2,1,0:T(2,128)(2,1)S(1)}, u32[]{:S(2)}, u32[]{:S(2)}) async-start(bf16[128,3,2,128]{3,2,1,0:T(2,128)(2,1)} %bitcast.18), calls=%async_computation.5 | async-start | bytes 393216 | tf_op jit(solution)/shard_map/all_to_all | solution.py:421
  113.9 0.0 copy-start.7
  113.9 0.6 copy-done.7
  114.6 4.7 %shard_map.126 = bf16[1152,128]{1,0:T(8,128)(2,1)} custom-call(bf16[2304,128]{1,0:T(8,128)(2,1)S(1)} %bitcast.21, bf16[24,128,128]{2,1,0:T(8,128)(2,1)} %get-tuple-element.31.pg_h, bf16[24,128,128]{2,1,0:T(8,128)(2,1)} %get-tuple-element.32.pvg_h, bf16[1152,128]{1,0:T(8,128)(2,1)S(1)} %get-tuple-element.34.d_og_ref, ...), custom_call_target="tpu_custom_call" | custom-call | flops 400000000 | bytes 3506432 | tf_op jit(solution)/shard_map/pallas_call | solution.py:405
  119.3 4.4 %all-to-all-done.5 = bf16[128,3,2,128]{3,2,1,0:T(2,128)(2,1)S(1)} async-done(((bf16[128,3,2,128]{3,2,1,0:T(2,128)(2,1)}), bf16[128,3,2,128]{3,2,1,0:T(2,128)(2,1)S(1)}, u32[]{:S(2)}, u32[]{:S(2)}) %all-to-all-start.5) | async-done | bytes 196640 | tf_op jit(solution)/shard_map/all_to_all | solution.py:421
  123.7 0.9 shard_map.129
  (7 shorter events, 0.0 us)
Async XLA Ops:
  33.5 5.6 %copy-start = (bf16[128,640]{1,0:T(8,128)(2,1)S(1)}, bf16[128,640]{1,0:T(8,128)(2,1)}, u32[]{:S(2)}) copy-start(bf16[128,640]{1,0:T(8,128)(2,1)} %w_ref.5) | copy-start | bytes 491524
  33.5 5.6 %copy-start.1 = (bf16[24,48,128]{2,1,0:T(8,128)(2,1)S(1)}, bf16[24,48,128]{2,1,0:T(8,128)(2,1)}, u32[]{:S(2)}) copy-start(bf16[24,48,128]{2,1,0:T(8,128)(2,1)} %param.9) | copy-start | bytes 884740
  33.5 5.6 %copy-start.2 = (bf16[24,48,128]{2,1,0:T(8,128)(2,1)S(1)}, bf16[24,48,128]{2,1,0:T(8,128)(2,1)}, u32[]{:S(2)}) copy-start(bf16[24,48,128]{2,1,0:T(8,128)(2,1)} %param.17) | copy-start | bytes 884740
  33.5 16.7 %all-to-all-start.1 = ((bf16[128,3,4,128]{3,2,1,0:T(4,128)(2,1)}), bf16[128,3,4,128]{3,2,1,0:T(4,128)(2,1)S(1)}, u32[]{:S(2)}, u32[]{:S(2)}) async-start(bf16[128,3,4,128]{3,2,1,0:T(4,128)(2,1)} %bitcast.5), calls=%async_computation.1 | async-start | bytes 786432 | tf_op jit(solution)/shard_map/all_to_all | solution.py:421
  39.1 0.7 copy-start.6
  39.7 10.5 %copy-start.5 = (bf16[128,128]{1,0:T(8,128)(2,1)S(1)}, bf16[128,128]{1,0:T(8,128)(2,1)}, u32[]{:S(2)}) copy-start(bf16[128,128]{1,0:T(8,128)(2,1)} %w_out_ref.3) | copy-start | bytes 98308
  51.7 5.3 %copy-start.8 = (s32[384]{0:T(512)S(1)}, s32[384]{0:T(512)}, u32[]{:S(2)}) copy-start(s32[384]{0:T(512)} %mask_s.1) | copy-start | bytes 4612
  51.7 16.6 %all-to-all-start.2 = ((bf16[128,3,4,128]{3,2,1,0:T(4,128)(2,1)}), bf16[128,3,4,128]{3,2,1,0:T(4,128)(2,1)S(1)}, u32[]{:S(2)}, u32[]{:S(2)}) async-start(bf16[128,3,4,128]{3,2,1,0:T(4,128)(2,1)} %bitcast.11), calls=%async_computation.2 | async-start | bytes 786432 | tf_op jit(solution)/shard_map/all_to_all | solution.py:421
  57.0 0.7 copy-start.9
  61.5 13.1 %copy-start.3 = (bf16[2,128,128]{2,1,0:T(8,128)(2,1)}, bf16[2,128,128]{2,1,0:T(8,128)(2,1)S(1)}, u32[]{:S(2)}) copy-start(bf16[2,128,128]{2,1,0:T(8,128)(2,1)S(1)} %get-tuple-element.39.grads_ref) | copy-start | bytes 196612
  74.7 18.0 %copy-start.4 = (bf16[2,128,128]{2,1,0:T(8,128)(2,1)S(1)}, bf16[2,128,128]{2,1,0:T(8,128)(2,1)}, u32[]{:S(2)}) copy-start(bf16[2,128,128]{2,1,0:T(8,128)(2,1)} %copy-done.3) | copy-start | bytes 196612
  109.3 14.5 %all-to-all-start.5 = ((bf16[128,3,2,128]{3,2,1,0:T(2,128)(2,1)}), bf16[128,3,2,128]{3,2,1,0:T(2,128)(2,1)S(1)}, u32[]{:S(2)}, u32[]{:S(2)}) async-start(bf16[128,3,2,128]{3,2,1,0:T(2,128)(2,1)} %bitcast.18), calls=%async_computation.5 | async-start | bytes 393216 | tf_op jit(solution)/shard_map/all_to_all | solution.py:421
  113.9 0.7 copy-start.7

commit v4 on v3

--- a/solution.py
+++ b/solution.py
@@ -17,7 +17,7 @@
 CELLS = A * B
 H = 128
 N = NR * A
-BOTH, ONE, SUMS = 18, 12, 6
+BOTH, ONE, SUMS = 24, 12, 6
 
 NT = ((1,), (1,))
 TN = ((0,), (0,))
@@ -39,10 +39,10 @@
 
 
 def two_sided(x):
-    none = jnp.zeros_like(x)
-    rest = jnp.zeros((LANES - 2 * B, 2 * x.shape[1]), x.dtype)
+    padded = jnp.concatenate([x, jnp.zeros((HALF - B, x.shape[1]), x.dtype)], 0)
+    none = jnp.zeros_like(padded)
     return jnp.concatenate(
-        [jnp.concatenate([x, none], 1), jnp.concatenate([none, x], 1), rest], 0
+        [jnp.concatenate([padded, none], 1), jnp.concatenate([none, padded], 1)], 0
     )
 
 
@@ -68,7 +68,7 @@
 def column_mask(mask_s):
     start = lax.axis_index("col") * B
     lane = lane_of((8, LANES))
-    place = jnp.where(lane < B, lane, lane - B)
+    place = lane & (HALF - 1)
     out = jnp.zeros((8, LANES), F32)
     for b in range(B):
         out = jnp.where(place == b, mask_s[start + b].astype(F32), out)
@@ -86,28 +86,6 @@
         yield value, gate, gate * seen
 
 
-def pack_both(block, third, a):
-    shift = LANES - 32 if a < 8 else HALF
-    return jnp.where(lane_of(block.shape) < 2 * B, block, roll(third, shift))
-
-
-def pack_tail(third, n):
-    lane = lane_of((H, LANES))
-    out = roll(third[4 * n], -HALF)
-    for m in range(1, 4):
-        out = jnp.where(lane >= 32 * m, roll(third[4 * n + m], 32 * m - HALF), out)
-    return out
-
-
-def unpack_third(block, s):
-    first, second, last = block(s), block(8 + s), block(16 + s // 4)
-    lane = lane_of(first.shape)
-    return jnp.where(
-        lane < 32, roll(first, 32),
-        jnp.where(lane < HALF, roll(second, HALF), roll(last, HALF - 32 * (s % 4))),
-    )
-
-
 def norm_rows(x):
     center = x - jnp.mean(x, 1, keepdims=True)
     scale = lax.rsqrt(jnp.mean(center * center, 1, keepdims=True) + EPS)
@@ -121,7 +99,7 @@
 
 
 def project_kernel(mask_h, pair_h, gain_h, bias_h, w_h, send_ref, normed_ref,
-                   mask_s, pair_v, gain_v, bias_v, w_v, third, scratch, sems):
+                   mask_s, pair_v, gain_v, bias_v, w_v, scratch, sems):
     copies = [
         pltpu.make_async_copy(src, dst, sems.at[n])
         for n, (src, dst) in enumerate(
@@ -135,20 +113,13 @@
     weights = stacked_weights(w_v)
     col_mask = column_mask(mask_s)
     gain, bias = gain_v[...], bias_v[...]
-    for pair_at in (8, 9, 10, 11, 0, 1, 2, 3, 4, 5, 6, 7):
+    for pair_at in range(A // 2):
         rows = pl.ds(pair_at * 2 * B, 2 * B)
         normal, _ = norm_rows(pair_v[rows, :].astype(F32))
         normed = (normal * gain + bias).astype(BF16)
         normed_ref[rows, :] = normed
         for k, (value, _, pg) in enumerate(gate_parts(weights, normed, pair_at, col_mask, mask_s)):
-            a = pair_at * 2 + k
-            if a >= 16:
-                third[a - 16] = pg * value
-            else:
-                scratch[pl.ds(a, H, stride=BOTH), :] = pack_both(pg * value, third[a % 8], a)
-        if pair_at == 11:
-            for n in range(2):
-                scratch[pl.ds(16 + n, H, stride=BOTH), :] = pack_tail(third, n)
+            scratch[pl.ds(pair_at * 2 + k, H, stride=BOTH), :] = pg * value
     send_ref[...] = scratch[...].astype(BF16)
 
 
@@ -162,58 +133,17 @@
     scale_ref[...] = jnp.broadcast_to(scale, (CELLS, H))
 
 
-def third_tile(scratch, start, first, second):
-    lane, at = lane_of((8, LANES)), lax.broadcasted_iota(jnp.int32, (8, LANES), 0)
-    tail = jnp.where(
-        at < 4,
-        jnp.broadcast_to(scratch[pl.ds(start + 16, 1), :], (8, LANES)),
-        jnp.broadcast_to(scratch[pl.ds(start + 17, 1), :], (8, LANES)),
-    )
-    last = roll(tail, HALF)
-    for m in range(1, 4):
-        last = jnp.where((at & 3) == m, roll(tail, HALF - 32 * m), last)
-    return jnp.where(lane < 32, roll(first, 32), jnp.where(lane < HALF, roll(second, HALF), last))
-
-
-def store_both(out, start, x):
-    lane, at = lane_of((8, LANES)), lax.broadcasted_iota(jnp.int32, (8, LANES), 0)
-    t0, t1, t2 = x[:8], x[8:16], x[16:]
-    out[pl.ds(start, 8), :] = jnp.where(lane < 2 * B, t0, roll(t2, LANES - 32))
-    out[pl.ds(start + 8, 8), :] = jnp.where(lane < 2 * B, t1, roll(t2, HALF))
-    tail = jnp.zeros((8, LANES), F32)
-    for m in range(4):
-        here = ((at & 3) == m) & (lane >= 32 * m) & (lane < 32 * m + 32)
-        tail = jnp.where(here, roll(t2, 32 * m - HALF), tail)
-    tail = tail + pltpu.roll(tail, 1, 0)
-    tail = tail + pltpu.roll(tail, 2, 0)
-    out[pl.ds(start + 16, 1), :] = tail[3:4]
-    out[pl.ds(start + 17, 1), :] = tail[7:8]
-
-
-def mix_kernel(recv_ref, send_ref, left_h, right_h, left_ref, right_ref, scratch, mixed, out, sems):
-    scratch[...] = recv_ref[...].astype(F32)
+def mix_kernel(recv_ref, send_ref, left_h, right_h, left_ref, right_ref, mixed, out, sems):
     right_ref[...] = jnp.zeros_like(right_ref)
-    lane = lane_of((A, LANES))
+    low = lane_of((A, LANES)) < HALF
     for r2 in range(NR // 2):
         for p in range(NC // 2):
             lefts, rights = [], []
             for r in (2 * r2, 2 * r2 + 1):
-                two = []
-                for c in (2 * p, 2 * p + 1):
-                    start = (r * NC + c) * BOTH
-                    top = scratch[pl.ds(start, 16), :]
-                    two.append(
-                        jnp.concatenate([top, third_tile(scratch, start, top[:8], top[8:])], 0)
-                    )
-                x, y = two
-                lefts.append(jnp.where(lane < HALF, x, roll(y, HALF)))
-                rights.append(
-                    jnp.where(
-                        lane < HALF,
-                        jnp.where(lane < B, roll(x, -B), 0.0),
-                        jnp.where(lane < HALF + B, roll(y, HALF - B), 0.0),
-                    )
-                )
+                both = recv_ref[pl.ds((r * NC + 2 * p) * BOTH, 2 * BOTH), :].astype(F32)
+                x, y = both[:A], both[A:]
+                lefts.append(jnp.where(low, x, roll(y, HALF)))
+                rights.append(jnp.where(low, roll(x, HALF), y))
             lanes = slice(p * LANES, (p + 1) * LANES)
             left_ref[r2 * B : (r2 + 1) * B, lanes] = jnp.concatenate(lefts, 0).astype(BF16)
             right_ref[r2 * HALF : r2 * HALF + B, lanes] = jnp.concatenate(rights, 0).astype(BF16)
@@ -287,7 +217,7 @@
 
 
 def back_kernel(recv_ref, left_h, right_h, pg_h, pvg_h, send_ref, pg_ref, pvg_ref,
-                left_ref, right_ref, scratch, d_tile, d_left, d_right, out, sems):
+                left_ref, right_ref, scratch, d_tile, d_left, d_right, sems):
     copies = [
         pltpu.make_async_copy(src, dst, sems.at[n])
         for n, (src, dst) in enumerate(
@@ -311,24 +241,23 @@
     copies[1].wait()
     d_left[...] = dot(d, right_ref[...], NN)
     d_right[...] = dot(d, left_ref[...], TN)
-    lane = lane_of((A, LANES))
+    low = lane_of((A, LANES)) < HALF
     for r in range(NR):
         for p in range(NC // 2):
             lanes = slice(p * LANES, (p + 1) * LANES)
             x = d_left[r * A : (r + 1) * A, lanes]
             at = (r // 2) * HALF + (r % 2) * A
             y = d_right[at : at + A, lanes]
-            start = (r * NC + 2 * p) * BOTH
-            store_both(out, start, jnp.where(lane < B, x, roll(y, B)))
-            store_both(out, start + BOTH, jnp.where(lane < B, roll(x, HALF), roll(y, B - HALF)))
-    send_ref[...] = out[...].astype(BF16)
+            rows = jnp.concatenate(
+                [jnp.where(low, x, roll(y, HALF)), jnp.where(low, roll(x, HALF), y)], 0
+            )
+            send_ref[pl.ds((r * NC + 2 * p) * BOTH, 2 * BOTH), :] = rows.astype(BF16)
     copies[2].wait()
     copies[3].wait()
 
 
 def gated(scratch, a, pg_v, pvg_v):
-    block = lambda p: scratch[pl.ds(p, H, stride=BOTH), :]
-    d = block(a) if a < 16 else unpack_third(block, a - 16)
+    d = scratch[pl.ds(a, H, stride=BOTH), :]
     return jnp.concatenate([d * pg_v[a].astype(F32), d * pvg_v[a].astype(F32)], 0).astype(BF16)
 
 
@@ -362,7 +291,7 @@
     for a in range(A):
         rows = pl.ds(a * B, B)
         both = dot(gated(scratch, a, pg_v, pvg_v), weights, TN)
-        d = both[:B, :H] + both[B : 2 * B, H:] + dot(d_og_ref[rows, :], w_og, NT)
+        d = both[:B, :H] + both[HALF : HALF + B, H:] + dot(d_og_ref[rows, :], w_og, NT)
         normal = normal_ref[rows, :]
         weighted = d * gain
         out_ref[rows, :] = (
@@ -435,10 +364,10 @@
         [mask, pair2, line(in_gain), line(in_bias), w_in],
         [(both_shape, BF16), ((CELLS, H), BF16)],
         [pltpu.SMEM((N,), jnp.int32), vm(CELLS, H, dtype=BF16), vm(1, H), vm(1, H),
-         vm(H, 5 * H, dtype=BF16), vm(8, H, LANES), vm(*both_shape), dma((5,))],
+         vm(H, 5 * H, dtype=BF16), vm(*both_shape), dma((5,))],
         400_000_000, hbm_in=range(5),
     )
-    recv = exchange(send, 9, 2)
+    recv = exchange(send, BOTH)
     dproj, normal, scale, spread = call(
         gate_kernel,
         [normed, w_in, cot2, pair2, line(out_gain)],
@@ -450,8 +379,8 @@
         mix_kernel,
         [recv],
         [(one_shape, BF16), ((N, 512), BF16), ((512, 512), BF16)],
-        [vm(N, 512, dtype=BF16), vm(512, 512, dtype=BF16), vm(*both_shape), vm(N, 512),
-         vm(*one_shape), dma((2,))],
+        [vm(N, 512, dtype=BF16), vm(512, 512, dtype=BF16), vm(N, 512), vm(*one_shape),
+         dma((2,))],
         400_000_000, hbm_out=(1, 2),
     )
     mixed = exchange(send, 3, 4)
@@ -476,10 +405,10 @@
         [recv, left, right, pg, pvg],
         [(both_shape, BF16), ((A, H, LANES), BF16), ((A, H, LANES), BF16)],
         [vm(N, 512, dtype=BF16), vm(512, 512, dtype=BF16), vm(*one_shape), vm(N, 512),
-         vm(N, 512), vm(512, 512), vm(*both_shape), dma((4,))],
+         vm(N, 512), vm(512, 512), dma((4,))],
         800_000_000, hbm_in=(1, 2, 3, 4),
     )
-    recv = exchange(send, 9, 2)
+    recv = exchange(send, BOTH)
     (send,) = call(
         grad_kernel,
         [recv, pg_near, pvg_near, normed, grads],

time: 125 us -> 121 us (0.968)
  Pallas kernels: 27.9 us -> 17.9 us
  blocking collectives: 57.4 us -> 61.5 us
  waiting for transfers between devices: 21.1 us -> 22.5 us
    pallas_call x10, Pallas kernels: 27.9 us -> 17.9 us  [call(): pl.pallas_call(kernel, out_shape=shapes, in_specs=specs, out_specs=[HBM_S...]
    all_to_all x3, blocking collectives: 57.4 us -> 61.5 us  [exchange(): moved = lax.all_to_all(x.reshape(ND, *tile, LANES), AXES, 0, 0, tiled=True)]
    all_to_all x3, waiting for transfers between devices: 21.1 us -> 22.5 us  [exchange(): moved = lax.all_to_all(x.reshape(ND, *tile, LANES), AXES, 0, 0, tiled=True)]
  transfers between devices with their start and end apart: 3 -> 3, of which waited for: 3 -> 3; matrix products, arithmetic and copies ran while one was open for 0% -> 0% of each run, Pallas kernels for 7% -> 6%
where the time goes in v4:
time: 121 us; the launch traced here: 120 us
  blocking collectives  61.5 us (51%)
  waiting for transfers between devices  22.5 us (19%)
  Pallas kernels  17.9 us (15%)
  starting transfers between devices  15.5 us (13%)
  local copies, waits for them, and re-layouts  1.94 us (2%)
    all_to_all x3, blocking collectives, exchange(): moved = lax.all_to_all(x.reshape(ND, *tile, LANES), AXES, 0, 0, tiled=True)  61.5 us
    all_to_all x3, waiting for transfers between devices, exchange(): moved = lax.all_to_all(x.reshape(ND, *tile, LANES), AXES, 0, 0, tiled=True)  22.5 us
    pallas_call x10, Pallas kernels, call(): pl.pallas_call(kernel, out_shape=shapes, in_specs=specs, out_specs=[HBM_S...  17.9 us
    all_to_all x3, starting transfers between devices, exchange(): moved = lax.all_to_all(x.reshape(ND, *tile, LANES), AXES, 0, 0, tiled=True)  15.5 us
  transfers between devices with their start and end apart: 3, of which 3 were waited for; matrix products, arithmetic and copies ran while one was open for 0% of the time, Pallas kernels for 6%

profile of v4, /device:TPU:1, one launch (start us, length us, event | category | flops | bytes accessed | tf_op | source)
XLA Modules:
  0.0 120.2 jit_solution(16096119485292797638)
XLA Ops:
  0.6 2.3 %shard_map.120 = (bf16[3072,128]{1,0:T(8,128)(2,1)S(1)}, bf16[1152,128]{1,0:T(8,128)(2,1)S(1)}) custom-call(s32[384]{0:T(512)} %mask_s.1, bf16[1152,128]{1,0:T(8,128)(2,1)} %bitcast.31, f32[1,128]{1,0:T(1,128)} %bitcast.37, f32[1,128]{1,0:T(1,128)} %bitcast.41, bf16[128,640]{1,0:T(8,128)(2,1)} %w_ref.5), custom_call_target="tpu_custom_call" | custom-call | flops 400000000 | bytes 1541376 | tf_op jit(solution)/shard_map/pallas_call | solution.py:334
  2.9 26.2 %all_to_all.30 = bf16[128,24,128]{2,1,0:T(8,128)(2,1)S(1)} all-to-all(bf16[128,24,128]{2,1,0:T(8,128)(2,1)S(1)} %bitcast.27), channel_id=1, replica_groups=mesh['row'=16,'col'=8] {'row','col'}, dimensions={0} | all-to-all | bytes 1572864 | tf_op jit(solution)/shard_map/all_to_all | solution.py:350
  29.2 2.1 %shard_map.121 = (bf16[1536,128]{1,0:T(8,128)(2,1)}, bf16[384,512]{1,0:T(8,128)(2,1)}, bf16[512,512]{1,0:T(8,128)(2,1)}) custom-call(bf16[3072,128]{1,0:T(8,128)(2,1)S(1)} %bitcast.26), custom_call_target="tpu_custom_call" | custom-call | flops 400000000 | bytes 2097152 | tf_op jit(solution)/shard_map/pallas_call | solution.py:334
  31.2 0.0 copy-start
  31.3 0.0 copy-start.1
  31.3 0.0 copy-start.2
  31.3 5.6 %all-to-all-start.1 = ((bf16[128,3,4,128]{3,2,1,0:T(4,128)(2,1)}), bf16[128,3,4,128]{3,2,1,0:T(4,128)(2,1)S(1)}, u32[]{:S(2)}, u32[]{:S(2)}) async-start(bf16[128,3,4,128]{3,2,1,0:T(4,128)(2,1)} %bitcast.5), calls=%async_computation.1 | async-start | bytes 786432 | tf_op jit(solution)/shard_map/all_to_all | solution.py:350
  36.9 0.0 copy-start.4
  36.9 0.0 copy-done
  36.9 0.0 copy-done.1
  36.9 0.0 copy-done.2
  36.9 0.6 copy-done.4
  37.5 0.5 shard_map.122
  38.0 10.0 %all-to-all-done.1 = bf16[128,3,4,128]{3,2,1,0:T(4,128)(2,1)S(1)} async-done(((bf16[128,3,4,128]{3,2,1,0:T(4,128)(2,1)}), bf16[128,3,4,128]{3,2,1,0:T(4,128)(2,1)S(1)}, u32[]{:S(2)}, u32[]{:S(2)}) %all-to-all-start.1) | async-done | bytes 393248 | tf_op jit(solution)/shard_map/all_to_all | solution.py:350
  48.0 0.0 copy-done.3
  48.0 1.4 %shard_map.124 = bf16[1536,128]{1,0:T(8,128)(2,1)} custom-call(bf16[1536,128]{1,0:T(8,128)(2,1)S(1)} %bitcast.22, bf16[1152,128]{1,0:T(8,128)(2,1)S(1)} %get-tuple-element.26.dproj_ref, bf16[128,128]{1,0:T(8,128)(2,1)S(1)} %copy-done.3, f32[128,128]{1,0:T(8,128)S(1)} %get-tuple-element.28.spread_ref), custom_call_target="tpu_custom_call" | custom-call | flops 50000000 | bytes 1146880 | tf_op jit(solution)/shard_map/pallas_call | solution.py:334
  49.4 5.3 %all-to-all-start.2 = ((bf16[128,3,4,128]{3,2,1,0:T(4,128)(2,1)}), bf16[128,3,4,128]{3,2,1,0:T(4,128)(2,1)S(1)}, u32[]{:S(2)}, u32[]{:S(2)}) async-start(bf16[128,3,4,128]{3,2,1,0:T(4,128)(2,1)} %bitcast.11), calls=%async_computation.2 | async-start | bytes 786432 | tf_op jit(solution)/shard_map/all_to_all | solution.py:350
  54.7 0.0 copy-start.7
  54.8 0.6 copy-done.7
  55.4 3.9 %shard_map.123 = (bf16[1152,128]{1,0:T(8,128)(2,1)}, bf16[1152,128]{1,0:T(8,128)(2,1)S(1)}, bf16[2,128,128]{2,1,0:T(8,128)(2,1)S(1)}, bf16[24,128,128]{2,1,0:T(8,128)(2,1)}, bf16[24,128,128]{2,1,0:T(8,128)(2,1)}) custom-call(s32[384]{0:T(512)S(1)} %copy-done.6, bf16[1536,128]{1,0:T(8,128)(2,1)S(1)} %bitcast.23, bf16[128,128]{1,0:T(8,128)(2,1)S(1)} %copy-done.3, ...), custom_call_target="tpu_custom_call" | custom-call | flops 600000000 | bytes 3704064 | tf_op jit(solution)/shard_map/pallas_call | solution.py:334
  59.3 6.7 %all-to-all-done.2 = bf16[128,3,4,128]{3,2,1,0:T(4,128)(2,1)S(1)} async-done(((bf16[128,3,4,128]{3,2,1,0:T(4,128)(2,1)}), bf16[128,3,4,128]{3,2,1,0:T(4,128)(2,1)S(1)}, u32[]{:S(2)}, u32[]{:S(2)}) %all-to-all-start.2) | async-done | bytes 393248 | tf_op jit(solution)/shard_map/all_to_all | solution.py:350
  66.0 2.0 %shard_map.125 = (bf16[3072,128]{1,0:T(8,128)(2,1)S(1)}, bf16[24,128,128]{2,1,0:T(8,128)(2,1)S(1)}, bf16[24,128,128]{2,1,0:T(8,128)(2,1)S(1)}) custom-call(bf16[1536,128]{1,0:T(8,128)(2,1)S(1)} %bitcast.30, bf16[384,512]{1,0:T(8,128)(2,1)} %get-tuple-element.29.left_h, bf16[512,512]{1,0:T(8,128)(2,1)} %get-tuple-element.30.right_h, ...), custom_call_target="tpu_custom_call" | custom-call | flops 800000000 | bytes 5242880 | tf_op jit(solution)/shard_map/pallas_call | solution.py:334
  68.0 20.0 %all_to_all.31 = bf16[128,24,128]{2,1,0:T(8,128)(2,1)S(1)} all-to-all(bf16[128,24,128]{2,1,0:T(8,128)(2,1)S(1)} %bitcast.25), channel_id=1, replica_groups=mesh['row'=16,'col'=8] {'row','col'}, dimensions={0} | all-to-all | bytes 1572864 | tf_op jit(solution)/shard_map/all_to_all | solution.py:350
  88.0 0.8 shard_map.127
  88.9 15.3 %all_to_all.32 = bf16[128,3,2,128]{3,2,1,0:T(2,128)(2,1)S(1)} all-to-all(bf16[128,3,2,128]{3,2,1,0:T(2,128)(2,1)S(1)} %bitcast.24), channel_id=1, replica_groups=mesh['row'=16,'col'=8] {'row','col'}, dimensions={0} | all-to-all | bytes 393216 | tf_op jit(solution)/shard_map/all_to_all | solution.py:350
  104.1 0.7 shard_map.128
  104.8 4.7 %all-to-all-start.5 = ((bf16[128,3,2,128]{3,2,1,0:T(2,128)(2,1)}), bf16[128,3,2,128]{3,2,1,0:T(2,128)(2,1)S(1)}, u32[]{:S(2)}, u32[]{:S(2)}) async-start(bf16[128,3,2,128]{3,2,1,0:T(2,128)(2,1)} %bitcast.18), calls=%async_computation.5 | async-start | bytes 393216 | tf_op jit(solution)/shard_map/all_to_all | solution.py:350
  109.5 0.0 copy-start.5
  109.5 0.6 copy-done.5
  110.2 3.4 %shard_map.126 = bf16[1152,128]{1,0:T(8,128)(2,1)} custom-call(bf16[3072,128]{1,0:T(8,128)(2,1)S(1)} %bitcast.21, bf16[24,128,128]{2,1,0:T(8,128)(2,1)} %get-tuple-element.31.pg_h, bf16[24,128,128]{2,1,0:T(8,128)(2,1)} %get-tuple-element.32.pvg_h, bf16[1152,128]{1,0:T(8,128)(2,1)S(1)} %get-tuple-element.34.d_og_ref, ...), custom_call_target="tpu_custom_call" | custom-call | flops 400000000 | bytes 3703040 | tf_op jit(solution)/shard_map/pallas_call | solution.py:334
  113.5 5.8 %all-to-all-done.5 = bf16[128,3,2,128]{3,2,1,0:T(2,128)(2,1)S(1)} async-done(((bf16[128,3,2,128]{3,2,1,0:T(2,128)(2,1)}), bf16[128,3,2,128]{3,2,1,0:T(2,128)(2,1)S(1)}, u32[]{:S(2)}, u32[]{:S(2)}) %all-to-all-start.5) | async-done | bytes 196640 | tf_op jit(solution)/shard_map/all_to_all | solution.py:350
  119.3 0.9 shard_map.129
  (3 shorter events, 0.0 us)
Async XLA Ops:
  31.2 5.6 %copy-start = (bf16[128,640]{1,0:T(8,128)(2,1)S(1)}, bf16[128,640]{1,0:T(8,128)(2,1)}, u32[]{:S(2)}) copy-start(bf16[128,640]{1,0:T(8,128)(2,1)} %w_ref.5) | copy-start | bytes 491524
  31.3 5.6 %copy-start.1 = (bf16[24,48,128]{2,1,0:T(8,128)(2,1)S(1)}, bf16[24,48,128]{2,1,0:T(8,128)(2,1)}, u32[]{:S(2)}) copy-start(bf16[24,48,128]{2,1,0:T(8,128)(2,1)} %param.9) | copy-start | bytes 884740
  31.3 5.6 %copy-start.2 = (bf16[24,48,128]{2,1,0:T(8,128)(2,1)S(1)}, bf16[24,48,128]{2,1,0:T(8,128)(2,1)}, u32[]{:S(2)}) copy-start(bf16[24,48,128]{2,1,0:T(8,128)(2,1)} %param.17) | copy-start | bytes 884740
  31.3 16.7 %all-to-all-start.1 = ((bf16[128,3,4,128]{3,2,1,0:T(4,128)(2,1)}), bf16[128,3,4,128]{3,2,1,0:T(4,128)(2,1)S(1)}, u32[]{:S(2)}, u32[]{:S(2)}) async-start(bf16[128,3,4,128]{3,2,1,0:T(4,128)(2,1)} %bitcast.5), calls=%async_computation.1 | async-start | bytes 786432 | tf_op jit(solution)/shard_map/all_to_all | solution.py:350
  36.9 0.7 copy-start.4
  37.5 10.5 %copy-start.3 = (bf16[128,128]{1,0:T(8,128)(2,1)S(1)}, bf16[128,128]{1,0:T(8,128)(2,1)}, u32[]{:S(2)}) copy-start(bf16[128,128]{1,0:T(8,128)(2,1)} %w_out_ref.3) | copy-start | bytes 98308
  49.4 5.3 %copy-start.6 = (s32[384]{0:T(512)S(1)}, s32[384]{0:T(512)}, u32[]{:S(2)}) copy-start(s32[384]{0:T(512)} %mask_s.1) | copy-start | bytes 4612
  49.4 16.6 %all-to-all-start.2 = ((bf16[128,3,4,128]{3,2,1,0:T(4,128)(2,1)}), bf16[128,3,4,128]{3,2,1,0:T(4,128)(2,1)S(1)}, u32[]{:S(2)}, u32[]{:S(2)}) async-start(bf16[128,3,4,128]{3,2,1,0:T(4,128)(2,1)} %bitcast.11), calls=%async_computation.2 | async-start | bytes 786432 | tf_op jit(solution)/shard_map/all_to_all | solution.py:350
  54.7 0.7 copy-start.7
  104.8 14.5 %all-to-all-start.5 = ((bf16[128,3,2,128]{3,2,1,0:T(2,128)(2,1)}), bf16[128,3,2,128]{3,2,1,0:T(2,128)(2,1)S(1)}, u32[]{:S(2)}, u32[]{:S(2)}) async-start(bf16[128,3,2,128]{3,2,1,0:T(2,128)(2,1)} %bitcast.18), calls=%async_computation.5 | async-start | bytes 393216 | tf_op jit(solution)/shard_map/all_to_all | solution.py:350
  109.5 0.7 copy-start.5

commit v5 on v3

--- a/solution.py
+++ b/solution.py
@@ -162,58 +162,48 @@
     scale_ref[...] = jnp.broadcast_to(scale, (CELLS, H))
 
 
-def third_tile(scratch, start, first, second):
-    lane, at = lane_of((8, LANES)), lax.broadcasted_iota(jnp.int32, (8, LANES), 0)
-    tail = jnp.where(
-        at < 4,
-        jnp.broadcast_to(scratch[pl.ds(start + 16, 1), :], (8, LANES)),
-        jnp.broadcast_to(scratch[pl.ds(start + 17, 1), :], (8, LANES)),
-    )
-    last = roll(tail, HALF)
+def pick(lane, *parts):
+    out = parts[-1]
+    for n in range(len(parts) - 3, -1, -2):
+        out = jnp.where(lane < parts[n + 1], parts[n], out)
+    return out
+
+
+def by_row(x, shift, step):
+    at = lax.broadcasted_iota(jnp.int32, (8, LANES), 0) & 3
+    out = roll(x, shift)
     for m in range(1, 4):
-        last = jnp.where((at & 3) == m, roll(tail, HALF - 32 * m), last)
-    return jnp.where(lane < 32, roll(first, 32), jnp.where(lane < HALF, roll(second, HALF), last))
-
-
-def store_both(out, start, x):
-    lane, at = lane_of((8, LANES)), lax.broadcasted_iota(jnp.int32, (8, LANES), 0)
-    t0, t1, t2 = x[:8], x[8:16], x[16:]
-    out[pl.ds(start, 8), :] = jnp.where(lane < 2 * B, t0, roll(t2, LANES - 32))
-    out[pl.ds(start + 8, 8), :] = jnp.where(lane < 2 * B, t1, roll(t2, HALF))
-    tail = jnp.zeros((8, LANES), F32)
-    for m in range(4):
-        here = ((at & 3) == m) & (lane >= 32 * m) & (lane < 32 * m + 32)
-        tail = jnp.where(here, roll(t2, 32 * m - HALF), tail)
-    tail = tail + pltpu.roll(tail, 1, 0)
-    tail = tail + pltpu.roll(tail, 2, 0)
-    out[pl.ds(start + 16, 1), :] = tail[3:4]
-    out[pl.ds(start + 17, 1), :] = tail[7:8]
+        out = jnp.where(at == m, roll(x, shift + step * m), out)
+    return out
+
+
+def two_rows(scratch, start):
+    first, second = (
+        jnp.broadcast_to(scratch[pl.ds(start + n, 1), :], (8, LANES)) for n in range(2)
+    )
+    return jnp.where(lax.broadcasted_iota(jnp.int32, (8, LANES), 0) < 4, first, second)
 
 
 def mix_kernel(recv_ref, send_ref, left_h, right_h, left_ref, right_ref, scratch, mixed, out, sems):
     scratch[...] = recv_ref[...].astype(F32)
     right_ref[...] = jnp.zeros_like(right_ref)
-    lane = lane_of((A, LANES))
+    lane, wide = lane_of((8, LANES)), lane_of((16, LANES))
     for r2 in range(NR // 2):
         for p in range(NC // 2):
             lefts, rights = [], []
             for r in (2 * r2, 2 * r2 + 1):
-                two = []
-                for c in (2 * p, 2 * p + 1):
-                    start = (r * NC + c) * BOTH
-                    top = scratch[pl.ds(start, 16), :]
-                    two.append(
-                        jnp.concatenate([top, third_tile(scratch, start, top[:8], top[8:])], 0)
-                    )
-                x, y = two
-                lefts.append(jnp.where(lane < HALF, x, roll(y, HALF)))
-                rights.append(
-                    jnp.where(
-                        lane < HALF,
-                        jnp.where(lane < B, roll(x, -B), 0.0),
-                        jnp.where(lane < HALF + B, roll(y, HALF - B), 0.0),
-                    )
-                )
+                start = (r * NC + 2 * p) * BOTH
+                x, y = scratch[pl.ds(start, 16), :], scratch[pl.ds(start + BOTH, 16), :]
+                x_tail, y_tail = two_rows(scratch, start + 16), two_rows(scratch, start + BOTH + 16)
+                lefts += [
+                    jnp.where(wide < HALF, x, roll(y, HALF)),
+                    pick(lane, roll(x[:8], 32), 32, roll(x[8:], HALF), HALF, roll(y[:8], 96), 96, y[8:]),
+                ]
+                rights += [
+                    pick(wide, roll(x, -B), B, 0.0, HALF, roll(y, HALF - B), HALF + B, 0.0),
+                    pick(lane, roll(x[8:], 16), 16, by_row(x_tail, 16, -32), B, 0.0, HALF,
+                         roll(y[8:], 80), 80, by_row(y_tail, 80, -32), HALF + B, 0.0),
+                ]
             lanes = slice(p * LANES, (p + 1) * LANES)
             left_ref[r2 * B : (r2 + 1) * B, lanes] = jnp.concatenate(lefts, 0).astype(BF16)
             right_ref[r2 * HALF : r2 * HALF + B, lanes] = jnp.concatenate(rights, 0).astype(BF16)
@@ -287,7 +277,7 @@
 
 
 def back_kernel(recv_ref, left_h, right_h, pg_h, pvg_h, send_ref, pg_ref, pvg_ref,
-                left_ref, right_ref, scratch, d_tile, d_left, d_right, out, sems):
+                left_ref, right_ref, scratch, d_tile, d_left, d_right, out, tails, sems):
     copies = [
         pltpu.make_async_copy(src, dst, sems.at[n])
         for n, (src, dst) in enumerate(
@@ -311,16 +301,31 @@
     copies[1].wait()
     d_left[...] = dot(d, right_ref[...], NN)
     d_right[...] = dot(d, left_ref[...], TN)
-    lane = lane_of((A, LANES))
+    lane = lane_of((8, LANES))
+    mine = (lane >> 5) == (lax.broadcasted_iota(jnp.int32, (8, LANES), 0) & 3)
     for r in range(NR):
         for p in range(NC // 2):
             lanes = slice(p * LANES, (p + 1) * LANES)
-            x = d_left[r * A : (r + 1) * A, lanes]
             at = (r // 2) * HALF + (r % 2) * A
-            y = d_right[at : at + A, lanes]
-            start = (r * NC + 2 * p) * BOTH
-            store_both(out, start, jnp.where(lane < B, x, roll(y, B)))
-            store_both(out, start + BOTH, jnp.where(lane < B, roll(x, HALF), roll(y, B - HALF)))
+            x0, x1, x2 = (d_left[r * A + 8 * t : r * A + 8 * t + 8, lanes] for t in range(3))
+            y0, y1, y2 = (d_right[at + 8 * t : at + 8 * t + 8, lanes] for t in range(3))
+            first = (r * NC + 2 * p) * BOTH
+            second = first + BOTH
+            out[pl.ds(first, 8), :] = pick(lane, x0, B, roll(y0, B), 2 * B, roll(x2, 96))
+            out[pl.ds(first + 8, 8), :] = pick(
+                lane, x1, B, roll(y1, B), 2 * B, roll(x2, HALF), 112, roll(y2, 112)
+            )
+            out[pl.ds(second, 8), :] = pick(lane, roll(x0, HALF), B, roll(y0, -16), 2 * B, roll(x2, 32))
+            out[pl.ds(second + 8, 8), :] = pick(
+                lane, roll(x1, HALF), B, roll(y1, -16), 2 * B, x2, 112, roll(y2, B)
+            )
+            for start, shift in ((first, -16), (second, -80)):
+                row = start // BOTH * 8
+                tails[row : row + 8, :] = jnp.where(mine, by_row(y2, shift, 32), 0.0)
+    quarters = [tails[pl.ds(n, 2 * ND, stride=4), :] for n in range(4)]
+    tails[: 2 * ND, :] = quarters[0] + quarters[1] + quarters[2] + quarters[3]
+    for n in range(2):
+        out[pl.ds(16 + n, ND, stride=BOTH), :] = tails[pl.ds(n, ND, stride=2), :]
     send_ref[...] = out[...].astype(BF16)
     copies[2].wait()
     copies[3].wait()
@@ -476,7 +481,8 @@
         [recv, left, right, pg, pvg],
         [(both_shape, BF16), ((A, H, LANES), BF16), ((A, H, LANES), BF16)],
         [vm(N, 512, dtype=BF16), vm(512, 512, dtype=BF16), vm(*one_shape), vm(N, 512),
-         vm(N, 512), vm(512, 512), vm(*both_shape), dma((4,))],
+         vm(N, 512), vm(512, 512), vm(*both_shape), vm(8 * ND, LANES),
+         dma((4,))],
         800_000_000, hbm_in=(1, 2, 3, 4),
     )
     recv = exchange(send, 9, 2)

time: 125 us -> 118 us (0.944)
  Pallas kernels: 27.9 us -> 20.6 us
    pallas_call x10, Pallas kernels: 27.9 us -> 20.6 us  [call(): pl.pallas_call(kernel, out_shape=shapes, in_specs=specs, out_specs=[HBM_S...]
  transfers between devices with their start and end apart: 3 -> 3, of which waited for: 3 -> 3; matrix products, arithmetic and copies ran while one was open for 0% -> 0% of each run, Pallas kernels for 7% -> 8%
where the time goes in v5:
time: 118 us; the launch traced here: 117 us
  blocking collectives  57.4 us (49%)
  waiting for transfers between devices  21.1 us (18%)
  Pallas kernels  20.6 us (17%)
  starting transfers between devices  15.5 us (13%)
  local copies, waits for them, and re-layouts  1.95 us (2%)
    all_to_all x3, blocking collectives, exchange(): moved = lax.all_to_all(x.reshape(ND, *tile, LANES), AXES, 0, 0, tiled=True)  57.4 us
    all_to_all x3, waiting for transfers between devices, exchange(): moved = lax.all_to_all(x.reshape(ND, *tile, LANES), AXES, 0, 0, tiled=True)  21.1 us
    pallas_call x10, Pallas kernels, call(): pl.pallas_call(kernel, out_shape=shapes, in_specs=specs, out_specs=[HBM_S...  20.6 us
    all_to_all x3, starting transfers between devices, exchange(): moved = lax.all_to_all(x.reshape(ND, *tile, LANES), AXES, 0, 0, tiled=True)  15.5 us
  transfers between devices with their start and end apart: 3, of which 3 were waited for; matrix products, arithmetic and copies ran while one was open for 0% of the time, Pallas kernels for 8%

profile of v5, /device:TPU:1, one launch (start us, length us, event | category | flops | bytes accessed | tf_op | source)
XLA Modules:
  0.0 117.4 jit_solution(1265326513613574231)
XLA Ops:
  0.6 2.7 %shard_map.120 = (bf16[2304,128]{1,0:T(8,128)(2,1)S(1)}, bf16[1152,128]{1,0:T(8,128)(2,1)S(1)}) custom-call(s32[384]{0:T(512)} %mask_s.1, bf16[1152,128]{1,0:T(8,128)(2,1)} %bitcast.31, f32[1,128]{1,0:T(1,128)} %bitcast.37, f32[1,128]{1,0:T(1,128)} %bitcast.41, bf16[128,640]{1,0:T(8,128)(2,1)} %w_ref.5), custom_call_target="tpu_custom_call" | custom-call | flops 400000000 | bytes 1344768 | tf_op jit(solution)/shard_map/pallas_call | solution.py:410
  3.3 24.2 %all_to_all.30 = bf16[128,9,2,128]{3,2,1,0:T(2,128)(2,1)S(1)} all-to-all(bf16[128,9,2,128]{3,2,1,0:T(2,128)(2,1)S(1)} %bitcast.29), channel_id=1, replica_groups=mesh['row'=16,'col'=8] {'row','col'}, dimensions={0} | all-to-all | bytes 1179648 | tf_op jit(solution)/shard_map/all_to_all | solution.py:426
  27.5 2.5 %shard_map.121 = (bf16[1536,128]{1,0:T(8,128)(2,1)}, bf16[384,512]{1,0:T(8,128)(2,1)}, bf16[512,512]{1,0:T(8,128)(2,1)}) custom-call(bf16[2304,128]{1,0:T(8,128)(2,1)S(1)} %bitcast.28), custom_call_target="tpu_custom_call" | custom-call | flops 400000000 | bytes 1900544 | tf_op jit(solution)/shard_map/pallas_call | solution.py:410
  30.0 0.0 copy-start
  30.0 0.0 copy-start.1
  30.1 0.0 copy-start.2
  30.1 5.5 %all-to-all-start.1 = ((bf16[128,3,4,128]{3,2,1,0:T(4,128)(2,1)}), bf16[128,3,4,128]{3,2,1,0:T(4,128)(2,1)S(1)}, u32[]{:S(2)}, u32[]{:S(2)}) async-start(bf16[128,3,4,128]{3,2,1,0:T(4,128)(2,1)} %bitcast.5), calls=%async_computation.1 | async-start | bytes 786432 | tf_op jit(solution)/shard_map/all_to_all | solution.py:426
  35.6 0.0 copy-start.6
  35.6 0.0 copy-done
  35.6 0.0 copy-done.1
  35.7 0.6 copy-done.6
  36.3 0.5 shard_map.122
  36.8 10.0 %all-to-all-done.1 = bf16[128,3,4,128]{3,2,1,0:T(4,128)(2,1)S(1)} async-done(((bf16[128,3,4,128]{3,2,1,0:T(4,128)(2,1)}), bf16[128,3,4,128]{3,2,1,0:T(4,128)(2,1)S(1)}, u32[]{:S(2)}, u32[]{:S(2)}) %all-to-all-start.1) | async-done | bytes 393248 | tf_op jit(solution)/shard_map/all_to_all | solution.py:426
  46.8 1.4 %shard_map.124 = bf16[1536,128]{1,0:T(8,128)(2,1)} custom-call(bf16[1536,128]{1,0:T(8,128)(2,1)S(1)} %bitcast.22, bf16[1152,128]{1,0:T(8,128)(2,1)S(1)} %get-tuple-element.26.dproj_ref, bf16[128,128]{1,0:T(8,128)(2,1)S(1)} %copy-done.5, f32[128,128]{1,0:T(8,128)S(1)} %get-tuple-element.28.spread_ref), custom_call_target="tpu_custom_call" | custom-call | flops 50000000 | bytes 1146880 | tf_op jit(solution)/shard_map/pallas_call | solution.py:410
  48.2 5.3 %all-to-all-start.2 = ((bf16[128,3,4,128]{3,2,1,0:T(4,128)(2,1)}), bf16[128,3,4,128]{3,2,1,0:T(4,128)(2,1)S(1)}, u32[]{:S(2)}, u32[]{:S(2)}) async-start(bf16[128,3,4,128]{3,2,1,0:T(4,128)(2,1)} %bitcast.11), calls=%async_computation.2 | async-start | bytes 786432 | tf_op jit(solution)/shard_map/all_to_all | solution.py:426
  53.5 0.0 copy-start.9
  53.5 0.6 copy-done.9
  54.1 3.9 %shard_map.123 = (bf16[1152,128]{1,0:T(8,128)(2,1)}, bf16[1152,128]{1,0:T(8,128)(2,1)S(1)}, bf16[2,128,128]{2,1,0:T(8,128)(2,1)S(1)}, bf16[24,128,128]{2,1,0:T(8,128)(2,1)}, bf16[24,128,128]{2,1,0:T(8,128)(2,1)}) custom-call(s32[384]{0:T(512)S(1)} %copy-done.8, bf16[1536,128]{1,0:T(8,128)(2,1)S(1)} %bitcast.23, bf16[128,128]{1,0:T(8,128)(2,1)S(1)} %copy-done.5, ...), custom_call_target="tpu_custom_call" | custom-call | flops 600000000 | bytes 3704064 | tf_op jit(solution)/shard_map/pallas_call | solution.py:410
  58.0 0.0 copy-start.3
  58.0 6.7 %all-to-all-done.2 = bf16[128,3,4,128]{3,2,1,0:T(4,128)(2,1)S(1)} async-done(((bf16[128,3,4,128]{3,2,1,0:T(4,128)(2,1)}), bf16[128,3,4,128]{3,2,1,0:T(4,128)(2,1)S(1)}, u32[]{:S(2)}, u32[]{:S(2)}) %all-to-all-start.2) | async-done | bytes 393248 | tf_op jit(solution)/shard_map/all_to_all | solution.py:426
  64.8 2.6 %shard_map.125 = (bf16[2304,128]{1,0:T(8,128)(2,1)S(1)}, bf16[24,128,128]{2,1,0:T(8,128)(2,1)S(1)}, bf16[24,128,128]{2,1,0:T(8,128)(2,1)S(1)}) custom-call(bf16[1536,128]{1,0:T(8,128)(2,1)S(1)} %bitcast.30, bf16[384,512]{1,0:T(8,128)(2,1)} %get-tuple-element.29.left_h, bf16[512,512]{1,0:T(8,128)(2,1)} %get-tuple-element.30.right_h, ...), custom_call_target="tpu_custom_call" | custom-call | flops 800000000 | bytes 5046272 | tf_op jit(solution)/shard_map/pallas_call | solution.py:410
  67.4 0.0 copy-start.4
  67.4 18.0 %all_to_all.31 = bf16[128,9,2,128]{3,2,1,0:T(2,128)(2,1)S(1)} all-to-all(bf16[128,9,2,128]{3,2,1,0:T(2,128)(2,1)S(1)} %bitcast.27), channel_id=1, replica_groups=mesh['row'=16,'col'=8] {'row','col'}, dimensions={0} | all-to-all | bytes 1179648 | tf_op jit(solution)/shard_map/all_to_all | solution.py:426
  85.4 0.6 shard_map.127
  86.1 15.2 %all_to_all.32 = bf16[128,3,2,128]{3,2,1,0:T(2,128)(2,1)S(1)} all-to-all(bf16[128,3,2,128]{3,2,1,0:T(2,128)(2,1)S(1)} %bitcast.26), channel_id=1, replica_groups=mesh['row'=16,'col'=8] {'row','col'}, dimensions={0} | all-to-all | bytes 393216 | tf_op jit(solution)/shard_map/all_to_all | solution.py:426
  101.3 0.7 shard_map.128
  102.0 4.7 %all-to-all-start.5 = ((bf16[128,3,2,128]{3,2,1,0:T(2,128)(2,1)}), bf16[128,3,2,128]{3,2,1,0:T(2,128)(2,1)S(1)}, u32[]{:S(2)}, u32[]{:S(2)}) async-start(bf16[128,3,2,128]{3,2,1,0:T(2,128)(2,1)} %bitcast.18), calls=%async_computation.5 | async-start | bytes 393216 | tf_op jit(solution)/shard_map/all_to_all | solution.py:426
  106.7 0.0 copy-start.7
  106.7 0.6 copy-done.7
  107.4 4.7 %shard_map.126 = bf16[1152,128]{1,0:T(8,128)(2,1)} custom-call(bf16[2304,128]{1,0:T(8,128)(2,1)S(1)} %bitcast.21, bf16[24,128,128]{2,1,0:T(8,128)(2,1)} %get-tuple-element.31.pg_h, bf16[24,128,128]{2,1,0:T(8,128)(2,1)} %get-tuple-element.32.pvg_h, bf16[1152,128]{1,0:T(8,128)(2,1)S(1)} %get-tuple-element.34.d_og_ref, ...), custom_call_target="tpu_custom_call" | custom-call | flops 400000000 | bytes 3506432 | tf_op jit(solution)/shard_map/pallas_call | solution.py:410
  112.1 4.4 %all-to-all-done.5 = bf16[128,3,2,128]{3,2,1,0:T(2,128)(2,1)S(1)} async-done(((bf16[128,3,2,128]{3,2,1,0:T(2,128)(2,1)}), bf16[128,3,2,128]{3,2,1,0:T(2,128)(2,1)S(1)}, u32[]{:S(2)}, u32[]{:S(2)}) %all-to-all-start.5) | async-done | bytes 196640 | tf_op jit(solution)/shard_map/all_to_all | solution.py:426
  116.5 0.9 shard_map.129
  (7 shorter events, 0.0 us)
Async XLA Ops:
  30.0 5.6 %copy-start = (bf16[128,640]{1,0:T(8,128)(2,1)S(1)}, bf16[128,640]{1,0:T(8,128)(2,1)}, u32[]{:S(2)}) copy-start(bf16[128,640]{1,0:T(8,128)(2,1)} %w_ref.5) | copy-start | bytes 491524
  30.0 5.6 %copy-start.1 = (bf16[24,48,128]{2,1,0:T(8,128)(2,1)S(1)}, bf16[24,48,128]{2,1,0:T(8,128)(2,1)}, u32[]{:S(2)}) copy-start(bf16[24,48,128]{2,1,0:T(8,128)(2,1)} %param.9) | copy-start | bytes 884740
  30.1 5.6 %copy-start.2 = (bf16[24,48,128]{2,1,0:T(8,128)(2,1)S(1)}, bf16[24,48,128]{2,1,0:T(8,128)(2,1)}, u32[]{:S(2)}) copy-start(bf16[24,48,128]{2,1,0:T(8,128)(2,1)} %param.17) | copy-start | bytes 884740
  30.1 16.7 %all-to-all-start.1 = ((bf16[128,3,4,128]{3,2,1,0:T(4,128)(2,1)}), bf16[128,3,4,128]{3,2,1,0:T(4,128)(2,1)S(1)}, u32[]{:S(2)}, u32[]{:S(2)}) async-start(bf16[128,3,4,128]{3,2,1,0:T(4,128)(2,1)} %bitcast.5), calls=%async_computation.1 | async-start | bytes 786432 | tf_op jit(solution)/shard_map/all_to_all | solution.py:426
  35.6 0.7 copy-start.6
  36.3 10.5 %copy-start.5 = (bf16[128,128]{1,0:T(8,128)(2,1)S(1)}, bf16[128,128]{1,0:T(8,128)(2,1)}, u32[]{:S(2)}) copy-start(bf16[128,128]{1,0:T(8,128)(2,1)} %w_out_ref.3) | copy-start | bytes 98308
  48.2 5.3 %copy-start.8 = (s32[384]{0:T(512)S(1)}, s32[384]{0:T(512)}, u32[]{:S(2)}) copy-start(s32[384]{0:T(512)} %mask_s.1) | copy-start | bytes 4612
  48.2 16.6 %all-to-all-start.2 = ((bf16[128,3,4,128]{3,2,1,0:T(4,128)(2,1)}), bf16[128,3,4,128]{3,2,1,0:T(4,128)(2,1)S(1)}, u32[]{:S(2)}, u32[]{:S(2)}) async-start(bf16[128,3,4,128]{3,2,1,0:T(4,128)(2,1)} %bitcast.11), calls=%async_computation.2 | async-start | bytes 786432 | tf_op jit(solution)/shard_map/all_to_all | solution.py:426
  53.5 0.7 copy-start.9
  58.0 9.4 %copy-start.3 = (bf16[2,128,128]{2,1,0:T(8,128)(2,1)}, bf16[2,128,128]{2,1,0:T(8,128)(2,1)S(1)}, u32[]{:S(2)}) copy-start(bf16[2,128,128]{2,1,0:T(8,128)(2,1)S(1)} %get-tuple-element.39.grads_ref) | copy-start | bytes 196612
  67.4 18.0 %copy-start.4 = (bf16[2,128,128]{2,1,0:T(8,128)(2,1)S(1)}, bf16[2,128,128]{2,1,0:T(8,128)(2,1)}, u32[]{:S(2)}) copy-start(bf16[2,128,128]{2,1,0:T(8,128)(2,1)} %copy-done.3) | copy-start | bytes 196612
  102.0 14.5 %all-to-all-start.5 = ((bf16[128,3,2,128]{3,2,1,0:T(2,128)(2,1)}), bf16[128,3,2,128]{3,2,1,0:T(2,128)(2,1)S(1)}, u32[]{:S(2)}, u32[]{:S(2)}) async-start(bf16[128,3,2,128]{3,2,1,0:T(2,128)(2,1)} %bitcast.18), calls=%async_computation.5 | async-start | bytes 393216 | tf_op jit(solution)/shard_map/all_to_all | solution.py:426
  106.7 0.7 copy-start.7

commit v6 on v5

--- a/solution.py
+++ b/solution.py
@@ -17,7 +17,7 @@
 CELLS = A * B
 H = 128
 N = NR * A
-BOTH, ONE, SUMS = 18, 12, 6
+BOTH, ONE, SUMS = 18, 10, 6
 
 NT = ((1,), (1,))
 TN = ((0,), (0,))
@@ -46,11 +46,14 @@
     )
 
 
+def pieces(q):
+    if q == 8:
+        return [((16 + n) * B + 32, 16 * n, 16) for n in range(8)]
+    return [(q * B, 0, B), ((8 + q) * B, B, B), ((16 + q) * B, 2 * B, 32)]
+
+
 def row_cells(ref, q):
-    none = jnp.zeros((HALF - B, H), BF16)
-    return jnp.concatenate(
-        [ref[q * B : (q + 1) * B, :], none, ref[(q + ONE) * B : (q + ONE + 1) * B, :], none], 0
-    )
+    return jnp.concatenate([ref[at : at + size, :] for at, _, size in pieces(q)], 0)
 
 
 def column(row):
@@ -125,17 +128,24 @@
     copies = [
         pltpu.make_async_copy(src, dst, sems.at[n])
         for n, (src, dst) in enumerate(
-            [(w_h, w_v), (pair_h, pair_v), (mask_h, mask_s), (gain_h, gain_v), (bias_h, bias_v)]
+            [(mask_h, mask_s), (gain_h, gain_v), (bias_h, bias_v), (w_h, w_v)]
         )
     ]
-    for copy in copies:
+    parts = [
+        pltpu.make_async_copy(pair_h.at[rows], pair_v.at[rows], sems.at[4 + n])
+        for n, rows in enumerate(pl.ds(start * CELLS // 3, CELLS // 3) for start in (2, 0, 1))
+    ]
+    for copy in copies[3:] + parts + copies[:3]:
         copy.start()
-    for copy in copies:
+    copies[3].wait()
+    weights = stacked_weights(w_v)
+    for copy in copies[:3]:
         copy.wait()
-    weights = stacked_weights(w_v)
     col_mask = column_mask(mask_s)
     gain, bias = gain_v[...], bias_v[...]
-    for pair_at in (8, 9, 10, 11, 0, 1, 2, 3, 4, 5, 6, 7):
+    for n, pair_at in enumerate((8, 9, 10, 11, 0, 1, 2, 3, 4, 5, 6, 7)):
+        if n % 4 == 0:
+            parts[n // 4].wait()
         rows = pl.ds(pair_at * 2 * B, 2 * B)
         normal, _ = norm_rows(pair_v[rows, :].astype(F32))
         normed = (normal * gain + bias).astype(BF16)
@@ -169,40 +179,36 @@
     return out
 
 
-def by_row(x, shift, step):
-    at = lax.broadcasted_iota(jnp.int32, (8, LANES), 0) & 3
-    out = roll(x, shift)
-    for m in range(1, 4):
-        out = jnp.where(at == m, roll(x, shift + step * m), out)
-    return out
-
-
-def two_rows(scratch, start):
-    first, second = (
-        jnp.broadcast_to(scratch[pl.ds(start + n, 1), :], (8, LANES)) for n in range(2)
-    )
-    return jnp.where(lax.broadcasted_iota(jnp.int32, (8, LANES), 0) < 4, first, second)
-
-
-def mix_kernel(recv_ref, send_ref, left_h, right_h, left_ref, right_ref, scratch, mixed, out, sems):
-    scratch[...] = recv_ref[...].astype(F32)
-    right_ref[...] = jnp.zeros_like(right_ref)
-    lane, wide = lane_of((8, LANES)), lane_of((16, LANES))
+def mix_kernel(recv_ref, send_ref, left_h, right_h, left_ref, right_ref, scratch, third, mixed,
+               out, sems):
+    scratch[...] = recv_ref[...].astype(F32)
+    lane, wide = lane_of((8, LANES)), lane_of((NR, LANES))
+    for p in range(NC // 2):
+        for n in range(8):
+            x, y = (
+                scratch[pl.ds(c * BOTH + 16 + n // 4, NR, stride=NC * BOTH), :]
+                for c in (2 * p, 2 * p + 1)
+            )
+            shift = -32 * (n % 4)
+            third[pl.ds(p * LANES + n, NR, stride=8), :] = jnp.where(
+                wide < HALF, roll(x, shift + 16), roll(y, shift + 80)
+            )
     for r2 in range(NR // 2):
+        right_ref[r2 * HALF + B : (r2 + 1) * HALF, :] = jnp.zeros((HALF - B, 512), BF16)
         for p in range(NC // 2):
             lefts, rights = [], []
             for r in (2 * r2, 2 * r2 + 1):
                 start = (r * NC + 2 * p) * BOTH
                 x, y = scratch[pl.ds(start, 16), :], scratch[pl.ds(start + BOTH, 16), :]
-                x_tail, y_tail = two_rows(scratch, start + 16), two_rows(scratch, start + BOTH + 16)
+                tail = third[p * LANES + r * 8 : p * LANES + r * 8 + 8, :]
                 lefts += [
                     jnp.where(wide < HALF, x, roll(y, HALF)),
                     pick(lane, roll(x[:8], 32), 32, roll(x[8:], HALF), HALF, roll(y[:8], 96), 96, y[8:]),
                 ]
                 rights += [
                     pick(wide, roll(x, -B), B, 0.0, HALF, roll(y, HALF - B), HALF + B, 0.0),
-                    pick(lane, roll(x[8:], 16), 16, by_row(x_tail, 16, -32), B, 0.0, HALF,
-                         roll(y[8:], 80), 80, by_row(y_tail, 80, -32), HALF + B, 0.0),
+                    pick(lane, roll(x[8:], 16), 16, tail, B, 0.0, HALF,
+                         roll(y[8:], 80), 80, tail, HALF + B, 0.0),
                 ]
             lanes = slice(p * LANES, (p + 1) * LANES)
             left_ref[r2 * B : (r2 + 1) * B, lanes] = jnp.concatenate(lefts, 0).astype(BF16)
@@ -211,16 +217,29 @@
               pltpu.make_async_copy(right_ref, right_h, sems.at[1])]
     for copy in copies:
         copy.start()
-    mixed[...] = dot(left_ref[...], right_ref[...], NT)
-    low = lane_of((ONE, LANES)) < HALF
+    product = dot(left_ref[...], right_ref[...], NT)
+    for p in range(NC // 2):
+        mixed[p * N : (p + 1) * N, :] = product[:, p * LANES : (p + 1) * LANES]
     for r in range(NR):
         for p in range(NC // 2):
-            lanes = slice(p * LANES, (p + 1) * LANES)
-            x = mixed[pl.ds(r * A, ONE), lanes]
-            y = mixed[pl.ds(r * A + ONE, ONE), lanes]
+            t0, t1, t2 = (
+                mixed[p * N + r * A + 8 * t : p * N + r * A + 8 * t + 8, :] for t in range(3)
+            )
             start = (r * NC + 2 * p) * ONE
-            out[pl.ds(start, ONE), :] = jnp.where(low, x, roll(y, HALF))
-            out[pl.ds(start + ONE, ONE), :] = jnp.where(low, roll(x, HALF), y)
+            out[pl.ds(start, 8), :] = pick(lane, t0, B, roll(t1, B), 2 * B, roll(t2, 96))
+            out[pl.ds(start + ONE, 8), :] = pick(
+                lane, roll(t0, HALF), B, roll(t1, -16), 2 * B, roll(t2, 32)
+            )
+    out[pl.ds(9, ND, stride=ONE), :] = jnp.zeros((ND, LANES), F32)
+    group = wide >> 4
+    for p in range(NC // 2):
+        first = second = jnp.zeros((NR, LANES), F32)
+        for n in range(8):
+            t2 = mixed[pl.ds(p * N + 16 + n, NR, stride=A), :]
+            first = jnp.where(group == n, roll(t2, 16 * n - 32), first)
+            second = jnp.where(group == n, roll(t2, 16 * n - 96), second)
+        out[pl.ds(2 * p * ONE + 8, NR, stride=NC * ONE), :] = first
+        out[pl.ds((2 * p + 1) * ONE + 8, NR, stride=NC * ONE), :] = second
     send_ref[...] = out[...].astype(BF16)
     for copy in copies:
         copy.wait()
@@ -230,7 +249,7 @@
     scratch[...] = recv_ref[...].astype(F32)
     gain = spread_ref[...]
     w_out = w_out_ref[...]
-    for q in range(ONE):
+    for q in range(9):
         wt = dot(w_out, row_cells(dproj_ref, q), NT) * gain
         normal, scale = norm_cells(scratch[pl.ds(q, H, stride=ONE), :])
         scratch[pl.ds(q, H, stride=ONE), :] = scale * (
@@ -257,15 +276,15 @@
     gain, bias = column(gain_ref[...]), column(bias_ref[...])
     w_out, w_og = w_out_ref[...], w_ref[:, 4 * H :]
     grad = jnp.zeros((H, H), F32)
-    for q in range(ONE):
+    for q in range(9):
         normal, _ = norm_cells(scratch[pl.ds(q, H, stride=ONE), :])
         out_normed = (normal * gain + bias).astype(BF16)
         projected = dot(out_normed, w_out, TN)
         grad = grad + dot(out_normed, row_cells(dproj_ref, q), NN)
-        for k in range(2):
-            rows = pl.ds((q + ONE * k) * B, B)
-            sig = jax.nn.sigmoid(dot(normed_ref[rows, :], w_og, NN))
-            proj = projected[k * HALF : k * HALF + B]
+        gates = jax.nn.sigmoid(dot(row_cells(normed_ref, q), w_og, NN))
+        for at, lane, size in pieces(q):
+            rows = pl.ds(at, size)
+            sig, proj = gates[lane : lane + size], projected[lane : lane + size]
             update_ref[rows, :] = (sig * proj).astype(BF16)
             d_og_ref[rows, :] = (
                 cot_ref[rows, :].astype(F32) * proj * sig * (1.0 - sig)
@@ -277,7 +296,7 @@
 
 
 def back_kernel(recv_ref, left_h, right_h, pg_h, pvg_h, send_ref, pg_ref, pvg_ref,
-                left_ref, right_ref, scratch, d_tile, d_left, d_right, out, tails, sems):
+                left_ref, right_ref, scratch, d_tile, d_left, d_right, out, sems):
     copies = [
         pltpu.make_async_copy(src, dst, sems.at[n])
         for n, (src, dst) in enumerate(
@@ -287,45 +306,62 @@
     for copy in copies:
         copy.start()
     scratch[...] = recv_ref[...].astype(F32)
-    low = lane_of((ONE, LANES)) < HALF
+    lane, wide = lane_of((8, LANES)), lane_of((NR, LANES))
+    for p in range(NC // 2):
+        x, y = (
+            scratch[pl.ds(c * ONE + 8, NR, stride=NC * ONE), :] for c in (2 * p, 2 * p + 1)
+        )
+        for n in range(8):
+            d_tile[pl.ds(p * N + 16 + n, NR, stride=A), :] = jnp.where(
+                wide < HALF, roll(x, 32 - 16 * n), roll(y, 96 - 16 * n)
+            )
+    for r in range(NR):
+        for p in range(NC // 2):
+            start = (r * NC + 2 * p) * ONE
+            x, y = scratch[pl.ds(start, 8), :], scratch[pl.ds(start + ONE, 8), :]
+            at = p * N + r * A
+            tail = d_tile[at + 16 : at + 24, :]
+            d_tile[at : at + 8, :] = jnp.where(lane < HALF, x, roll(y, HALF))
+            d_tile[at + 8 : at + 16, :] = jnp.where(lane < HALF, roll(x, -B), roll(y, 16))
+            d_tile[at + 16 : at + 24, :] = pick(
+                lane, roll(x, 32), 32, tail, HALF, roll(y, 96), 96, tail
+            )
+    d = jnp.concatenate([d_tile[p * N : (p + 1) * N, :].astype(BF16) for p in range(4)], 1)
+    copies[0].wait()
+    copies[1].wait()
+    d_left[...] = dot(d, right_ref[...], NN)
+    product = dot(d, left_ref[...], TN)
+    for p in range(NC // 2):
+        d_right[p * 512 : (p + 1) * 512, :] = product[:, p * LANES : (p + 1) * LANES]
     for r in range(NR):
         for p in range(NC // 2):
             lanes = slice(p * LANES, (p + 1) * LANES)
-            start = (r * NC + 2 * p) * ONE
-            x = scratch[pl.ds(start, ONE), :]
-            y = scratch[pl.ds(start + ONE, ONE), :]
-            d_tile[pl.ds(r * A, ONE), lanes] = jnp.where(low, x, roll(y, HALF))
-            d_tile[pl.ds(r * A + ONE, ONE), lanes] = jnp.where(low, roll(x, HALF), y)
-    d = d_tile[...].astype(BF16)
-    copies[0].wait()
-    copies[1].wait()
-    d_left[...] = dot(d, right_ref[...], NN)
-    d_right[...] = dot(d, left_ref[...], TN)
-    lane = lane_of((8, LANES))
-    mine = (lane >> 5) == (lax.broadcasted_iota(jnp.int32, (8, LANES), 0) & 3)
-    for r in range(NR):
-        for p in range(NC // 2):
-            lanes = slice(p * LANES, (p + 1) * LANES)
-            at = (r // 2) * HALF + (r % 2) * A
+            at = p * 512 + (r // 2) * HALF + (r % 2) * A
             x0, x1, x2 = (d_left[r * A + 8 * t : r * A + 8 * t + 8, lanes] for t in range(3))
-            y0, y1, y2 = (d_right[at + 8 * t : at + 8 * t + 8, lanes] for t in range(3))
-            first = (r * NC + 2 * p) * BOTH
-            second = first + BOTH
-            out[pl.ds(first, 8), :] = pick(lane, x0, B, roll(y0, B), 2 * B, roll(x2, 96))
-            out[pl.ds(first + 8, 8), :] = pick(
+            y0, y1, y2 = (d_right[at + 8 * t : at + 8 * t + 8, :] for t in range(3))
+            start = (r * NC + 2 * p) * BOTH
+            out[pl.ds(start, 8), :] = pick(lane, x0, B, roll(y0, B), 2 * B, roll(x2, 96))
+            out[pl.ds(start + 8, 8), :] = pick(
                 lane, x1, B, roll(y1, B), 2 * B, roll(x2, HALF), 112, roll(y2, 112)
             )
-            out[pl.ds(second, 8), :] = pick(lane, roll(x0, HALF), B, roll(y0, -16), 2 * B, roll(x2, 32))
-            out[pl.ds(second + 8, 8), :] = pick(
+            start = start + BOTH
+            out[pl.ds(start, 8), :] = pick(lane, roll(x0, HALF), B, roll(y0, -16), 2 * B, roll(x2, 32))
+            out[pl.ds(start + 8, 8), :] = pick(
                 lane, roll(x1, HALF), B, roll(y1, -16), 2 * B, x2, 112, roll(y2, B)
             )
-            for start, shift in ((first, -16), (second, -80)):
-                row = start // BOTH * 8
-                tails[row : row + 8, :] = jnp.where(mine, by_row(y2, shift, 32), 0.0)
-    quarters = [tails[pl.ds(n, 2 * ND, stride=4), :] for n in range(4)]
-    tails[: 2 * ND, :] = quarters[0] + quarters[1] + quarters[2] + quarters[3]
-    for n in range(2):
-        out[pl.ds(16 + n, ND, stride=BOTH), :] = tails[pl.ds(n, ND, stride=2), :]
+    group = lane >> 5
+    for p in range(NC // 2):
+        for odd in range(2):
+            for half in range(2):
+                first = second = jnp.zeros((8, LANES), F32)
+                for m in range(4):
+                    at = p * 512 + odd * A + 16 + 4 * half + m
+                    y2 = d_right[pl.ds(at, 8, stride=HALF), :]
+                    first = jnp.where(group == m, roll(y2, 32 * m - 16), first)
+                    second = jnp.where(group == m, roll(y2, 32 * m - 80), second)
+                start = (odd * NC + 2 * p) * BOTH + 16 + half
+                out[pl.ds(start, 8, stride=2 * NC * BOTH), :] = first
+                out[pl.ds(start + BOTH, 8, stride=2 * NC * BOTH), :] = second
     send_ref[...] = out[...].astype(BF16)
     copies[2].wait()
     copies[3].wait()
@@ -440,7 +476,7 @@
         [mask, pair2, line(in_gain), line(in_bias), w_in],
         [(both_shape, BF16), ((CELLS, H), BF16)],
         [pltpu.SMEM((N,), jnp.int32), vm(CELLS, H, dtype=BF16), vm(1, H), vm(1, H),
-         vm(H, 5 * H, dtype=BF16), vm(8, H, LANES), vm(*both_shape), dma((5,))],
+         vm(H, 5 * H, dtype=BF16), vm(8, H, LANES), vm(*both_shape), dma((7,))],
         400_000_000, hbm_in=range(5),
     )
     recv = exchange(send, 9, 2)
@@ -455,11 +491,11 @@
         mix_kernel,
         [recv],
         [(one_shape, BF16), ((N, 512), BF16), ((512, 512), BF16)],
-        [vm(N, 512, dtype=BF16), vm(512, 512, dtype=BF16), vm(*both_shape), vm(N, 512),
-         vm(*one_shape), dma((2,))],
+        [vm(N, 512, dtype=BF16), vm(512, 512, dtype=BF16), vm(*both_shape), vm(512, LANES),
+         vm(4 * N, LANES), vm(*one_shape), dma((2,))],
         400_000_000, hbm_out=(1, 2),
     )
-    mixed = exchange(send, 3, 4)
+    mixed = exchange(send, 5, 2)
     (send,) = call(
         d_mixed_kernel,
         [mixed, dproj, w_out, spread],
@@ -467,7 +503,7 @@
         [vm(*one_shape)],
         50_000_000,
     )
-    recv = exchange(send, 3, 4)
+    recv = exchange(send, 5, 2)
     update, d_og, grads, pg, pvg = call(
         update_kernel,
         [mask, mixed, w_out, line(out_gain), line(out_bias), dproj, cot2, normed, w_in],
@@ -480,9 +516,8 @@
         back_kernel,
         [recv, left, right, pg, pvg],
         [(both_shape, BF16), ((A, H, LANES), BF16), ((A, H, LANES), BF16)],
-        [vm(N, 512, dtype=BF16), vm(512, 512, dtype=BF16), vm(*one_shape), vm(N, 512),
-         vm(N, 512), vm(512, 512), vm(*both_shape), vm(8 * ND, LANES),
-         dma((4,))],
+        [vm(N, 512, dtype=BF16), vm(512, 512, dtype=BF16), vm(*one_shape), vm(4 * N, LANES),
+         vm(N, 512), vm(4 * 512, LANES), vm(*both_shape), dma((4,))],
         800_000_000, hbm_in=(1, 2, 3, 4),
     )
     recv = exchange(send, 9, 2)

time: 118 us -> 117 us (level)
  no operation moved by 1% of the time
where the time goes in v6:
time: 117 us
  blocking collectives  57.3 us (49%)
  Pallas kernels  21.1 us (18%)
  waiting for transfers between devices  20.3 us (17%)
  starting transfers between devices  15.4 us (13%)
  local copies, waits for them, and re-layouts  1.94 us (2%)
    all_to_all x3, blocking collectives, exchange(): moved = lax.all_to_all(x.reshape(ND, *tile, LANES), AXES, 0, 0, tiled=True)  57.3 us
    pallas_call x10, Pallas kernels, call(): pl.pallas_call(kernel, out_shape=shapes, in_specs=specs, out_specs=[HBM_S...  21.1 us
    all_to_all x3, waiting for transfers between devices, exchange(): moved = lax.all_to_all(x.reshape(ND, *tile, LANES), AXES, 0, 0, tiled=True)  20.3 us
    all_to_all x3, starting transfers between devices, exchange(): moved = lax.all_to_all(x.reshape(ND, *tile, LANES), AXES, 0, 0, tiled=True)  15.4 us
  transfers between devices with their start and end apart: 3, of which 3 were waited for; matrix products, arithmetic and copies ran while one was open for 0% of the time, Pallas kernels for 8%

profile of v6, /device:TPU:1, one launch (start us, length us, event | category | flops | bytes accessed | tf_op | source)
XLA Modules:
  0.0 116.8 jit_solution(15679668617107326252)
XLA Ops:
  0.6 3.0 %shard_map.120 = (bf16[2304,128]{1,0:T(8,128)(2,1)S(1)}, bf16[1152,128]{1,0:T(8,128)(2,1)S(1)}) custom-call(s32[384]{0:T(512)} %mask_s.1, bf16[1152,128]{1,0:T(8,128)(2,1)} %bitcast.31, f32[1,128]{1,0:T(1,128)} %bitcast.37, f32[1,128]{1,0:T(1,128)} %bitcast.41, bf16[128,640]{1,0:T(8,128)(2,1)} %w_ref.5), custom_call_target="tpu_custom_call" | custom-call | flops 400000000 | bytes 1344768 | tf_op jit(solution)/shard_map/pallas_call | solution.py:446
  3.6 24.2 %all_to_all.30 = bf16[128,9,2,128]{3,2,1,0:T(2,128)(2,1)S(1)} all-to-all(bf16[128,9,2,128]{3,2,1,0:T(2,128)(2,1)S(1)} %bitcast.29), channel_id=1, replica_groups=mesh['row'=16,'col'=8] {'row','col'}, dimensions={0} | all-to-all | bytes 1179648 | tf_op jit(solution)/shard_map/all_to_all | solution.py:462
  27.8 3.0 %shard_map.121 = (bf16[1280,128]{1,0:T(8,128)(2,1)}, bf16[384,512]{1,0:T(8,128)(2,1)}, bf16[512,512]{1,0:T(8,128)(2,1)}) custom-call(bf16[2304,128]{1,0:T(8,128)(2,1)S(1)} %bitcast.28), custom_call_target="tpu_custom_call" | custom-call | flops 400000000 | bytes 1835008 | tf_op jit(solution)/shard_map/pallas_call | solution.py:446
  30.8 0.0 copy-start
  30.8 0.0 copy-start.1
  30.8 5.5 %all-to-all-start.1 = ((bf16[128,5,2,128]{3,2,1,0:T(2,128)(2,1)}), bf16[128,5,2,128]{3,2,1,0:T(2,128)(2,1)S(1)}, u32[]{:S(2)}, u32[]{:S(2)}) async-start(bf16[128,5,2,128]{3,2,1,0:T(2,128)(2,1)} %bitcast.5), calls=%async_computation.1 | async-start | bytes 655360 | tf_op jit(solution)/shard_map/all_to_all | solution.py:462
  36.3 0.0 copy-start.4
  36.4 0.0 copy-done.2
  36.4 0.0 copy-done
  36.4 0.0 copy-done.1
  36.4 0.6 copy-done.4
  37.0 0.5 shard_map.122
  37.5 9.5 %all-to-all-done.1 = bf16[128,5,2,128]{3,2,1,0:T(2,128)(2,1)S(1)} async-done(((bf16[128,5,2,128]{3,2,1,0:T(2,128)(2,1)}), bf16[128,5,2,128]{3,2,1,0:T(2,128)(2,1)S(1)}, u32[]{:S(2)}, u32[]{:S(2)}) %all-to-all-start.1) | async-done | bytes 327712 | tf_op jit(solution)/shard_map/all_to_all | solution.py:462
  47.0 0.0 copy-done.3
  47.0 1.3 %shard_map.124 = bf16[1280,128]{1,0:T(8,128)(2,1)} custom-call(bf16[1280,128]{1,0:T(8,128)(2,1)S(1)} %bitcast.22, bf16[1152,128]{1,0:T(8,128)(2,1)S(1)} %get-tuple-element.26.dproj_ref, bf16[128,128]{1,0:T(8,128)(2,1)S(1)} %copy-done.3, f32[128,128]{1,0:T(8,128)S(1)} %get-tuple-element.28.spread_ref), custom_call_target="tpu_custom_call" | custom-call | flops 50000000 | bytes 1015808 | tf_op jit(solution)/shard_map/pallas_call | solution.py:446
  48.2 5.2 %all-to-all-start.2 = ((bf16[128,5,2,128]{3,2,1,0:T(2,128)(2,1)}), bf16[128,5,2,128]{3,2,1,0:T(2,128)(2,1)S(1)}, u32[]{:S(2)}, u32[]{:S(2)}) async-start(bf16[128,5,2,128]{3,2,1,0:T(2,128)(2,1)} %bitcast.11), calls=%async_computation.2 | async-start | bytes 655360 | tf_op jit(solution)/shard_map/all_to_all | solution.py:462
  53.4 0.0 copy-start.7
  53.5 0.0 copy-done.6
  53.5 0.6 copy-done.7
  54.1 3.6 %shard_map.123 = (bf16[1152,128]{1,0:T(8,128)(2,1)}, bf16[1152,128]{1,0:T(8,128)(2,1)S(1)}, bf16[2,128,128]{2,1,0:T(8,128)(2,1)S(1)}, bf16[24,128,128]{2,1,0:T(8,128)(2,1)}, bf16[24,128,128]{2,1,0:T(8,128)(2,1)}) custom-call(s32[384]{0:T(512)S(1)} %copy-done.6, bf16[1280,128]{1,0:T(8,128)(2,1)S(1)} %bitcast.23, bf16[128,128]{1,0:T(8,128)(2,1)S(1)} %copy-done.3, ...), custom_call_target="tpu_custom_call" | custom-call | flops 600000000 | bytes 3638528 | tf_op jit(solution)/shard_map/pallas_call | solution.py:446
  57.7 6.5 %all-to-all-done.2 = bf16[128,5,2,128]{3,2,1,0:T(2,128)(2,1)S(1)} async-done(((bf16[128,5,2,128]{3,2,1,0:T(2,128)(2,1)}), bf16[128,5,2,128]{3,2,1,0:T(2,128)(2,1)S(1)}, u32[]{:S(2)}, u32[]{:S(2)}) %all-to-all-start.2) | async-done | bytes 327712 | tf_op jit(solution)/shard_map/all_to_all | solution.py:462
  64.2 2.8 %shard_map.125 = (bf16[2304,128]{1,0:T(8,128)(2,1)S(1)}, bf16[24,128,128]{2,1,0:T(8,128)(2,1)S(1)}, bf16[24,128,128]{2,1,0:T(8,128)(2,1)S(1)}) custom-call(bf16[1280,128]{1,0:T(8,128)(2,1)S(1)} %bitcast.30, bf16[384,512]{1,0:T(8,128)(2,1)} %get-tuple-element.29.left_h, bf16[512,512]{1,0:T(8,128)(2,1)} %get-tuple-element.30.right_h, ...), custom_call_target="tpu_custom_call" | custom-call | flops 800000000 | bytes 4980736 | tf_op jit(solution)/shard_map/pallas_call | solution.py:446
  67.0 17.8 %all_to_all.31 = bf16[128,9,2,128]{3,2,1,0:T(2,128)(2,1)S(1)} all-to-all(bf16[128,9,2,128]{3,2,1,0:T(2,128)(2,1)S(1)} %bitcast.27), channel_id=1, replica_groups=mesh['row'=16,'col'=8] {'row','col'}, dimensions={0} | all-to-all | bytes 1179648 | tf_op jit(solution)/shard_map/all_to_all | solution.py:462
  84.8 0.6 shard_map.127
  85.5 15.2 %all_to_all.32 = bf16[128,3,2,128]{3,2,1,0:T(2,128)(2,1)S(1)} all-to-all(bf16[128,3,2,128]{3,2,1,0:T(2,128)(2,1)S(1)} %bitcast.26), channel_id=1, replica_groups=mesh['row'=16,'col'=8] {'row','col'}, dimensions={0} | all-to-all | bytes 393216 | tf_op jit(solution)/shard_map/all_to_all | solution.py:462
  100.7 0.7 shard_map.128
  101.4 4.7 %all-to-all-start.5 = ((bf16[128,3,2,128]{3,2,1,0:T(2,128)(2,1)}), bf16[128,3,2,128]{3,2,1,0:T(2,128)(2,1)S(1)}, u32[]{:S(2)}, u32[]{:S(2)}) async-start(bf16[128,3,2,128]{3,2,1,0:T(2,128)(2,1)} %bitcast.18), calls=%async_computation.5 | async-start | bytes 393216 | tf_op jit(solution)/shard_map/all_to_all | solution.py:462
  106.1 0.0 copy-start.5
  106.1 0.6 copy-done.5
  106.8 4.7 %shard_map.126 = bf16[1152,128]{1,0:T(8,128)(2,1)} custom-call(bf16[2304,128]{1,0:T(8,128)(2,1)S(1)} %bitcast.21, bf16[24,128,128]{2,1,0:T(8,128)(2,1)} %get-tuple-element.31.pg_h, bf16[24,128,128]{2,1,0:T(8,128)(2,1)} %get-tuple-element.32.pvg_h, bf16[1152,128]{1,0:T(8,128)(2,1)S(1)} %get-tuple-element.34.d_og_ref, ...), custom_call_target="tpu_custom_call" | custom-call | flops 400000000 | bytes 3506432 | tf_op jit(solution)/shard_map/pallas_call | solution.py:446
  111.5 4.4 %all-to-all-done.5 = bf16[128,3,2,128]{3,2,1,0:T(2,128)(2,1)S(1)} async-done(((bf16[128,3,2,128]{3,2,1,0:T(2,128)(2,1)}), bf16[128,3,2,128]{3,2,1,0:T(2,128)(2,1)S(1)}, u32[]{:S(2)}, u32[]{:S(2)}) %all-to-all-start.5) | async-done | bytes 196640 | tf_op jit(solution)/shard_map/all_to_all | solution.py:462
  115.9 0.9 shard_map.129
  (3 shorter events, 0.0 us)
Async XLA Ops:
  27.8 8.6 %copy-start.2 = (bf16[24,48,128]{2,1,0:T(8,128)(2,1)S(1)}, bf16[24,48,128]{2,1,0:T(8,128)(2,1)}, u32[]{:S(2)}) copy-start(bf16[24,48,128]{2,1,0:T(8,128)(2,1)} %param.17) | copy-start | bytes 884740
  30.8 5.6 %copy-start = (bf16[128,640]{1,0:T(8,128)(2,1)S(1)}, bf16[128,640]{1,0:T(8,128)(2,1)}, u32[]{:S(2)}) copy-start(bf16[128,640]{1,0:T(8,128)(2,1)} %w_ref.5) | copy-start | bytes 491524
  30.8 5.6 %copy-start.1 = (bf16[24,48,128]{2,1,0:T(8,128)(2,1)S(1)}, bf16[24,48,128]{2,1,0:T(8,128)(2,1)}, u32[]{:S(2)}) copy-start(bf16[24,48,128]{2,1,0:T(8,128)(2,1)} %param.9) | copy-start | bytes 884740
  30.8 16.2 %all-to-all-start.1 = ((bf16[128,5,2,128]{3,2,1,0:T(2,128)(2,1)}), bf16[128,5,2,128]{3,2,1,0:T(2,128)(2,1)S(1)}, u32[]{:S(2)}, u32[]{:S(2)}) async-start(bf16[128,5,2,128]{3,2,1,0:T(2,128)(2,1)} %bitcast.5), calls=%async_computation.1 | async-start | bytes 655360 | tf_op jit(solution)/shard_map/all_to_all | solution.py:462
  36.3 0.7 copy-start.4
  37.0 10.0 %copy-start.3 = (bf16[128,128]{1,0:T(8,128)(2,1)S(1)}, bf16[128,128]{1,0:T(8,128)(2,1)}, u32[]{:S(2)}) copy-start(bf16[128,128]{1,0:T(8,128)(2,1)} %w_out_ref.3) | copy-start | bytes 98308
  48.2 5.2 %copy-start.6 = (s32[384]{0:T(512)S(1)}, s32[384]{0:T(512)}, u32[]{:S(2)}) copy-start(s32[384]{0:T(512)} %mask_s.1) | copy-start | bytes 4612
  48.2 16.0 %all-to-all-start.2 = ((bf16[128,5,2,128]{3,2,1,0:T(2,128)(2,1)}), bf16[128,5,2,128]{3,2,1,0:T(2,128)(2,1)S(1)}, u32[]{:S(2)}, u32[]{:S(2)}) async-start(bf16[128,5,2,128]{3,2,1,0:T(2,128)(2,1)} %bitcast.11), calls=%async_computation.2 | async-start | bytes 655360 | tf_op jit(solution)/shard_map/all_to_all | solution.py:462
  53.4 0.7 copy-start.7
  101.4 14.5 %all-to-all-start.5 = ((bf16[128,3,2,128]{3,2,1,0:T(2,128)(2,1)}), bf16[128,3,2,128]{3,2,1,0:T(2,128)(2,1)S(1)}, u32[]{:S(2)}, u32[]{:S(2)}) async-start(bf16[128,3,2,128]{3,2,1,0:T(2,128)(2,1)} %bitcast.18), calls=%async_computation.5 | async-start | bytes 393216 | tf_op jit(solution)/shard_map/all_to_all | solution.py:462
  106.1 0.7 copy-start.5

commit v7 on v6

--- a/solution.py
+++ b/solution.py
@@ -123,33 +123,33 @@
     return center * scale, scale
 
 
-def project_kernel(mask_h, pair_h, gain_h, bias_h, w_h, send_ref, normed_ref,
-                   mask_s, pair_v, gain_v, bias_v, w_v, third, scratch, sems):
+def project_kernel(mask_h, pair_h, gain_h, bias_h, w_h, cot_h, out_gain_h, w_out_h,
+                   send_ref, normed_ref, dproj_ref, spread_ref, w_out_ref,
+                   mask_s, pair_v, gain_v, bias_v, w_v, cot_v, out_gain_v, third, scratch, sems):
     copies = [
         pltpu.make_async_copy(src, dst, sems.at[n])
-        for n, (src, dst) in enumerate(
-            [(mask_h, mask_s), (gain_h, gain_v), (bias_h, bias_v), (w_h, w_v)]
-        )
+        for n, (src, dst) in enumerate([
+            (w_h, w_v), (pair_h, pair_v), (mask_h, mask_s), (gain_h, gain_v), (bias_h, bias_v),
+            (cot_h, cot_v), (out_gain_h, out_gain_v), (w_out_h, w_out_ref),
+        ])
     ]
-    parts = [
-        pltpu.make_async_copy(pair_h.at[rows], pair_v.at[rows], sems.at[4 + n])
-        for n, rows in enumerate(pl.ds(start * CELLS // 3, CELLS // 3) for start in (2, 0, 1))
-    ]
-    for copy in copies[3:] + parts + copies[:3]:
+    for copy in copies:
         copy.start()
-    copies[3].wait()
+    copies[0].wait()
     weights = stacked_weights(w_v)
-    for copy in copies[:3]:
+    w_og = w_v[:, 4 * H :]
+    for copy in copies[1:]:
         copy.wait()
+    spread_ref[...] = jnp.broadcast_to(column(out_gain_v[...]), (H, LANES))
     col_mask = column_mask(mask_s)
     gain, bias = gain_v[...], bias_v[...]
-    for n, pair_at in enumerate((8, 9, 10, 11, 0, 1, 2, 3, 4, 5, 6, 7)):
-        if n % 4 == 0:
-            parts[n // 4].wait()
+    for pair_at in (8, 9, 10, 11, 0, 1, 2, 3, 4, 5, 6, 7):
         rows = pl.ds(pair_at * 2 * B, 2 * B)
         normal, _ = norm_rows(pair_v[rows, :].astype(F32))
         normed = (normal * gain + bias).astype(BF16)
         normed_ref[rows, :] = normed
+        sig = jax.nn.sigmoid(dot(normed, w_og, NN))
+        dproj_ref[rows, :] = (cot_v[rows, :].astype(F32) * sig).astype(BF16)
         for k, (value, _, pg) in enumerate(gate_parts(weights, normed, pair_at, col_mask, mask_s)):
             a = pair_at * 2 + k
             if a >= 16:
@@ -160,16 +160,6 @@
             for n in range(2):
                 scratch[pl.ds(16 + n, H, stride=BOTH), :] = pack_tail(third, n)
     send_ref[...] = scratch[...].astype(BF16)
-
-
-def gate_kernel(normed_ref, w_ref, cot_ref, pair_ref, gain_ref,
-                dproj_ref, normal_ref, scale_ref, spread_ref):
-    spread_ref[...] = jnp.broadcast_to(column(gain_ref[...]), (H, LANES))
-    sig = jax.nn.sigmoid(dot(normed_ref[...], w_ref[:, 4 * H :], NN))
-    dproj_ref[...] = (cot_ref[...].astype(F32) * sig).astype(BF16)
-    normal, scale = norm_rows(pair_ref[...].astype(F32))
-    normal_ref[...] = normal
-    scale_ref[...] = jnp.broadcast_to(scale, (CELLS, H))
 
 
 def pick(lane, *parts):
@@ -388,7 +378,7 @@
     send_ref[...] = packed[...].astype(BF16)
 
 
-def pair_grad_kernel(recv_ref, pg_h, pvg_h, d_og_ref, normal_ref, scale_ref, gain_ref, w_ref,
+def pair_grad_kernel(recv_ref, pg_h, pvg_h, d_og_ref, pair_ref, gain_ref, w_ref,
                      out_ref, scratch, pg_v, pvg_v, sems):
     copies = [pltpu.make_async_copy(pg_h, pg_v, sems.at[0]),
               pltpu.make_async_copy(pvg_h, pvg_v, sems.at[1])]
@@ -404,11 +394,11 @@
         rows = pl.ds(a * B, B)
         both = dot(gated(scratch, a, pg_v, pvg_v), weights, TN)
         d = both[:B, :H] + both[B : 2 * B, H:] + dot(d_og_ref[rows, :], w_og, NT)
-        normal = normal_ref[rows, :]
+        normal, scale = norm_rows(pair_ref[rows, :].astype(F32))
         weighted = d * gain
         out_ref[rows, :] = (
-            scale_ref[rows, :] * (weighted - jnp.mean(weighted, 1, keepdims=True)
-                                  - normal * jnp.mean(weighted * normal, 1, keepdims=True))
+            scale * (weighted - jnp.mean(weighted, 1, keepdims=True)
+                     - normal * jnp.mean(weighted * normal, 1, keepdims=True))
         ).astype(BF16)
 
 
@@ -471,22 +461,17 @@
     both_shape, one_shape, sum_shape = ((ND * n, LANES) for n in (BOTH, ONE, SUMS))
     gates = [vm(A, H, LANES, dtype=BF16)] * 2
 
-    send, normed = call(
+    send, normed, dproj, spread, w_out_near = call(
         project_kernel,
-        [mask, pair2, line(in_gain), line(in_bias), w_in],
-        [(both_shape, BF16), ((CELLS, H), BF16)],
+        [mask, pair2, line(in_gain), line(in_bias), w_in, cot2, line(out_gain), w_out],
+        [(both_shape, BF16), ((CELLS, H), BF16), ((CELLS, H), BF16), ((H, LANES), F32),
+         ((H, H), BF16)],
         [pltpu.SMEM((N,), jnp.int32), vm(CELLS, H, dtype=BF16), vm(1, H), vm(1, H),
-         vm(H, 5 * H, dtype=BF16), vm(8, H, LANES), vm(*both_shape), dma((7,))],
-        400_000_000, hbm_in=range(5),
+         vm(H, 5 * H, dtype=BF16), vm(CELLS, H, dtype=BF16), vm(1, H), vm(8, H, LANES),
+         vm(*both_shape), dma((8,))],
+        500_000_000, hbm_in=range(8),
     )
     recv = exchange(send, 9, 2)
-    dproj, normal, scale, spread = call(
-        gate_kernel,
-        [normed, w_in, cot2, pair2, line(out_gain)],
-        [((CELLS, H), BF16), ((CELLS, H), F32), ((CELLS, H), F32), ((H, LANES), F32)],
-        [],
-        100_000_000,
-    )
     send, left, right = call(
         mix_kernel,
         [recv],
@@ -498,7 +483,7 @@
     mixed = exchange(send, 5, 2)
     (send,) = call(
         d_mixed_kernel,
-        [mixed, dproj, w_out, spread],
+        [mixed, dproj, w_out_near, spread],
         [(one_shape, BF16)],
         [vm(*one_shape)],
         50_000_000,
@@ -506,7 +491,7 @@
     recv = exchange(send, 5, 2)
     update, d_og, grads, pg, pvg = call(
         update_kernel,
-        [mask, mixed, w_out, line(out_gain), line(out_bias), dproj, cot2, normed, w_in],
+        [mask, mixed, w_out_near, line(out_gain), line(out_bias), dproj, cot2, normed, w_in],
         [((CELLS, H), BF16), ((CELLS, H), BF16), ((2, H, H), BF16),
          ((A, H, LANES), BF16), ((A, H, LANES), BF16)],
         [vm(*one_shape), *gates, dma((2,))],
@@ -531,7 +516,7 @@
     parts = exchange(send, 3, 2)
     (pair_grad,) = call(
         pair_grad_kernel,
-        [recv, pg, pvg, d_og, normal, scale, line(in_gain), w_in],
+        [recv, pg, pvg, d_og, pair2, line(in_gain), w_in],
         [((CELLS, H), BF16)],
         [vm(*both_shape), *gates, dma((2,))],
         400_000_000, hbm_in=(1, 2),

time: 117 us -> 116 us (level)
  blocking collectives: 57.3 us -> 73.2 us
  waiting for transfers between devices: 20.3 us -> 8.41 us
  starting transfers between devices: 15.4 us -> 9.92 us
    all_to_all x3 -> x4, blocking collectives: 57.3 us -> 73.2 us  [exchange(): moved = lax.all_to_all(x.reshape(ND, *tile, LANES), AXES, 0, 0, tiled=True)]
    all_to_all x3 -> x2, waiting for transfers between devices: 20.3 us -> 8.41 us  [exchange(): moved = lax.all_to_all(x.reshape(ND, *tile, LANES), AXES, 0, 0, tiled=True)]
    all_to_all x3 -> x2, starting transfers between devices: 15.4 us -> 9.92 us  [exchange(): moved = lax.all_to_all(x.reshape(ND, *tile, LANES), AXES, 0, 0, tiled=True)]
    pallas_call x10 -> x9, Pallas kernels: 21.1 us -> 22.2 us  [call(): pl.pallas_call(kernel, out_shape=shapes, in_specs=specs, out_specs=[HBM_S...]
  transfers between devices with their start and end apart: 3 -> 2, of which waited for: 3 -> 2; matrix products, arithmetic and copies ran while one was open for 0% -> 0% of each run, Pallas kernels for 8% -> 9%
where the time goes in v7:
time: 116 us
  blocking collectives  73.2 us (63%)
  Pallas kernels  22.2 us (19%)
  starting transfers between devices  9.92 us (9%)
  waiting for transfers between devices  8.41 us (7%)
  local copies, waits for them, and re-layouts  1.3 us (1%)
    all_to_all x4, blocking collectives, exchange(): moved = lax.all_to_all(x.reshape(ND, *tile, LANES), AXES, 0, 0, tiled=True)  73.2 us
    pallas_call x9, Pallas kernels, call(): pl.pallas_call(kernel, out_shape=shapes, in_specs=specs, out_specs=[HBM_S...  22.2 us
    all_to_all x2, starting transfers between devices, exchange(): moved = lax.all_to_all(x.reshape(ND, *tile, LANES), AXES, 0, 0, tiled=True)  9.92 us
    all_to_all x2, waiting for transfers between devices, exchange(): moved = lax.all_to_all(x.reshape(ND, *tile, LANES), AXES, 0, 0, tiled=True)  8.41 us
  transfers between devices with their start and end apart: 2, of which 2 were waited for; matrix products, arithmetic and copies ran while one was open for 0% of the time, Pallas kernels for 9%

profile of v7, /device:TPU:1, one launch (start us, length us, event | category | flops | bytes accessed | tf_op | source)
XLA Modules:
  0.0 115.8 jit_solution(13003162087825131814)
XLA Ops:
  0.6 2.8 %shard_map.120 = (bf16[2304,128]{1,0:T(8,128)(2,1)S(1)}, bf16[1152,128]{1,0:T(8,128)(2,1)S(1)}, bf16[1152,128]{1,0:T(8,128)(2,1)S(1)}, f32[128,128]{1,0:T(8,128)S(1)}, bf16[128,128]{1,0:T(8,128)(2,1)S(1)}) custom-call(s32[384]{0:T(512)} %mask_s.1, bf16[1152,128]{1,0:T(8,128)(2,1)} %bitcast.32, f32[1,128]{1,0:T(1,128)} %bitcast.34, f32[1,128]{1,0:T(1,128)} %bitcast.42, ...), custom_call_target="tpu_custom_call" | custom-call | flops 500000000 | bytes 2033152 | tf_op jit(solution)/shard_map/pallas_call | solution.py:436
  3.4 24.2 %all_to_all.30 = bf16[128,9,2,128]{3,2,1,0:T(2,128)(2,1)S(1)} all-to-all(bf16[128,9,2,128]{3,2,1,0:T(2,128)(2,1)S(1)} %bitcast.28), channel_id=1, replica_groups=mesh['row'=16,'col'=8] {'row','col'}, dimensions={0} | all-to-all | bytes 1179648 | tf_op jit(solution)/shard_map/all_to_all | solution.py:452
  27.6 2.2 %shard_map.121 = (bf16[1280,128]{1,0:T(8,128)(2,1)S(1)}, bf16[384,512]{1,0:T(8,128)(2,1)}, bf16[512,512]{1,0:T(8,128)(2,1)}) custom-call(bf16[2304,128]{1,0:T(8,128)(2,1)S(1)} %bitcast.29), custom_call_target="tpu_custom_call" | custom-call | flops 400000000 | bytes 1835008 | tf_op jit(solution)/shard_map/pallas_call | solution.py:436
  29.8 15.9 %all_to_all.31 = bf16[128,5,2,128]{3,2,1,0:T(2,128)(2,1)S(1)} all-to-all(bf16[128,5,2,128]{3,2,1,0:T(2,128)(2,1)S(1)} %bitcast.31), channel_id=1, replica_groups=mesh['row'=16,'col'=8] {'row','col'}, dimensions={0} | all-to-all | bytes 655360 | tf_op jit(solution)/shard_map/all_to_all | solution.py:452
  45.8 1.3 %shard_map.123 = bf16[1280,128]{1,0:T(8,128)(2,1)} custom-call(bf16[1280,128]{1,0:T(8,128)(2,1)S(1)} %bitcast.22, bf16[1152,128]{1,0:T(8,128)(2,1)S(1)} %get-tuple-element.25.dproj_ref, bf16[128,128]{1,0:T(8,128)(2,1)S(1)} %get-tuple-element.24.w_out_ref, f32[128,128]{1,0:T(8,128)S(1)} %get-tuple-element.28.spread_ref), custom_call_target="tpu_custom_call" | custom-call | flops 50000000 | bytes 1015808 | tf_op jit(solution)/shard_map/pallas_call | solution.py:436
  47.0 0.0 copy-start.1
  47.0 0.0 copy-start.3
  47.0 5.2 %all-to-all-start.2 = ((bf16[128,5,2,128]{3,2,1,0:T(2,128)(2,1)}), bf16[128,5,2,128]{3,2,1,0:T(2,128)(2,1)S(1)}, u32[]{:S(2)}, u32[]{:S(2)}) async-start(bf16[128,5,2,128]{3,2,1,0:T(2,128)(2,1)} %bitcast.11), calls=%async_computation.2 | async-start | bytes 655360 | tf_op jit(solution)/shard_map/all_to_all | solution.py:452
  52.3 0.0 copy-start.4
  52.3 0.0 copy-start.5
  52.3 0.0 copy-start.6
  52.3 0.0 copy-done.1
  52.3 0.0 copy-done.3
  52.3 0.6 copy-done.4
  53.0 0.0 copy-done.5
  53.0 0.0 copy-done.6
  53.0 3.6 %shard_map.122 = (bf16[1152,128]{1,0:T(8,128)(2,1)}, bf16[1152,128]{1,0:T(8,128)(2,1)S(1)}, bf16[2,128,128]{2,1,0:T(8,128)(2,1)S(1)}, bf16[24,128,128]{2,1,0:T(8,128)(2,1)}, bf16[24,128,128]{2,1,0:T(8,128)(2,1)}) custom-call(s32[384]{0:T(512)S(1)} %copy-done.4, bf16[1280,128]{1,0:T(8,128)(2,1)S(1)} %bitcast.23, ...), custom_call_target="tpu_custom_call" | custom-call | flops 600000000 | bytes 3638528 | tf_op jit(solution)/shard_map/pallas_call | solution.py:436
  56.6 6.5 %all-to-all-done.2 = bf16[128,5,2,128]{3,2,1,0:T(2,128)(2,1)S(1)} async-done(((bf16[128,5,2,128]{3,2,1,0:T(2,128)(2,1)}), bf16[128,5,2,128]{3,2,1,0:T(2,128)(2,1)S(1)}, u32[]{:S(2)}, u32[]{:S(2)}) %all-to-all-start.2) | async-done | bytes 327712 | tf_op jit(solution)/shard_map/all_to_all | solution.py:452
  63.0 2.8 %shard_map.124 = (bf16[2304,128]{1,0:T(8,128)(2,1)S(1)}, bf16[24,128,128]{2,1,0:T(8,128)(2,1)S(1)}, bf16[24,128,128]{2,1,0:T(8,128)(2,1)S(1)}) custom-call(bf16[1280,128]{1,0:T(8,128)(2,1)S(1)} %bitcast.30, bf16[384,512]{1,0:T(8,128)(2,1)} %get-tuple-element.29.left_h, bf16[512,512]{1,0:T(8,128)(2,1)} %get-tuple-element.30.right_h, ...), custom_call_target="tpu_custom_call" | custom-call | flops 800000000 | bytes 4980736 | tf_op jit(solution)/shard_map/pallas_call | solution.py:436
  65.8 17.8 %all_to_all.32 = bf16[128,9,2,128]{3,2,1,0:T(2,128)(2,1)S(1)} all-to-all(bf16[128,9,2,128]{3,2,1,0:T(2,128)(2,1)S(1)} %bitcast.27), channel_id=1, replica_groups=mesh['row'=16,'col'=8] {'row','col'}, dimensions={0} | all-to-all | bytes 1179648 | tf_op jit(solution)/shard_map/all_to_all | solution.py:452
  83.6 0.6 shard_map.126
  84.3 15.2 %all_to_all.33 = bf16[128,3,2,128]{3,2,1,0:T(2,128)(2,1)S(1)} all-to-all(bf16[128,3,2,128]{3,2,1,0:T(2,128)(2,1)S(1)} %bitcast.26), channel_id=1, replica_groups=mesh['row'=16,'col'=8] {'row','col'}, dimensions={0} | all-to-all | bytes 393216 | tf_op jit(solution)/shard_map/all_to_all | solution.py:452
  99.5 0.7 shard_map.127
  100.3 0.0 copy-start
  100.3 4.7 %all-to-all-start.5 = ((bf16[128,3,2,128]{3,2,1,0:T(2,128)(2,1)}), bf16[128,3,2,128]{3,2,1,0:T(2,128)(2,1)S(1)}, u32[]{:S(2)}, u32[]{:S(2)}) async-start(bf16[128,3,2,128]{3,2,1,0:T(2,128)(2,1)} %bitcast.18), calls=%async_computation.5 | async-start | bytes 393216 | tf_op jit(solution)/shard_map/all_to_all | solution.py:452
  105.0 0.0 copy-start.2
  105.0 0.0 copy-done
  105.0 0.6 copy-done.2
  105.6 7.3 %shard_map.125 = bf16[1152,128]{1,0:T(8,128)(2,1)} custom-call(bf16[2304,128]{1,0:T(8,128)(2,1)S(1)} %bitcast.21, bf16[24,128,128]{2,1,0:T(8,128)(2,1)} %get-tuple-element.31.pg_h, bf16[24,128,128]{2,1,0:T(8,128)(2,1)} %get-tuple-element.32.pvg_h, bf16[1152,128]{1,0:T(8,128)(2,1)S(1)} %get-tuple-element.34.d_og_ref, bf16[1152,128]{1,0:T(8,128)(2,1)S(1)} %bitcast.33, ...), custom_call_target="tpu_custom_call" | custom-call | flops 400000000 | bytes 3211520 | tf_op jit(solution)/shard_map/pallas_call | solution.py:436
  112.9 2.0 %all-to-all-done.5 = bf16[128,3,2,128]{3,2,1,0:T(2,128)(2,1)S(1)} async-done(((bf16[128,3,2,128]{3,2,1,0:T(2,128)(2,1)}), bf16[128,3,2,128]{3,2,1,0:T(2,128)(2,1)S(1)}, u32[]{:S(2)}, u32[]{:S(2)}) %all-to-all-start.5) | async-done | bytes 196640 | tf_op jit(solution)/shard_map/all_to_all | solution.py:452
  114.9 0.9 shard_map.128
Async XLA Ops:
  47.0 5.3 %copy-start.1 = (bf16[128,640]{1,0:T(8,128)(2,1)S(1)}, bf16[128,640]{1,0:T(8,128)(2,1)}, u32[]{:S(2)}) copy-start(bf16[128,640]{1,0:T(8,128)(2,1)} %w_ref.3) | copy-start | bytes 491524
  47.0 5.3 %copy-start.3 = (bf16[24,48,128]{2,1,0:T(8,128)(2,1)S(1)}, bf16[24,48,128]{2,1,0:T(8,128)(2,1)}, u32[]{:S(2)}) copy-start(bf16[24,48,128]{2,1,0:T(8,128)(2,1)} %param.17) | copy-start | bytes 884740
  47.0 16.0 %all-to-all-start.2 = ((bf16[128,5,2,128]{3,2,1,0:T(2,128)(2,1)}), bf16[128,5,2,128]{3,2,1,0:T(2,128)(2,1)S(1)}, u32[]{:S(2)}, u32[]{:S(2)}) async-start(bf16[128,5,2,128]{3,2,1,0:T(2,128)(2,1)} %bitcast.11), calls=%async_computation.2 | async-start | bytes 655360 | tf_op jit(solution)/shard_map/all_to_all | solution.py:452
  52.3 0.7 copy-start.4
  52.3 0.7 copy-start.5
  52.3 0.7 copy-start.6
  100.3 4.7 %copy-start = (bf16[24,48,128]{2,1,0:T(8,128)(2,1)S(1)}, bf16[24,48,128]{2,1,0:T(8,128)(2,1)}, u32[]{:S(2)}) copy-start(bf16[24,48,128]{2,1,0:T(8,128)(2,1)} %param.9) | copy-start | bytes 884740
  100.3 14.6 %all-to-all-start.5 = ((bf16[128,3,2,128]{3,2,1,0:T(2,128)(2,1)}), bf16[128,3,2,128]{3,2,1,0:T(2,128)(2,1)S(1)}, u32[]{:S(2)}, u32[]{:S(2)}) async-start(bf16[128,3,2,128]{3,2,1,0:T(2,128)(2,1)} %bitcast.18), calls=%async_computation.5 | async-start | bytes 393216 | tf_op jit(solution)/shard_map/all_to_all | solution.py:452
  105.0 0.7 copy-start.2

commit v8 on v7

--- a/solution.py
+++ b/solution.py
@@ -169,8 +169,7 @@
     return out
 
 
-def mix_kernel(recv_ref, send_ref, left_h, right_h, left_ref, right_ref, scratch, third, mixed,
-               out, sems):
+def mix_kernel(recv_ref, send_ref, left_ref, right_ref, scratch, third, mixed, out):
     scratch[...] = recv_ref[...].astype(F32)
     lane, wide = lane_of((8, LANES)), lane_of((NR, LANES))
     for p in range(NC // 2):
@@ -203,10 +202,6 @@
             lanes = slice(p * LANES, (p + 1) * LANES)
             left_ref[r2 * B : (r2 + 1) * B, lanes] = jnp.concatenate(lefts, 0).astype(BF16)
             right_ref[r2 * HALF : r2 * HALF + B, lanes] = jnp.concatenate(rights, 0).astype(BF16)
-    copies = [pltpu.make_async_copy(left_ref, left_h, sems.at[0]),
-              pltpu.make_async_copy(right_ref, right_h, sems.at[1])]
-    for copy in copies:
-        copy.start()
     product = dot(left_ref[...], right_ref[...], NT)
     for p in range(NC // 2):
         mixed[p * N : (p + 1) * N, :] = product[:, p * LANES : (p + 1) * LANES]
@@ -231,8 +226,6 @@
         out[pl.ds(2 * p * ONE + 8, NR, stride=NC * ONE), :] = first
         out[pl.ds((2 * p + 1) * ONE + 8, NR, stride=NC * ONE), :] = second
     send_ref[...] = out[...].astype(BF16)
-    for copy in copies:
-        copy.wait()
 
 
 def d_mixed_kernel(recv_ref, dproj_ref, w_out_ref, spread_ref, send_ref, scratch):
@@ -285,12 +278,12 @@
         copy.wait()
 
 
-def back_kernel(recv_ref, left_h, right_h, pg_h, pvg_h, send_ref, pg_ref, pvg_ref,
-                left_ref, right_ref, scratch, d_tile, d_left, d_right, out, sems):
+def back_kernel(recv_ref, left_ref, right_ref, pg_h, pvg_h, send_ref, pg_ref, pvg_ref,
+                scratch, d_tile, d_left, d_right, out, sems):
     copies = [
         pltpu.make_async_copy(src, dst, sems.at[n])
         for n, (src, dst) in enumerate(
-            [(right_h, right_ref), (left_h, left_ref), (pg_h, pg_ref), (pvg_h, pvg_ref)]
+            [(pg_h, pg_ref), (pvg_h, pvg_ref)]
         )
     ]
     for copy in copies:
@@ -317,8 +310,6 @@
                 lane, roll(x, 32), 32, tail, HALF, roll(y, 96), 96, tail
             )
     d = jnp.concatenate([d_tile[p * N : (p + 1) * N, :].astype(BF16) for p in range(4)], 1)
-    copies[0].wait()
-    copies[1].wait()
     d_left[...] = dot(d, right_ref[...], NN)
     product = dot(d, left_ref[...], TN)
     for p in range(NC // 2):
@@ -353,8 +344,8 @@
                 out[pl.ds(start, 8, stride=2 * NC * BOTH), :] = first
                 out[pl.ds(start + BOTH, 8, stride=2 * NC * BOTH), :] = second
     send_ref[...] = out[...].astype(BF16)
-    copies[2].wait()
-    copies[3].wait()
+    for copy in copies:
+        copy.wait()
 
 
 def gated(scratch, a, pg_v, pvg_v):
@@ -476,9 +467,8 @@
         mix_kernel,
         [recv],
         [(one_shape, BF16), ((N, 512), BF16), ((512, 512), BF16)],
-        [vm(N, 512, dtype=BF16), vm(512, 512, dtype=BF16), vm(*both_shape), vm(512, LANES),
-         vm(4 * N, LANES), vm(*one_shape), dma((2,))],
-        400_000_000, hbm_out=(1, 2),
+        [vm(*both_shape), vm(512, LANES), vm(4 * N, LANES), vm(*one_shape)],
+        400_000_000,
     )
     mixed = exchange(send, 5, 2)
     (send,) = call(
@@ -501,9 +491,9 @@
         back_kernel,
         [recv, left, right, pg, pvg],
         [(both_shape, BF16), ((A, H, LANES), BF16), ((A, H, LANES), BF16)],
-        [vm(N, 512, dtype=BF16), vm(512, 512, dtype=BF16), vm(*one_shape), vm(4 * N, LANES),
-         vm(N, 512), vm(4 * 512, LANES), vm(*both_shape), dma((4,))],
-        800_000_000, hbm_in=(1, 2, 3, 4),
+        [vm(*one_shape), vm(4 * N, LANES), vm(N, 512), vm(4 * 512, LANES), vm(*both_shape),
+         dma((2,))],
+        800_000_000, hbm_in=(3, 4),
     )
     recv = exchange(send, 9, 2)
     (send,) = call(

time: 116 us -> 114 us (0.983)
  Pallas kernels: 22.2 us -> 20.3 us
    pallas_call x9, Pallas kernels: 22.2 us -> 20.3 us  [call(): pl.pallas_call(kernel, out_shape=shapes, in_specs=specs, out_specs=[HBM_S...]
  transfers between devices with their start and end apart: 2 -> 2, of which waited for: 2 -> 2; matrix products, arithmetic and copies ran while one was open for 0% -> 0% of each run, Pallas kernels for 9% -> 10%
where the time goes in v8:
time: 114 us
  blocking collectives  73.2 us (64%)
  Pallas kernels  20.3 us (18%)
  starting transfers between devices  9.92 us (9%)
  waiting for transfers between devices  8.41 us (7%)
  local copies, waits for them, and re-layouts  1.3 us (1%)
    all_to_all x4, blocking collectives, exchange(): moved = lax.all_to_all(x.reshape(ND, *tile, LANES), AXES, 0, 0, tiled=True)  73.2 us
    pallas_call x9, Pallas kernels, call(): pl.pallas_call(kernel, out_shape=shapes, in_specs=specs, out_specs=[HBM_S...  20.3 us
    all_to_all x2, starting transfers between devices, exchange(): moved = lax.all_to_all(x.reshape(ND, *tile, LANES), AXES, 0, 0, tiled=True)  9.92 us
    all_to_all x2, waiting for transfers between devices, exchange(): moved = lax.all_to_all(x.reshape(ND, *tile, LANES), AXES, 0, 0, tiled=True)  8.41 us
  transfers between devices with their start and end apart: 2, of which 2 were waited for; matrix products, arithmetic and copies ran while one was open for 0% of the time, Pallas kernels for 10%

profile of v8, /device:TPU:1, one launch (start us, length us, event | category | flops | bytes accessed | tf_op | source)
XLA Modules:
  0.0 113.9 jit_solution(6405554258624111411)
XLA Ops:
  0.6 2.8 %shard_map.120 = (bf16[2304,128]{1,0:T(8,128)(2,1)S(1)}, bf16[1152,128]{1,0:T(8,128)(2,1)S(1)}, bf16[1152,128]{1,0:T(8,128)(2,1)S(1)}, f32[128,128]{1,0:T(8,128)S(1)}, bf16[128,128]{1,0:T(8,128)(2,1)S(1)}) custom-call(s32[384]{0:T(512)} %mask_s.1, bf16[1152,128]{1,0:T(8,128)(2,1)} %bitcast.32, f32[1,128]{1,0:T(1,128)} %bitcast.34, f32[1,128]{1,0:T(1,128)} %bitcast.42, ...), custom_call_target="tpu_custom_call" | custom-call | flops 500000000 | bytes 2033152 | tf_op jit(solution)/shard_map/pallas_call | solution.py:427
  3.4 24.2 %all_to_all.30 = bf16[128,9,2,128]{3,2,1,0:T(2,128)(2,1)S(1)} all-to-all(bf16[128,9,2,128]{3,2,1,0:T(2,128)(2,1)S(1)} %bitcast.28), channel_id=1, replica_groups=mesh['row'=16,'col'=8] {'row','col'}, dimensions={0} | all-to-all | bytes 1179648 | tf_op jit(solution)/shard_map/all_to_all | solution.py:443
  27.6 1.4 %shard_map.121 = (bf16[1280,128]{1,0:T(8,128)(2,1)S(1)}, bf16[384,512]{1,0:T(8,128)(2,1)S(1)}, bf16[512,512]{1,0:T(8,128)(2,1)S(1)}) custom-call(bf16[2304,128]{1,0:T(8,128)(2,1)S(1)} %bitcast.29), custom_call_target="tpu_custom_call" | custom-call | flops 400000000 | bytes 1835008 | tf_op jit(solution)/shard_map/pallas_call | solution.py:427
  29.0 15.9 %all_to_all.31 = bf16[128,5,2,128]{3,2,1,0:T(2,128)(2,1)S(1)} all-to-all(bf16[128,5,2,128]{3,2,1,0:T(2,128)(2,1)S(1)} %bitcast.31), channel_id=1, replica_groups=mesh['row'=16,'col'=8] {'row','col'}, dimensions={0} | all-to-all | bytes 655360 | tf_op jit(solution)/shard_map/all_to_all | solution.py:443
  44.9 1.3 %shard_map.123 = bf16[1280,128]{1,0:T(8,128)(2,1)} custom-call(bf16[1280,128]{1,0:T(8,128)(2,1)S(1)} %bitcast.22, bf16[1152,128]{1,0:T(8,128)(2,1)S(1)} %get-tuple-element.25.dproj_ref, bf16[128,128]{1,0:T(8,128)(2,1)S(1)} %get-tuple-element.24.w_out_ref, f32[128,128]{1,0:T(8,128)S(1)} %get-tuple-element.28.spread_ref), custom_call_target="tpu_custom_call" | custom-call | flops 50000000 | bytes 1015808 | tf_op jit(solution)/shard_map/pallas_call | solution.py:427
  46.2 0.0 copy-start.1
  46.2 0.0 copy-start.3
  46.2 5.2 %all-to-all-start.2 = ((bf16[128,5,2,128]{3,2,1,0:T(2,128)(2,1)}), bf16[128,5,2,128]{3,2,1,0:T(2,128)(2,1)S(1)}, u32[]{:S(2)}, u32[]{:S(2)}) async-start(bf16[128,5,2,128]{3,2,1,0:T(2,128)(2,1)} %bitcast.11), calls=%async_computation.2 | async-start | bytes 655360 | tf_op jit(solution)/shard_map/all_to_all | solution.py:443
  51.4 0.0 copy-start.4
  51.4 0.0 copy-start.5
  51.4 0.0 copy-start.6
  51.4 0.0 copy-done.1
  51.4 0.0 copy-done.3
  51.5 0.6 copy-done.4
  52.1 0.0 copy-done.5
  52.1 0.0 copy-done.6
  52.1 3.6 %shard_map.122 = (bf16[1152,128]{1,0:T(8,128)(2,1)}, bf16[1152,128]{1,0:T(8,128)(2,1)S(1)}, bf16[2,128,128]{2,1,0:T(8,128)(2,1)S(1)}, bf16[24,128,128]{2,1,0:T(8,128)(2,1)}, bf16[24,128,128]{2,1,0:T(8,128)(2,1)}) custom-call(s32[384]{0:T(512)S(1)} %copy-done.4, bf16[1280,128]{1,0:T(8,128)(2,1)S(1)} %bitcast.23, ...), custom_call_target="tpu_custom_call" | custom-call | flops 600000000 | bytes 3638528 | tf_op jit(solution)/shard_map/pallas_call | solution.py:427
  55.7 6.5 %all-to-all-done.2 = bf16[128,5,2,128]{3,2,1,0:T(2,128)(2,1)S(1)} async-done(((bf16[128,5,2,128]{3,2,1,0:T(2,128)(2,1)}), bf16[128,5,2,128]{3,2,1,0:T(2,128)(2,1)S(1)}, u32[]{:S(2)}, u32[]{:S(2)}) %all-to-all-start.2) | async-done | bytes 327712 | tf_op jit(solution)/shard_map/all_to_all | solution.py:443
  62.2 1.7 %shard_map.124 = (bf16[2304,128]{1,0:T(8,128)(2,1)S(1)}, bf16[24,128,128]{2,1,0:T(8,128)(2,1)S(1)}, bf16[24,128,128]{2,1,0:T(8,128)(2,1)S(1)}) custom-call(bf16[1280,128]{1,0:T(8,128)(2,1)S(1)} %bitcast.30, bf16[384,512]{1,0:T(8,128)(2,1)S(1)} %get-tuple-element.29.left_ref, bf16[512,512]{1,0:T(8,128)(2,1)S(1)} %get-tuple-element.30.right_ref, ...), custom_call_target="tpu_custom_call" | custom-call | flops 800000000 | bytes 4980736 | tf_op jit(solution)/shard_map/pallas_call | solution.py:427
  63.9 17.8 %all_to_all.32 = bf16[128,9,2,128]{3,2,1,0:T(2,128)(2,1)S(1)} all-to-all(bf16[128,9,2,128]{3,2,1,0:T(2,128)(2,1)S(1)} %bitcast.27), channel_id=1, replica_groups=mesh['row'=16,'col'=8] {'row','col'}, dimensions={0} | all-to-all | bytes 1179648 | tf_op jit(solution)/shard_map/all_to_all | solution.py:443
  81.7 0.6 shard_map.126
  82.4 15.2 %all_to_all.33 = bf16[128,3,2,128]{3,2,1,0:T(2,128)(2,1)S(1)} all-to-all(bf16[128,3,2,128]{3,2,1,0:T(2,128)(2,1)S(1)} %bitcast.26), channel_id=1, replica_groups=mesh['row'=16,'col'=8] {'row','col'}, dimensions={0} | all-to-all | bytes 393216 | tf_op jit(solution)/shard_map/all_to_all | solution.py:443
  97.6 0.7 shard_map.127
  98.4 0.0 copy-start
  98.4 4.7 %all-to-all-start.5 = ((bf16[128,3,2,128]{3,2,1,0:T(2,128)(2,1)}), bf16[128,3,2,128]{3,2,1,0:T(2,128)(2,1)S(1)}, u32[]{:S(2)}, u32[]{:S(2)}) async-start(bf16[128,3,2,128]{3,2,1,0:T(2,128)(2,1)} %bitcast.18), calls=%async_computation.5 | async-start | bytes 393216 | tf_op jit(solution)/shard_map/all_to_all | solution.py:443
  103.1 0.0 copy-start.2
  103.1 0.0 copy-done
  103.1 0.6 copy-done.2
  103.7 7.3 %shard_map.125 = bf16[1152,128]{1,0:T(8,128)(2,1)} custom-call(bf16[2304,128]{1,0:T(8,128)(2,1)S(1)} %bitcast.21, bf16[24,128,128]{2,1,0:T(8,128)(2,1)} %get-tuple-element.31.pg_h, bf16[24,128,128]{2,1,0:T(8,128)(2,1)} %get-tuple-element.32.pvg_h, bf16[1152,128]{1,0:T(8,128)(2,1)S(1)} %get-tuple-element.34.d_og_ref, bf16[1152,128]{1,0:T(8,128)(2,1)S(1)} %bitcast.33, ...), custom_call_target="tpu_custom_call" | custom-call | flops 400000000 | bytes 3211520 | tf_op jit(solution)/shard_map/pallas_call | solution.py:427
  111.0 2.0 %all-to-all-done.5 = bf16[128,3,2,128]{3,2,1,0:T(2,128)(2,1)S(1)} async-done(((bf16[128,3,2,128]{3,2,1,0:T(2,128)(2,1)}), bf16[128,3,2,128]{3,2,1,0:T(2,128)(2,1)S(1)}, u32[]{:S(2)}, u32[]{:S(2)}) %all-to-all-start.5) | async-done | bytes 196640 | tf_op jit(solution)/shard_map/all_to_all | solution.py:443
  113.0 0.9 shard_map.128
Async XLA Ops:
  46.2 5.3 %copy-start.1 = (bf16[128,640]{1,0:T(8,128)(2,1)S(1)}, bf16[128,640]{1,0:T(8,128)(2,1)}, u32[]{:S(2)}) copy-start(bf16[128,640]{1,0:T(8,128)(2,1)} %w_ref.3) | copy-start | bytes 491524
  46.2 5.3 %copy-start.3 = (bf16[24,48,128]{2,1,0:T(8,128)(2,1)S(1)}, bf16[24,48,128]{2,1,0:T(8,128)(2,1)}, u32[]{:S(2)}) copy-start(bf16[24,48,128]{2,1,0:T(8,128)(2,1)} %param.17) | copy-start | bytes 884740
  46.2 16.0 %all-to-all-start.2 = ((bf16[128,5,2,128]{3,2,1,0:T(2,128)(2,1)}), bf16[128,5,2,128]{3,2,1,0:T(2,128)(2,1)S(1)}, u32[]{:S(2)}, u32[]{:S(2)}) async-start(bf16[128,5,2,128]{3,2,1,0:T(2,128)(2,1)} %bitcast.11), calls=%async_computation.2 | async-start | bytes 655360 | tf_op jit(solution)/shard_map/all_to_all | solution.py:443
  51.4 0.7 copy-start.4
  51.4 0.7 copy-start.5
  51.4 0.7 copy-start.6
  98.4 4.7 %copy-start = (bf16[24,48,128]{2,1,0:T(8,128)(2,1)S(1)}, bf16[24,48,128]{2,1,0:T(8,128)(2,1)}, u32[]{:S(2)}) copy-start(bf16[24,48,128]{2,1,0:T(8,128)(2,1)} %param.9) | copy-start | bytes 884740
  98.4 14.6 %all-to-all-start.5 = ((bf16[128,3,2,128]{3,2,1,0:T(2,128)(2,1)}), bf16[128,3,2,128]{3,2,1,0:T(2,128)(2,1)S(1)}, u32[]{:S(2)}, u32[]{:S(2)}) async-start(bf16[128,3,2,128]{3,2,1,0:T(2,128)(2,1)} %bitcast.18), calls=%async_computation.5 | async-start | bytes 393216 | tf_op jit(solution)/shard_map/all_to_all | solution.py:443
  103.1 0.7 copy-start.2

commit v9 on v8

--- a/solution.py
+++ b/solution.py
@@ -138,9 +138,8 @@
     copies[0].wait()
     weights = stacked_weights(w_v)
     w_og = w_v[:, 4 * H :]
-    for copy in copies[1:]:
+    for copy in copies[1:5]:
         copy.wait()
-    spread_ref[...] = jnp.broadcast_to(column(out_gain_v[...]), (H, LANES))
     col_mask = column_mask(mask_s)
     gain, bias = gain_v[...], bias_v[...]
     for pair_at in (8, 9, 10, 11, 0, 1, 2, 3, 4, 5, 6, 7):
@@ -148,8 +147,6 @@
         normal, _ = norm_rows(pair_v[rows, :].astype(F32))
         normed = (normal * gain + bias).astype(BF16)
         normed_ref[rows, :] = normed
-        sig = jax.nn.sigmoid(dot(normed, w_og, NN))
-        dproj_ref[rows, :] = (cot_v[rows, :].astype(F32) * sig).astype(BF16)
         for k, (value, _, pg) in enumerate(gate_parts(weights, normed, pair_at, col_mask, mask_s)):
             a = pair_at * 2 + k
             if a >= 16:
@@ -160,6 +157,13 @@
             for n in range(2):
                 scratch[pl.ds(16 + n, H, stride=BOTH), :] = pack_tail(third, n)
     send_ref[...] = scratch[...].astype(BF16)
+    for copy in copies[5:]:
+        copy.wait()
+    spread_ref[...] = jnp.broadcast_to(column(out_gain_v[...]), (H, LANES))
+    for n in range(6):
+        rows = pl.ds(n * CELLS // 6, CELLS // 6)
+        sig = jax.nn.sigmoid(dot(normed_ref[rows, :], w_og, NN))
+        dproj_ref[rows, :] = (cot_v[rows, :].astype(F32) * sig).astype(BF16)
 
 
 def pick(lane, *parts):
@@ -242,8 +246,8 @@
 
 
 def update_kernel(mask_s, recv_ref, w_out_ref, gain_ref, bias_ref, dproj_ref, cot_ref,
-                  normed_ref, w_ref, update_ref, d_og_ref, grads_ref, pg_h, pvg_h,
-                  scratch, pg_v, pvg_v, sems):
+                  normed_ref, w_ref, update_ref, grads_ref, pg_v, pvg_v, d_og_h, pg_h, pvg_h,
+                  scratch, d_og_ref, sems):
     weights = stacked_weights(w_ref)
     col_mask = column_mask(mask_s)
     for pair_at in range(A // 2):
@@ -272,22 +276,15 @@
             d_og_ref[rows, :] = (
                 cot_ref[rows, :].astype(F32) * proj * sig * (1.0 - sig)
             ).astype(BF16)
+    copies.append(pltpu.make_async_copy(d_og_ref, d_og_h, sems.at[2]))
+    copies[2].start()
     grads_ref[0] = dot(d_og_ref[...], normed_ref[...], TN).astype(BF16)
     grads_ref[1] = grad.astype(BF16)
     for copy in copies:
         copy.wait()
 
 
-def back_kernel(recv_ref, left_ref, right_ref, pg_h, pvg_h, send_ref, pg_ref, pvg_ref,
-                scratch, d_tile, d_left, d_right, out, sems):
-    copies = [
-        pltpu.make_async_copy(src, dst, sems.at[n])
-        for n, (src, dst) in enumerate(
-            [(pg_h, pg_ref), (pvg_h, pvg_ref)]
-        )
-    ]
-    for copy in copies:
-        copy.start()
+def back_kernel(recv_ref, left_ref, right_ref, send_ref, scratch, d_tile, d_left, d_right, out):
     scratch[...] = recv_ref[...].astype(F32)
     lane, wide = lane_of((8, LANES)), lane_of((NR, LANES))
     for p in range(NC // 2):
@@ -344,8 +341,6 @@
                 out[pl.ds(start, 8, stride=2 * NC * BOTH), :] = first
                 out[pl.ds(start + BOTH, 8, stride=2 * NC * BOTH), :] = second
     send_ref[...] = out[...].astype(BF16)
-    for copy in copies:
-        copy.wait()
 
 
 def gated(scratch, a, pg_v, pvg_v):
@@ -369,10 +364,12 @@
     send_ref[...] = packed[...].astype(BF16)
 
 
-def pair_grad_kernel(recv_ref, pg_h, pvg_h, d_og_ref, pair_ref, gain_ref, w_ref,
-                     out_ref, scratch, pg_v, pvg_v, sems):
-    copies = [pltpu.make_async_copy(pg_h, pg_v, sems.at[0]),
-              pltpu.make_async_copy(pvg_h, pvg_v, sems.at[1])]
+def pair_grad_kernel(recv_ref, pg_h, pvg_h, d_og_h, pair_ref, gain_ref, w_ref,
+                     out_ref, scratch, pg_v, pvg_v, d_og_ref, sems):
+    copies = [
+        pltpu.make_async_copy(src, dst, sems.at[n])
+        for n, (src, dst) in enumerate([(pg_h, pg_v), (pvg_h, pvg_v), (d_og_h, d_og_ref)])
+    ]
     for copy in copies:
         copy.start()
     scratch[...] = recv_ref[...].astype(F32)
@@ -479,21 +476,20 @@
         50_000_000,
     )
     recv = exchange(send, 5, 2)
-    update, d_og, grads, pg, pvg = call(
+    update, grads, pg_near, pvg_near, d_og, pg, pvg = call(
         update_kernel,
         [mask, mixed, w_out_near, line(out_gain), line(out_bias), dproj, cot2, normed, w_in],
-        [((CELLS, H), BF16), ((CELLS, H), BF16), ((2, H, H), BF16),
-         ((A, H, LANES), BF16), ((A, H, LANES), BF16)],
-        [vm(*one_shape), *gates, dma((2,))],
-        600_000_000, smem_in=(0,), hbm_out=(3, 4),
-    )
-    send, pg_near, pvg_near = call(
+        [((CELLS, H), BF16), ((2, H, H), BF16), ((A, H, LANES), BF16), ((A, H, LANES), BF16),
+         ((CELLS, H), BF16), ((A, H, LANES), BF16), ((A, H, LANES), BF16)],
+        [vm(*one_shape), vm(CELLS, H, dtype=BF16), dma((3,))],
+        600_000_000, smem_in=(0,), hbm_out=(4, 5, 6),
+    )
+    (send,) = call(
         back_kernel,
-        [recv, left, right, pg, pvg],
-        [(both_shape, BF16), ((A, H, LANES), BF16), ((A, H, LANES), BF16)],
-        [vm(*one_shape), vm(4 * N, LANES), vm(N, 512), vm(4 * 512, LANES), vm(*both_shape),
-         dma((2,))],
-        800_000_000, hbm_in=(3, 4),
+        [recv, left, right],
+        [(both_shape, BF16)],
+        [vm(*one_shape), vm(4 * N, LANES), vm(N, 512), vm(4 * 512, LANES), vm(*both_shape)],
+        800_000_000,
     )
     recv = exchange(send, 9, 2)
     (send,) = call(
@@ -508,8 +504,8 @@
         pair_grad_kernel,
         [recv, pg, pvg, d_og, pair2, line(in_gain), w_in],
         [((CELLS, H), BF16)],
-        [vm(*both_shape), *gates, dma((2,))],
-        400_000_000, hbm_in=(1, 2),
+        [vm(*both_shape), *gates, vm(CELLS, H, dtype=BF16), dma((3,))],
+        400_000_000, hbm_in=(1, 2, 3),
     )
     (send,) = call(sum_kernel, [parts], [(sum_shape, BF16)], [], 1_000_000)
     sums = exchange(send, 3, 2)

time: 114 us -> 114 us (level)
  blocking collectives: 73.2 us -> 70.9 us
  waiting for transfers between devices: 8.41 us -> 9.76 us
    all_to_all x4, blocking collectives: 73.2 us -> 70.9 us  [exchange(): moved = lax.all_to_all(x.reshape(ND, *tile, LANES), AXES, 0, 0, tiled=True)]
    all_to_all x2, waiting for transfers between devices: 8.41 us -> 9.76 us  [exchange(): moved = lax.all_to_all(x.reshape(ND, *tile, LANES), AXES, 0, 0, tiled=True)]
where the time goes in v9:
time: 114 us
  blocking collectives  70.9 us (62%)
  Pallas kernels  20.3 us (18%)
  starting transfers between devices  9.93 us (9%)
  waiting for transfers between devices  9.76 us (9%)
  local copies, waits for them, and re-layouts  2.27 us (2%)
    all_to_all x4, blocking collectives, exchange(): moved = lax.all_to_all(x.reshape(ND, *tile, LANES), AXES, 0, 0, tiled=True)  70.9 us
    pallas_call x9, Pallas kernels, call(): pl.pallas_call(kernel, out_shape=shapes, in_specs=specs, out_specs=[HBM_S...  20.3 us
    all_to_all x2, starting transfers between devices, exchange(): moved = lax.all_to_all(x.reshape(ND, *tile, LANES), AXES, 0, 0, tiled=True)  9.93 us
    all_to_all x2, waiting for transfers between devices, exchange(): moved = lax.all_to_all(x.reshape(ND, *tile, LANES), AXES, 0, 0, tiled=True)  9.76 us
  transfers between devices with their start and end apart: 2, of which 2 were waited for; matrix products, arithmetic and copies ran while one was open for 0% of the time, Pallas kernels for 10%

profile of v9, /device:TPU:1, one launch (start us, length us, event | category | flops | bytes accessed | tf_op | source)
XLA Modules:
  0.0 113.9 jit_solution(9640867205341331674)
XLA Ops:
  0.6 2.8 %shard_map.120 = (bf16[2304,128]{1,0:T(8,128)(2,1)S(1)}, bf16[1152,128]{1,0:T(8,128)(2,1)S(1)}, bf16[1152,128]{1,0:T(8,128)(2,1)S(1)}, f32[128,128]{1,0:T(8,128)S(1)}, bf16[128,128]{1,0:T(8,128)(2,1)S(1)}) custom-call(s32[384]{0:T(512)} %mask_s.1, bf16[1152,128]{1,0:T(8,128)(2,1)} %bitcast.32, f32[1,128]{1,0:T(1,128)} %bitcast.34, f32[1,128]{1,0:T(1,128)} %bitcast.42, ...), custom_call_target="tpu_custom_call" | custom-call | flops 500000000 | bytes 2033152 | tf_op jit(solution)/shard_map/pallas_call | solution.py:424
  3.4 24.2 %all_to_all.30 = bf16[128,9,2,128]{3,2,1,0:T(2,128)(2,1)S(1)} all-to-all(bf16[128,9,2,128]{3,2,1,0:T(2,128)(2,1)S(1)} %bitcast.28), channel_id=1, replica_groups=mesh['row'=16,'col'=8] {'row','col'}, dimensions={0} | all-to-all | bytes 1179648 | tf_op jit(solution)/shard_map/all_to_all | solution.py:440
  27.6 1.4 %shard_map.121 = (bf16[1280,128]{1,0:T(8,128)(2,1)S(1)}, bf16[384,512]{1,0:T(8,128)(2,1)S(1)}, bf16[512,512]{1,0:T(8,128)(2,1)S(1)}) custom-call(bf16[2304,128]{1,0:T(8,128)(2,1)S(1)} %bitcast.29), custom_call_target="tpu_custom_call" | custom-call | flops 400000000 | bytes 1835008 | tf_op jit(solution)/shard_map/pallas_call | solution.py:424
  28.9 15.9 %all_to_all.31 = bf16[128,5,2,128]{3,2,1,0:T(2,128)(2,1)S(1)} all-to-all(bf16[128,5,2,128]{3,2,1,0:T(2,128)(2,1)S(1)} %bitcast.30), channel_id=1, replica_groups=mesh['row'=16,'col'=8] {'row','col'}, dimensions={0} | all-to-all | bytes 655360 | tf_op jit(solution)/shard_map/all_to_all | solution.py:440
  44.9 0.5 shard_map.123
  45.4 15.6 %all_to_all.32 = bf16[128,5,2,128]{3,2,1,0:T(2,128)(2,1)S(1)} all-to-all(bf16[128,5,2,128]{3,2,1,0:T(2,128)(2,1)S(1)} %bitcast.24), channel_id=1, replica_groups=mesh['row'=16,'col'=8] {'row','col'}, dimensions={0} | all-to-all | bytes 655360 | tf_op jit(solution)/shard_map/all_to_all | solution.py:440
  61.0 2.5 %shard_map.124 = bf16[2304,128]{1,0:T(8,128)(2,1)} custom-call(bf16[1280,128]{1,0:T(8,128)(2,1)S(1)} %bitcast.31, bf16[384,512]{1,0:T(8,128)(2,1)S(1)} %get-tuple-element.28.left_ref, bf16[512,512]{1,0:T(8,128)(2,1)S(1)} %get-tuple-element.29.right_ref), custom_call_target="tpu_custom_call" | custom-call | flops 800000000 | bytes 1835008 | tf_op jit(solution)/shard_map/pallas_call | solution.py:424
  63.6 0.0 copy-start.1
  63.6 5.2 %all-to-all-start.3 = ((bf16[128,9,2,128]{3,2,1,0:T(2,128)(2,1)}), bf16[128,9,2,128]{3,2,1,0:T(2,128)(2,1)S(1)}, u32[]{:S(2)}, u32[]{:S(2)}) async-start(bf16[128,9,2,128]{3,2,1,0:T(2,128)(2,1)} %bitcast.13), calls=%async_computation.3 | async-start | bytes 1179648 | tf_op jit(solution)/shard_map/all_to_all | solution.py:440
  68.8 0.0 copy-start.4
  68.8 0.0 copy-start.5
  68.8 0.0 copy-start.6
  68.8 0.0 copy-done.1
  68.9 0.6 copy-done.4
  69.5 0.0 copy-done.5
  69.5 0.0 copy-done.6
  69.5 0.0 copy-start.3
  69.5 1.0 copy-done.3
  70.5 3.5 %shard_map.122 = (bf16[1152,128]{1,0:T(8,128)(2,1)}, bf16[2,128,128]{2,1,0:T(8,128)(2,1)S(1)}, bf16[24,128,128]{2,1,0:T(8,128)(2,1)S(1)}, bf16[24,128,128]{2,1,0...) custom-call(s32[384]{0:T(512)S(1)} %copy-done.4, ...), custom_call_target="tpu_custom_call" | custom-call | flops 600000000 | bytes 5211392 | tf_op jit(solution)/shard_map/pallas_call | solution.py:424
  73.9 7.9 %all-to-all-done.3 = bf16[128,9,2,128]{3,2,1,0:T(2,128)(2,1)S(1)} async-done(((bf16[128,9,2,128]{3,2,1,0:T(2,128)(2,1)}), bf16[128,9,2,128]{3,2,1,0:T(2,128)(2,1)S(1)}, u32[]{:S(2)}, u32[]{:S(2)}) %all-to-all-start.3) | async-done | bytes 589856 | tf_op jit(solution)/shard_map/all_to_all | solution.py:440
  81.8 0.6 shard_map.126
  82.5 15.2 %all_to_all.33 = bf16[128,3,2,128]{3,2,1,0:T(2,128)(2,1)S(1)} all-to-all(bf16[128,3,2,128]{3,2,1,0:T(2,128)(2,1)S(1)} %bitcast.27), channel_id=1, replica_groups=mesh['row'=16,'col'=8] {'row','col'}, dimensions={0} | all-to-all | bytes 393216 | tf_op jit(solution)/shard_map/all_to_all | solution.py:440
  97.7 0.7 shard_map.127
  98.4 0.0 copy-start
  98.4 4.7 %all-to-all-start.5 = ((bf16[128,3,2,128]{3,2,1,0:T(2,128)(2,1)}), bf16[128,3,2,128]{3,2,1,0:T(2,128)(2,1)S(1)}, u32[]{:S(2)}, u32[]{:S(2)}) async-start(bf16[128,3,2,128]{3,2,1,0:T(2,128)(2,1)} %bitcast.18), calls=%async_computation.5 | async-start | bytes 393216 | tf_op jit(solution)/shard_map/all_to_all | solution.py:440
  103.1 0.0 copy-start.2
  103.2 0.0 copy-done
  103.2 0.6 copy-done.2
  103.8 7.4 %shard_map.125 = bf16[1152,128]{1,0:T(8,128)(2,1)} custom-call(bf16[2304,128]{1,0:T(8,128)(2,1)S(1)} %bitcast.21, bf16[24,128,128]{2,1,0:T(8,128)(2,1)} %get-tuple-element.30.pg_h, bf16[24,128,128]{2,1,0:T(8,128)(2,1)} %get-tuple-element.31.pvg_h, bf16[1152,128]{1,0:T(8,128)(2,1)} %get-tuple-element.32.d_og_h, bf16[1152,128]{1,0:T(8,128)(2,1)S(1)} %bitcast.33, ...), custom_call_target="tpu_custom_call" | custom-call | flops 400000000 | bytes 3211520 | tf_op jit(solution)/shard_map/pallas_call | solution.py:424
  111.2 1.9 %all-to-all-done.5 = bf16[128,3,2,128]{3,2,1,0:T(2,128)(2,1)S(1)} async-done(((bf16[128,3,2,128]{3,2,1,0:T(2,128)(2,1)}), bf16[128,3,2,128]{3,2,1,0:T(2,128)(2,1)S(1)}, u32[]{:S(2)}, u32[]{:S(2)}) %all-to-all-start.5) | async-done | bytes 196640 | tf_op jit(solution)/shard_map/all_to_all | solution.py:440
  113.1 0.9 shard_map.128
Async XLA Ops:
  63.6 5.3 %copy-start.1 = (bf16[128,640]{1,0:T(8,128)(2,1)S(1)}, bf16[128,640]{1,0:T(8,128)(2,1)}, u32[]{:S(2)}) copy-start(bf16[128,640]{1,0:T(8,128)(2,1)} %w_ref.3) | copy-start | bytes 491524
  63.6 18.2 %all-to-all-start.3 = ((bf16[128,9,2,128]{3,2,1,0:T(2,128)(2,1)}), bf16[128,9,2,128]{3,2,1,0:T(2,128)(2,1)S(1)}, u32[]{:S(2)}, u32[]{:S(2)}) async-start(bf16[128,9,2,128]{3,2,1,0:T(2,128)(2,1)} %bitcast.13), calls=%async_computation.3 | async-start | bytes 1179648 | tf_op jit(solution)/shard_map/all_to_all | solution.py:440
  68.8 0.7 copy-start.4
  68.8 0.7 copy-start.5
  68.8 0.7 copy-start.6
  69.5 1.0 copy-start.3
  98.4 4.7 %copy-start = (bf16[24,48,128]{2,1,0:T(8,128)(2,1)S(1)}, bf16[24,48,128]{2,1,0:T(8,128)(2,1)}, u32[]{:S(2)}) copy-start(bf16[24,48,128]{2,1,0:T(8,128)(2,1)} %param.9) | copy-start | bytes 884740
  98.4 14.6 %all-to-all-start.5 = ((bf16[128,3,2,128]{3,2,1,0:T(2,128)(2,1)}), bf16[128,3,2,128]{3,2,1,0:T(2,128)(2,1)S(1)}, u32[]{:S(2)}, u32[]{:S(2)}) async-start(bf16[128,3,2,128]{3,2,1,0:T(2,128)(2,1)} %bitcast.18), calls=%async_computation.5 | async-start | bytes 393216 | tf_op jit(solution)/shard_map/all_to_all | solution.py:440
  103.1 0.7 copy-start.2
